TPU v7x, 256 devices: a whole 4x4x8 slice. The times are simulated.
256 devices in a mesh: ep: 32 (over x, y, core), gd: 8 (over z).
Axes of the slice: x: 4, y: 4, z: 8, core: 2. Of those that a mesh axis runs over, the one named last changes fastest.
Arguments:
- tokens: bfloat16 [2048, 4096], P(('ep', 'gd')), may hold values from -6 to 6
- expert_ids: int32 [2048, 8], P(('ep', 'gd')), may hold values from 0 to 31, all different within a row; in each aligned block of 8 rows (0 to 7, 8 to 15, ...) at most 3 rows name the same one
- combine: float32 [2048, 8], P(('ep', 'gd')), may hold values from 0.02 to 0.3
- w_gate: bfloat16 [32, 4096, 1536], P('ep', None, 'gd'), may hold values from -0.09375 to 0.09375
- w_up: bfloat16 [32, 4096, 1536], P('ep', None, 'gd'), may hold values from -0.09375 to 0.09375
- w_down: bfloat16 [32, 1536, 4096], P('ep', 'gd'), may hold values from -0.15625 to 0.15625
- w_query: bfloat16 [4096, 4096], P(None, 'gd'), may hold values from -0.09375 to 0.09375
- w_key: bfloat16 [4096, 1024], P(None, 'gd'), may hold values from -0.09375 to 0.09375
- w_value: bfloat16 [4096, 1024], P(None, 'gd'), may hold values from -0.09375 to 0.09375
- cache_keys: bfloat16 [2048, 8, 64, 128], P('ep', 'gd'), may hold values from -68 to 68
- cache_values: bfloat16 [2048, 8, 64, 128], P('ep', 'gd'), may hold values from -6 to 6
- lengths: int32 [2048], P('ep'), may hold values from 1 to 64, as said below
Outputs:
- stream: bfloat16 [2048, 4096], P(('ep', 'gd'))
- guard: bfloat16 [2048, 4096], P('ep', 'gd')
Inputs may be any that keep to these rules, and one draw needn't show every extreme that they name: `expert_ids`: each row names 8 different experts; in the rows of one device no expert is named by more than 3 rows. `lengths`: some row has the full window of 64 positions.
All inputs are finite; a program needn't handle non-finite values.
Results may differ from a plain program's by a relative error of at most 0.03.
Values may be sent and summed in bfloat16 or wider, within the bound.
No kernel may reach another device: no remote copies, remote signals or barrier semaphores. Data moves between devices by JAX's collectives and lax.ppermute only.
A program may use at most 128 MiB of HBM per device.

v0:
```python
import functools
import math

import jax
import jax.numpy as jnp
from jax import lax
from jax.experimental import pallas as pl
from jax.experimental.pallas import tpu as pltpu
from jax.sharding import Mesh
from jax.sharding import PartitionSpec as P

EPSILON = 1e-06
BF = jnp.bfloat16
F32 = jnp.float32
LANES = 128
CAP = 3


def shift(values, axis, step):
    size = lax.axis_size(axis)
    return lax.ppermute(values, axis, [(i, (i - step) % size) for i in range(size)])


def copies(values, axis):
    size = lax.axis_size(axis)
    return lax.all_to_all(
        jnp.broadcast_to(values[None], (size, *values.shape)), axis, 0, 0, tiled=True
    )


def expert_kernel(sizes, early, steps, place_ref, mask_ref, *refs):
    n = len(sizes)
    rows, meta = refs[:n], refs[n : 2 * n]
    w_refs = refs[2 * n : 2 * n + 4]
    out_ref, joined, totals = refs[2 * n + 4 :]
    k = pl.program_id(0)
    hidden = w_refs[0].shape[0]
    at = 0
    for m, row_ref in zip(sizes, rows):
        joined[at : at + m, :] = row_ref[...]
        at += m
    part = lax.dot_general(
        joined[...],
        jnp.concatenate([w_ref[...] for w_ref in w_refs], axis=0),
        (((1,), (1,)), ((), ())),
        preferred_element_type=F32,
    )

    @pl.when(k == 0)
    def _():
        totals[...] = part

    @pl.when(k > 0)
    def _():
        totals[...] += part

    @pl.when(k == steps - 1)
    def _():
        slots = out_ref.shape[0]
        held = lax.dot_general(
            mask_ref[...],
            jnp.concatenate([m_ref[...] for m_ref in meta], axis=0),
            (((1,), (1,)), ((), ())),
            preferred_element_type=F32,
        )
        s = lax.broadcasted_iota(jnp.int32, (slots, 1), 0)
        if early:
            piece = slots // 6
            per = piece // 4
            place = jnp.where(s < slots // 2, place_ref[0], place_ref[1])
            inner = (s % piece // per + 4 - place) % 4
            block = s // piece * (piece // CAP) + inner * (per // CAP) + s % per // CAP
        else:
            block = s // CAP
        same = lax.broadcasted_iota(jnp.int32, (slots, at), 1) // 8 == block
        rank = (s % CAP).astype(F32)
        for j in range(2):
            base = 2 * j * hidden
            gate = totals[:, base : base + hidden]
            up = totals[:, base + hidden : base + 2 * hidden]
            active = (gate / (1.0 + jnp.exp(-gate)) * up).astype(BF)
            pick = jnp.where(same & (held[j : j + 1, :] == rank), 1.0, 0.0).astype(BF)
            packed = jnp.dot(pick, active, preferred_element_type=F32)
            out_ref[:, j * hidden : (j + 1) * hidden] = packed.astype(BF)


def expert_slots(pieces, early, place, masks, weights):
    hidden, depth = weights[0].shape
    chunk = 1024
    steps = depth // chunk
    sizes = tuple(p.shape[0] for p in pieces)
    in_specs = [
        pl.BlockSpec(memory_space=pltpu.SMEM),
        pl.BlockSpec((8, LANES), lambda k: (0, 0)),
    ]
    in_specs += [pl.BlockSpec((m, chunk), lambda k: (0, k)) for m in sizes]
    in_specs += [pl.BlockSpec((m, LANES), lambda k: (0, depth // LANES)) for m in sizes]
    in_specs += [pl.BlockSpec((hidden, chunk), lambda k: (0, k))] * 4
    total = sum(sizes)
    slots = total // 8 * CAP
    return pl.pallas_call(
        functools.partial(expert_kernel, sizes, early, steps),
        grid=(steps,),
        in_specs=in_specs,
        out_specs=pl.BlockSpec((slots, 2 * hidden), lambda k: (0, 0)),
        out_shape=jax.ShapeDtypeStruct((slots, 2 * hidden), BF),
        scratch_shapes=[
            pltpu.VMEM((total, chunk), BF),
            pltpu.VMEM((total, 4 * hidden), F32),
        ],
        compiler_params=pltpu.CompilerParams(vmem_limit_bytes=20 << 20),
        cost_estimate=pl.CostEstimate(
            flops=8 * total * depth * hidden,
            bytes_accessed=8 * depth * hidden + 2 * total * depth,
            transcendentals=2 * total * hidden,
        ),
        name="expert_slots",
    )(place, masks, *pieces, *pieces, *weights)


def lower_kernel(place_ref, early_ref, late_ref, own_ref, other_ref, out_ref, *sums):
    members, first, _ = early_ref.shape
    hidden = own_ref.shape[1]
    for j, w_ref in enumerate((own_ref, other_ref)):
        for d in range(members):
            span = slice(j * hidden, (j + 1) * hidden)
            active = jnp.concatenate([early_ref[d][:, span], late_ref[d][:, span]], axis=0)
            part = jnp.dot(active, w_ref[d], preferred_element_type=F32)
            if d == 0:
                sums[j][...] = part
            else:
                sums[j][...] += part
    x, y = place_ref[0], place_ref[1]
    placed = sums[2]
    per = placed.shape[2] // 2
    for h in range(2):
        for o, step in enumerate((0, 1, 3, 2)):
            for i in range(4):
                at = (3 * h + o) * 4 * per if o < 3 else first + h * 4 * per
                at = at + i * per
                if h == 0:
                    inner = i if o < 3 else (x + i) % 4
                    chip = inner * 4 + (y + step) % 4
                else:
                    inner = i if o < 3 else (y + i) % 4
                    chip = (x + step) % 4 * 4 + inner
                for j in range(2):
                    placed[chip, j, h * per : (h + 1) * per, :] = sums[j][at : at + per, :]
    out_ref[...] = placed[...].astype(BF)


def lower(place, early, late, down_own, down_other, chips):
    members, first, width = early.shape
    slots = first + late.shape[1]
    cols = down_own.shape[2]
    per_chip = slots // chips
    return pl.pallas_call(
        lower_kernel,
        in_specs=[pl.BlockSpec(memory_space=pltpu.SMEM)]
        + [pl.BlockSpec(memory_space=pltpu.VMEM)] * 4,
        out_specs=pl.BlockSpec(memory_space=pltpu.VMEM),
        out_shape=jax.ShapeDtypeStruct((chips, 2, per_chip, cols), BF),
        scratch_shapes=[
            pltpu.VMEM((slots, cols), F32),
            pltpu.VMEM((slots, cols), F32),
            pltpu.VMEM((chips, 2, per_chip, cols), F32),
        ],
        compiler_params=pltpu.CompilerParams(vmem_limit_bytes=16 << 20),
        cost_estimate=pl.CostEstimate(
            flops=2 * members * slots * width * cols,
            bytes_accessed=2 * members * width * (slots + cols),
            transcendentals=0,
        ),
        name="lower",
    )(place, early, late, down_own, down_other)


def attend(group_stream, w_query, w_key, w_value, cache_keys, cache_values, lengths):
    widened = group_stream.astype(F32)
    guard_norm = (
        widened * lax.rsqrt(jnp.mean(widened * widened, axis=-1, keepdims=True) + EPSILON)
    ).astype(BF)
    queries = jnp.dot(guard_norm, w_query, preferred_element_type=F32)
    key_new = jnp.dot(guard_norm, w_key, preferred_element_type=F32).astype(BF)
    value_new = jnp.dot(guard_norm, w_value, preferred_element_type=F32).astype(BF)
    group_total, heads_kv, window_len, head_size = cache_keys.shape
    heads_per = w_query.shape[1] // (heads_kv * head_size)
    queries = queries.reshape(group_total, heads_kv, heads_per, head_size)
    key_new = key_new.reshape(group_total, heads_kv, head_size)
    value_new = value_new.reshape(group_total, heads_kv, head_size)
    scale_factor = 1.0 / math.sqrt(head_size)
    scores = (
        jnp.einsum(
            "rhgd,rhjd->rhgj", queries, cache_keys.astype(F32), precision=lax.Precision.HIGHEST
        )
        * scale_factor
    )
    own_score = (
        jnp.einsum(
            "rhgd,rhd->rhg", queries, key_new.astype(F32), precision=lax.Precision.HIGHEST
        )
        * scale_factor
    )
    positions = jnp.arange(window_len, dtype=jnp.int32)
    allowed = positions[None, None, None, :] >= (window_len - lengths)[:, None, None, None]
    masked = jnp.where(allowed, scores, -jnp.inf)
    highest = jnp.maximum(jnp.max(masked, axis=-1), own_score)
    weights = jnp.exp(masked - highest[..., None])
    own_weight = jnp.exp(own_score - highest)
    denominator = jnp.sum(weights, axis=-1) + own_weight
    probabilities = weights / denominator[..., None]
    own_prob = own_weight / denominator
    attended = jnp.einsum(
        "rhgj,rhjd->rhgd",
        probabilities,
        cache_values.astype(F32),
        precision=lax.Precision.HIGHEST,
    )
    attended = attended + own_prob[..., None] * value_new.astype(F32)[:, :, None, :]
    return attended.astype(BF).reshape(group_total, heads_kv * heads_per * head_size)


def split3(values):
    high = values.astype(BF)
    rest = values - high.astype(F32)
    middle = rest.astype(BF)
    return high, middle, (rest - middle.astype(F32)).astype(BF)


def routing_columns(expert_ids, combine, experts):
    named = expert_ids[:, :, None] == jnp.arange(experts, dtype=jnp.int32)
    chosen = jnp.any(named, axis=1)
    weight = jnp.sum(jnp.where(named, combine[:, :, None], 0.0), axis=1)
    rows = jnp.arange(expert_ids.shape[0])
    earlier = rows[None, :, None] < rows[:, None, None]
    rank = jnp.sum((earlier & chosen[None]).astype(jnp.int32), axis=1)
    rank = jnp.where(chosen, rank, CAP).astype(BF)
    return jnp.concatenate([rank, *split3(weight)], axis=1)


def per_device(
    tokens,
    expert_ids,
    combine,
    w_gate,
    w_up,
    w_down,
    w_query,
    w_key,
    w_value,
    cache_keys,
    cache_values,
    lengths,
):
    rows_n, width = tokens.shape
    x, y, c, z = (lax.axis_index(a) for a in ("x", "y", "c", "z"))
    chips = lax.axis_size("x") * lax.axis_size("y")
    experts = 2 * chips
    members = lax.axis_size("z")
    group = rows_n * members
    hidden = w_gate.shape[2]
    cols = width // members

    own = [w_gate[0].T, w_up[0].T]
    weights = own + [shift(w, "c", 1) for w in own]

    sent = jnp.concatenate([tokens, routing_columns(expert_ids, combine, experts)], axis=1)
    arrived = copies(sent, "z").reshape(group, width + LANES)
    group_tokens, meta = arrived[:, :width], arrived[:, width:]
    widened = group_tokens.astype(F32)
    normed = (
        widened * lax.rsqrt(jnp.mean(widened * widened, axis=-1, keepdims=True) + EPSILON)
    ).astype(BF)
    dense = jnp.concatenate([normed, meta], axis=1)

    lane = jnp.arange(LANES, dtype=jnp.int32)[None, :]
    e_own = (x * 4 + y) * 2 + c
    e_other = (x * 4 + y) * 2 + 1 - c
    masks = jnp.concatenate([lane == e_own, lane == e_other] + [lane < 0] * 6, axis=0).astype(F32)
    masks = masks.astype(BF)
    half = group // 2

    def first_ring(block, axis):
        mid = block.shape[0] // 2
        after, before = shift(block, axis, 1), shift(block, axis, -1)
        near = jnp.concatenate([block, after], axis=0)
        opposite = shift(before[:mid], axis, -1), shift(after[mid:], axis, 1)
        return near, jnp.concatenate([*opposite, before], axis=0)

    def second_ring(near, far, axis):
        near_after, near_before = shift(near, axis, 1), shift(near, axis, -1)
        far_after, far_before = shift(far, axis, 1), shift(far, axis, -1)
        opposite = shift(near_before, axis, -1), shift(far_after, axis, 1)
        return (near, far, near_after, far_after, near_before, far_before), opposite

    a_near, a_far = first_ring(dense[:half], "x")
    b_near, b_far = first_ring(dense[half:], "y")
    a_far, b_far, *weights = lax.optimization_barrier((a_far, b_far, *weights))
    _, _, down = lax.optimization_barrier((a_far[:8], b_far[:8], w_down[0]))
    down_own = lax.all_to_all(down, "z", 1, 0, tiled=True)
    down_own = down_own.reshape(members, hidden, cols)
    down_other = shift(down_own, "c", 1)
    a_early, a_late = second_ring(a_near, a_far, "y")
    b_early, b_late = second_ring(b_near, b_far, "x")
    place = jnp.stack([x, y]).astype(jnp.int32)
    early = expert_slots((*a_early, *b_early), True, place, masks, weights)
    early, *rest = lax.optimization_barrier((early, *a_late, *b_late))
    late = expert_slots(rest, False, place, masks, weights)
    early = lax.all_gather(early, "z", axis=0)
    late = copies(late, "z")
    result = lower(place, early, late, down_own, down_other, chips)
    per_chip = result.shape[2]
    result = result.reshape(chips, 2 * per_chip, cols)
    returned = lax.all_to_all(result, ("x", "y"), 0, 0, tiled=True)

    rank = meta[:, :experts].astype(F32)
    weight = sum(meta[:, i * experts : (i + 1) * experts].astype(F32) for i in (1, 2, 3))
    by_core = lambda v: v.reshape(group, chips, 2)
    order = lambda v: jnp.where(c == 0, by_core(v), by_core(v)[:, :, ::-1])
    rank, weight = order(rank), order(weight)
    slot = jnp.arange(per_chip, dtype=jnp.int32)
    mine = (slot // CAP)[None, :] == (jnp.arange(group) // rows_n)[:, None]
    hit = mine[:, None, None, :] & (
        rank[..., None] == (slot % CAP).astype(F32)[None, None, None, :]
    )
    spread = jnp.where(hit, weight[..., None], 0.0).reshape(group, chips * 2 * per_chip)
    mixture = jnp.dot(
        spread,
        returned.reshape(chips * 2 * per_chip, cols).astype(F32),
        precision=lax.Precision.HIGHEST,
        preferred_element_type=F32,
    )
    block_tokens = lax.dynamic_slice(group_tokens, (jnp.int32(0), z * cols), (group, cols))
    stream_block = (block_tokens.astype(F32) + mixture).astype(BF)
    group_stream = copies(stream_block, "z").transpose(1, 0, 2).reshape(group, width)
    stream = lax.dynamic_slice(group_stream, (z * rows_n, jnp.int32(0)), (rows_n, width))
    guard = attend(group_stream, w_query, w_key, w_value, cache_keys, cache_values, lengths)
    return (stream, guard)


def solution(mesh):
    torus = Mesh(mesh.devices.reshape(4, 4, 2, mesh.devices.shape[1]), ("x", "y", "c", "z"))
    ep = ("x", "y", "c")
    every = (*ep, "z")
    return jax.shard_map(
        per_device,
        mesh=torus,
        in_specs=(
            P(every, None),
            P(every, None),
            P(every, None),
            P(ep, None, "z"),
            P(ep, None, "z"),
            P(ep, "z", None),
            P(None, "z"),
            P(None, "z"),
            P(None, "z"),
            P(ep, "z", None, None),
            P(ep, "z", None, None),
            P(ep),
        ),
        out_specs=(P(every, None), P(ep, "z")),
        check_vma=False,
    )
```

profile of v0, /device:TPU:8, one launch (start us, length us, event | category | flops | bytes accessed | tf_op | source)
XLA Modules:
  0.0 220.2 jit_solution(4193576830784050415)
XLA Ops:
  7.2 0.9 fusion.19
  9.0 0.9 concatenate.21
  9.9 26.1 %all_to_all.36 = bf16[8,8,4224]{2,1,0:T(8,128)(2,1)S(1)} all-to-all(bf16[8,8,4224]{2,1,0:T(8,128)(2,1)S(1)} %broadcast_in_dim.45), channel_id=1, replica_groups=mesh['x'=4,'y'=4,'c'=2,'z'=8] {'z'}, dimensions={0} | all-to-all | bytes 1081344 | tf_op jit(solution)/shard_map/all_to_all | solution.py:26
  36.8 1.6 collective-permute-start.4
  39.4 1.3 copy.63
  40.7 3.6 %all-to-all-start.2 = ((bf16[192,8,512]{2,0,1:T(8,128)(2,1)}), bf16[192,8,512]{2,0,1:T(8,128)(2,1)S(1)}, u32[]{:S(2)}, u32[]{:S(2)}) async-start(bf16[192,8,512]{2,0,1:T(8,128)(2,1)} %bitcast.67), calls=%async_computation.2 | async-start | bytes 3145728 | tf_op jit(solution)/shard_map/all_to_all | solution.py:300
  44.3 1.6 collective-permute-start.1
  45.9 1.7 collective-permute-start
  47.7 1.7 collective-permute-start.5
  49.3 1.1 pad_maximum_fusion.3.refs_6_.refs_18_
  50.4 1.0 slice.65
  51.4 2.6 %collective-permute-done.1 = bf16[32,4224]{1,0:T(8,128)(2,1)S(1)} collective-permute-done((bf16[32,4224]{1,0:T(8,128)(2,1)S(1)}, bf16[32,4224]{1,0:T(8,128)(2,1)S(1)}, u32[]{:S(2)}, u32[]{:S(2)}) %collective-permute-start.1) | collective-permute-done | bytes 270368 | tf_op jit(solution)/shard_map/ppermute | solution.py:21
  54.0 1.7 collective-permute-start.7
  56.0 0.9 pad_maximum_fusion.refs_0_.refs_12_
  56.9 3.0 %collective-permute-start.3 = (bf16[16,4224]{1,0:T(8,128)(2,1)S(1)}, bf16[16,4224]{1,0:T(8,128)(2,1)S(1)}, u32[]{:S(2)}, u32[]{:S(2)}) collective-permute-start(bf16[16,4224]{1,0:T(8,128)(2,1)S(1)} %slice.63), channel_id=1, source_target_pairs={{0,192},{64,0},{128,64},{192,128},{1,193},{65,1},{129,65},{193,129... | collective-permute-start | bytes 405512 | tf_op jit(solution)/shard_map/ppermute | solution.py:21
  60.8 1.2 collective-permute-done.2
  62.0 2.1 collective-permute-start.14
  64.7 0.9 pad_maximum_fusion.1.refs_1_.refs_13_
  65.6 1.4 collective-permute-start.10
  67.0 3.0 %collective-permute-start.11 = (bf16[64,4224]{1,0:T(8,128)(2,1)}, bf16[64,4224]{1,0:T(8,128)(2,1)}, u32[]{:S(2)}, u32[]{:S(2)}) collective-permute-start(bf16[64,4224]{1,0:T(8,128)(2,1)} %pad_maximum_fusion.1.refs_1_.refs_13_), channel_id=1, source_target_pairs={{0,48},{16,0},{32,16},{48,32},{1,49},{17,1},{33,17},{49,33},{2,50}... | collective-permute-start | bytes 1622024 | tf_op jit(solution)/shard_map/ppermute | solution.py:21
  70.0 3.7 %collective-permute-done.16.refs_10_.refs_22_ = bf16[64,4224]{1,0:T(8,128)(2,1)S(1)} collective-permute-done((bf16[64,4224]{1,0:T(8,128)(2,1)S(1)}, bf16[64,4224]{1,0:T(8,128)(2,1)S(1)}, u32[]{:S(2)}, u32[]{:S(2)}) %collective-permute-start.16) | collective-permute-done | bytes 540704 | tf_op jit(solution)/shard_map/ppermute | solution.py:21
  74.3 4.2 %collective-permute-done.12.refs_4_.refs_16_ = bf16[64,4224]{1,0:T(8,128)(2,1)S(1)} collective-permute-done((bf16[64,4224]{1,0:T(8,128)(2,1)}, bf16[64,4224]{1,0:T(8,128)(2,1)S(1)}, u32[]{:S(2)}, u32[]{:S(2)}) %collective-permute-start.12) | collective-permute-done | bytes 540704 | tf_op jit(solution)/shard_map/ppermute | solution.py:21
  78.5 2.9 %collective-permute-start.15 = (bf16[64,4224]{1,0:T(8,128)(2,1)}, bf16[64,4224]{1,0:T(8,128)(2,1)}, u32[]{:S(2)}, u32[]{:S(2)}) collective-permute-start(bf16[64,4224]{1,0:T(8,128)(2,1)} %pad_maximum_fusion.2.refs_7_.refs_19_), channel_id=1, source_target_pairs={{0,192},{64,0},{128,64},{192,128},{1,193},{65,1},{129,65},{193,129... | collective-permute-start | bytes 1622024 | tf_op jit(solution)/shard_map/ppermute | solution.py:21
  82.4 7.5 %collective-permute-done.11.refs_3_.refs_15_ = bf16[64,4224]{1,0:T(8,128)(2,1)} collective-permute-done((bf16[64,4224]{1,0:T(8,128)(2,1)}, bf16[64,4224]{1,0:T(8,128)(2,1)}, u32[]{:S(2)}, u32[]{:S(2)}) %collective-permute-start.11) | collective-permute-done | bytes 540704 | tf_op jit(solution)/shard_map/ppermute | solution.py:21
  89.8 1.7 collective-permute-start.18
  91.9 1.5 collective-permute-start.21
  93.5 3.6 %collective-permute-done.17.refs_11_.refs_23_ = bf16[64,4224]{1,0:T(8,128)(2,1)} collective-permute-done((bf16[64,4224]{1,0:T(8,128)(2,1)}, bf16[64,4224]{1,0:T(8,128)(2,1)}, u32[]{:S(2)}, u32[]{:S(2)}) %collective-permute-start.17) | collective-permute-done | bytes 540704 | tf_op jit(solution)/shard_map/ppermute | solution.py:21
  97.1 1.0 copy-done.2
  98.1 1.0 copy-done.4
  99.2 1.0 copy-done.6
  100.2 11.1 %expert_slots.2 = bf16[288,384]{1,0:T(8,128)(2,1)} custom-call(s32[2]{0:T(128)S(1)} %pad_add_fusion.place_ref, bf16[8,128]{1,0:T(8,128)(2,1)S(1)} %convert_convert_fusion.mask_ref, bf16[64,4224]{1,0:T(8,128)(2,1)} %pad_maximum_fusion.refs_0_.refs_12_, bf16[64,4224]{1,0:T(8,128)(2,1)} %pad_maximum_fusion.1.refs_1_.refs_13_, ...), custom_call_target="tpu_custom_call" | custom-call | flops 4831838208 | bytes 12582912 | tf_op jit(solution)/shard_map/expert_slots/pallas_call | solution.py:101
  111.5 6.0 %expert_slots.3 = bf16[96,384]{1,0:T(8,128)(2,1)S(1)} custom-call(s32[2]{0:T(128)S(1)} %pad_add_fusion.place_ref, bf16[8,128]{1,0:T(8,128)(2,1)S(1)} %convert_convert_fusion.mask_ref, bf16[64,4224]{1,0:T(8,128)(2,1)} %collective-permute-done.18.refs_0_.refs_4_, bf16[64,4224]{1,0:T(8,128)(2,1)} %collective-permute-done.19.refs_1_.refs_5_, ...), custom_call_target="tpu_custom_call" | custom-call | flops 1610612736 | bytes 8388608 | tf_op jit(solution)/shard_map/expert_slots/pallas_call | solution.py:101
  117.5 0.9 broadcast_in_dim.48
  118.4 5.7 %all-to-all-start.1 = ((bf16[8,96,384]{2,1,0:T(8,128)(2,1)}), bf16[8,96,384]{2,1,0:T(8,128)(2,1)S(1)}, u32[]{:S(2)}, u32[]{:S(2)}) async-start(bf16[8,96,384]{2,1,0:T(8,128)(2,1)} %broadcast_in_dim.48), calls=%async_computation.1 | async-start | bytes 1179648 | tf_op jit(solution)/shard_map/all_to_all | solution.py:26
  124.2 24.1 %all-to-all-done.1.late_ref = bf16[8,96,384]{2,1,0:T(8,128)(2,1)S(1)} async-done(((bf16[8,96,384]{2,1,0:T(8,128)(2,1)}), bf16[8,96,384]{2,1,0:T(8,128)(2,1)S(1)}, u32[]{:S(2)}, u32[]{:S(2)}) %all-to-all-start.1) | async-done | bytes 589856 | tf_op jit(solution)/shard_map/all_to_all | solution.py:26
  148.3 10.4 %all-gather.3.cloned.1.call-done = bf16[2304,384]{1,0:T(8,128)(2,1)} async-done(((bf16[288,384]{1,0:T(8,128)(2,1)}), bf16[2304,384]{1,0:T(8,128)(2,1)}) %all-gather.3.cloned.1.call-update) | async-done | bytes 1769488 | tf_op jit(solution)/shard_map/all_gather | solution.py:309
  158.7 1.5 copy-done.7
  160.2 4.3 %lower.1 = bf16[16,2,24,512]{3,2,1,0:T(8,128)(2,1)} custom-call(s32[2]{0:T(128)S(1)} %pad_add_fusion.place_ref, bf16[8,288,384]{2,1,0:T(8,128)(2,1)S(1)} %bitcast.58, bf16[8,96,384]{2,1,0:T(8,128)(2,1)S(1)} %all-to-all-done.1.late_ref, bf16[8,192,512]{2,1,0:T(8,128)(2,1)S(1)} %bitcast.57, bf16[8,192,512]{2,1,0:T(8,128)(2,1)} %collective-permute-done.22.other_ref), custom_call_target="tpu_custom_call" | custom-call | flops 1207959552 | bytes 5505024 | tf_op jit(solution)/shard_map/lower/pallas_call | solution.py:157
  164.4 7.5 %all-to-all-start.3 = ((bf16[16,48,512]{2,1,0:T(8,128)(2,1)}), bf16[16,48,512]{2,1,0:T(8,128)(2,1)S(1)}, u32[]{:S(2)}, u32[]{:S(2)}) async-start(bf16[16,48,512]{2,1,0:T(8,128)(2,1)} %bitcast.15), calls=%async_computation.3 | async-start | bytes 1572864 | tf_op jit(solution)/shard_map/all_to_all | solution.py:314
  172.5 10.1 %all-to-all-done.3 = bf16[16,48,512]{2,1,0:T(8,128)(2,1)S(1)} async-done(((bf16[16,48,512]{2,1,0:T(8,128)(2,1)}), bf16[16,48,512]{2,1,0:T(8,128)(2,1)S(1)}, u32[]{:S(2)}, u32[]{:S(2)}) %all-to-all-start.3) | async-done | bytes 786464 | tf_op jit(solution)/shard_map/all_to_all | solution.py:314
  183.1 0.8 broadcast_in_dim.49
  183.9 4.0 %all-to-all-start.4 = ((bf16[8,64,512]{2,1,0:T(8,128)(2,1)}), bf16[8,64,512]{2,1,0:T(8,128)(2,1)S(1)}, u32[]{:S(2)}, u32[]{:S(2)}) async-start(bf16[8,64,512]{2,1,0:T(8,128)(2,1)} %broadcast_in_dim.49), calls=%async_computation.4 | async-start | bytes 1048576 | tf_op jit(solution)/shard_map/all_to_all | solution.py:26
  187.9 6.4 %copy.49 = bf16[512,4096]{1,0:T(8,128)(2,1)} copy(bf16[512,4096]{0,1:T(8,128)(2,1)} %bitcast.71) | data formatting | bytes 8388608 | tf_op jit(solution)/shard_map/reshape.127
  194.4 7.5 %all-to-all-done.4 = bf16[8,64,512]{2,1,0:T(8,128)(2,1)S(1)} async-done(((bf16[8,64,512]{2,1,0:T(8,128)(2,1)}), bf16[8,64,512]{2,1,0:T(8,128)(2,1)S(1)}, u32[]{:S(2)}, u32[]{:S(2)}) %all-to-all-start.4) | async-done | bytes 524320 | tf_op jit(solution)/shard_map/all_to_all | solution.py:26
  202.9 1.6 fusion.4
  204.5 3.7 %fusion.26 = f32[64,4,128]{2,0,1:T(8,128)S(1)} fusion(bf16[64,4096,1]{1,0,2:T(8,128)(2,1)S(1)} %reshape.297, bf16[4,128,4096]{2,1,0:T(8,128)(2,1)} %bitcast.59), kind=kOutput, calls=%fused_computation.79 | convolution fusion | flops 268435456 | bytes 4849664 | tf_op jit(solution)/shard_map/dot_general | solution.py:183
  208.6 1.8 fusion.25
  211.1 1.0 fusion.2
  (109 shorter events, 11.1 us)
Async XLA Ops:
  7.2 203.9 %copy-start = (bf16[64,1,64,128]{3,2,1,0:T(8,128)(2,1)S(1)}, bf16[64,1,64,128]{3,2,1,0:T(8,128)(2,1)}, u32[]{:S(2)}) copy-start(bf16[64,1,64,128]{3,2,1,0:T(8,128)(2,1)} %param.22) | copy-start | bytes 3145732
  36.1 0.8 copy-start.8
  36.3 3.1 %copy-start.10 = (bf16[1,192,4096]{2,1,0:T(8,128)(2,1)S(1)}, bf16[1,192,4096]{2,1,0:T(8,128)(2,1)}, u32[]{:S(2)}) copy-start(bf16[1,192,4096]{2,1,0:T(8,128)(2,1)} %param.17) | copy-start | bytes 4718596
  36.8 3.8 %copy-start.11 = (bf16[32,4224]{1,0:T(8,128)(2,1)}, bf16[32,4224]{1,0:T(8,128)(2,1)S(1)}, u32[]{:S(2)}) copy-start(bf16[32,4224]{1,0:T(8,128)(2,1)S(1)} %get-tuple-element.24) | copy-start | bytes 811012
  36.8 9.1 %collective-permute-start.4 = (bf16[32,4224]{1,0:T(8,128)(2,1)S(1)}, bf16[32,4224]{1,0:T(8,128)(2,1)S(1)}, u32[]{:S(2)}, u32[]{:S(2)}) collective-permute-start(bf16[32,4224]{1,0:T(8,128)(2,1)S(1)} %get-tuple-element.24), channel_id=1, source_target_pairs={{0,16},{16,32},{32,48},{48,0},{1,17},{17,33},{33,49},{49,1},{2,18}... | collective-permute-start | bytes 811016 | tf_op jit(solution)/shard_map/ppermute | solution.py:21
  38.4 9.2 %collective-permute-start.6 = (bf16[32,4224]{1,0:T(8,128)(2,1)S(1)}, bf16[32,4224]{1,0:T(8,128)(2,1)}, u32[]{:S(2)}, u32[]{:S(2)}) collective-permute-start(bf16[32,4224]{1,0:T(8,128)(2,1)S(1)} %get-tuple-element.24), channel_id=1, source_target_pairs={{0,48},{16,0},{32,16},{48,32},{1,49},{17,1},{33,17},{49,33},{2,50}... | collective-permute-start | bytes 811016 | tf_op jit(solution)/shard_map/ppermute | solution.py:21
  38.9 26.7 %collective-permute-start.8 = (bf16[192,4096]{1,0:T(8,128)(2,1)}, bf16[192,4096]{1,0:T(8,128)(2,1)}, u32[]{:S(2)}, u32[]{:S(2)}) collective-permute-start(bf16[192,4096]{1,0:T(8,128)(2,1)} %bitcast.7.refs_24_.refs_8_), channel_id=1, source_target_pairs={{0,8},{8,0},{1,9},{9,1},{2,10},{10,2},{3,11},{11,3},{4,12},{12,4},... | collective-permute-start | bytes 4718600 | tf_op jit(solution)/shard_map/ppermute | solution.py:21
  38.9 28.1 %collective-permute-start.9 = (bf16[192,4096]{1,0:T(8,128)(2,1)}, bf16[192,4096]{1,0:T(8,128)(2,1)}, u32[]{:S(2)}, u32[]{:S(2)}) collective-permute-start(bf16[192,4096]{1,0:T(8,128)(2,1)} %bitcast.9.refs_25_.refs_9_), channel_id=1, source_target_pairs={{0,8},{8,0},{1,9},{9,1},{2,10},{10,2},{3,11},{11,3},{4,12},{12,4},... | collective-permute-start | bytes 4718600 | tf_op jit(solution)/shard_map/ppermute | solution.py:21
  40.7 70.7 %all-to-all-start.2 = ((bf16[192,8,512]{2,0,1:T(8,128)(2,1)}), bf16[192,8,512]{2,0,1:T(8,128)(2,1)S(1)}, u32[]{:S(2)}, u32[]{:S(2)}) async-start(bf16[192,8,512]{2,0,1:T(8,128)(2,1)} %bitcast.67), calls=%async_computation.2 | async-start | bytes 3145728 | tf_op jit(solution)/shard_map/all_to_all | solution.py:300
  44.3 114.4 %all-gather.3.cloned.1.call-start = ((), (), s32[]{:S(2)}) async-start(), calls=%async_computation.5 | async-start | bytes 1990656 | tf_op jit(solution)/shard_map/all_gather | solution.py:309
  44.3 9.7 %collective-permute-start.1 = (bf16[32,4224]{1,0:T(8,128)(2,1)S(1)}, bf16[32,4224]{1,0:T(8,128)(2,1)S(1)}, u32[]{:S(2)}, u32[]{:S(2)}) collective-permute-start(bf16[32,4224]{1,0:T(8,128)(2,1)S(1)} %get-tuple-element.25), channel_id=1, source_target_pairs={{0,64},{64,128},{128,192},{192,0},{1,65},{65,129},{129,193},{193,1... | collective-permute-start | bytes 811016 | tf_op jit(solution)/shard_map/ppermute | solution.py:21
  45.9 1.8 copy-start.14
  45.9 9.8 %collective-permute-start = (bf16[32,4224]{1,0:T(8,128)(2,1)S(1)}, bf16[32,4224]{1,0:T(8,128)(2,1)S(1)}, u32[]{:S(2)}, u32[]{:S(2)}) collective-permute-start(bf16[32,4224]{1,0:T(8,128)(2,1)S(1)} %get-tuple-element.25), channel_id=1, source_target_pairs={{0,192},{64,0},{128,64},{192,128},{1,193},{65,1},{129,65},{193,129... | collective-permute-start | bytes 811016 | tf_op jit(solution)/shard_map/ppermute | solution.py:21
  47.7 9.2 %collective-permute-start.5 = (bf16[16,4224]{1,0:T(8,128)(2,1)S(1)}, bf16[16,4224]{1,0:T(8,128)(2,1)S(1)}, u32[]{:S(2)}, u32[]{:S(2)}) collective-permute-start(bf16[16,4224]{1,0:T(8,128)(2,1)S(1)} %slice.64), channel_id=1, source_target_pairs={{0,16},{16,32},{32,48},{48,0},{1,17},{17,33},{33,49},{49,1},{2,18}... | collective-permute-start | bytes 405512 | tf_op jit(solution)/shard_map/ppermute | solution.py:21
  50.4 9.6 %copy-start.15 = (bf16[32,4224]{1,0:T(8,128)(2,1)S(1)}, bf16[32,4224]{1,0:T(8,128)(2,1)}, u32[]{:S(2)}) copy-start(bf16[32,4224]{1,0:T(8,128)(2,1)} %copy-done.14) | copy-start | bytes 811012
  54.0 6.0 %collective-permute-start.7 = (bf16[16,4224]{1,0:T(8,128)(2,1)S(1)}, bf16[16,4224]{1,0:T(8,128)(2,1)S(1)}, u32[]{:S(2)}, u32[]{:S(2)}) collective-permute-start(bf16[16,4224]{1,0:T(8,128)(2,1)S(1)} %slice.65), channel_id=1, source_target_pairs={{0,48},{16,0},{32,16},{48,32},{1,49},{17,1},{33,17},{49,33},{2,50}... | collective-permute-start | bytes 405512 | tf_op jit(solution)/shard_map/ppermute | solution.py:21
  55.7 6.3 %collective-permute-start.2 = (bf16[16,4224]{1,0:T(8,128)(2,1)S(1)}, bf16[16,4224]{1,0:T(8,128)(2,1)S(1)}, u32[]{:S(2)}, u32[]{:S(2)}) collective-permute-start(bf16[16,4224]{1,0:T(8,128)(2,1)S(1)} %slice.62), channel_id=1, source_target_pairs={{0,64},{64,128},{128,192},{192,0},{1,65},{65,129},{129,193},{193,1... | collective-permute-start | bytes 405512 | tf_op jit(solution)/shard_map/ppermute | solution.py:21
  56.9 7.1 %collective-permute-start.3 = (bf16[16,4224]{1,0:T(8,128)(2,1)S(1)}, bf16[16,4224]{1,0:T(8,128)(2,1)S(1)}, u32[]{:S(2)}, u32[]{:S(2)}) collective-permute-start(bf16[16,4224]{1,0:T(8,128)(2,1)S(1)} %slice.63), channel_id=1, source_target_pairs={{0,192},{64,0},{128,64},{192,128},{1,193},{65,1},{129,65},{193,129... | collective-permute-start | bytes 405512 | tf_op jit(solution)/shard_map/ppermute | solution.py:21
  60.0 13.7 %collective-permute-start.16 = (bf16[64,4224]{1,0:T(8,128)(2,1)S(1)}, bf16[64,4224]{1,0:T(8,128)(2,1)S(1)}, u32[]{:S(2)}, u32[]{:S(2)}) collective-permute-start(bf16[64,4224]{1,0:T(8,128)(2,1)S(1)} %pad_maximum_fusion.3.refs_6_.refs_18_), channel_id=1, source_target_pairs={{0,64},{64,128},{128,192},{192,0},{1,65},{65,129},{129,193},{193,1... | collective-permute-start | bytes 1622024 | tf_op jit(solution)/shard_map/ppermute | solution.py:21
  62.0 19.4 %collective-permute-start.14 = (bf16[64,4224]{1,0:T(8,128)(2,1)S(1)}, bf16[64,4224]{1,0:T(8,128)(2,1)S(1)}, u32[]{:S(2)}, u32[]{:S(2)}) collective-permute-start(bf16[64,4224]{1,0:T(8,128)(2,1)S(1)} %pad_maximum_fusion.3.refs_6_.refs_18_), channel_id=1, source_target_pairs={{0,192},{64,0},{128,64},{192,128},{1,193},{65,1},{129,65},{193,129... | collective-permute-start | bytes 1622024 | tf_op jit(solution)/shard_map/ppermute | solution.py:21
  64.0 14.5 %collective-permute-start.12 = (bf16[64,4224]{1,0:T(8,128)(2,1)}, bf16[64,4224]{1,0:T(8,128)(2,1)S(1)}, u32[]{:S(2)}, u32[]{:S(2)}) collective-permute-start(bf16[64,4224]{1,0:T(8,128)(2,1)} %pad_maximum_fusion.refs_0_.refs_12_), channel_id=1, source_target_pairs={{0,16},{16,32},{32,48},{48,0},{1,17},{17,33},{33,49},{49,1},{2,18}... | collective-permute-start | bytes 1622024 | tf_op jit(solution)/shard_map/ppermute | solution.py:21
  65.6 16.7 %collective-permute-start.10 = (bf16[64,4224]{1,0:T(8,128)(2,1)}, bf16[64,4224]{1,0:T(8,128)(2,1)}, u32[]{:S(2)}, u32[]{:S(2)}) collective-permute-start(bf16[64,4224]{1,0:T(8,128)(2,1)} %pad_maximum_fusion.refs_0_.refs_12_), channel_id=1, source_target_pairs={{0,48},{16,0},{32,16},{48,32},{1,49},{17,1},{33,17},{49,33},{2,50}... | collective-permute-start | bytes 1622024 | tf_op jit(solution)/shard_map/ppermute | solution.py:21
  67.0 22.9 %collective-permute-start.11 = (bf16[64,4224]{1,0:T(8,128)(2,1)}, bf16[64,4224]{1,0:T(8,128)(2,1)}, u32[]{:S(2)}, u32[]{:S(2)}) collective-permute-start(bf16[64,4224]{1,0:T(8,128)(2,1)} %pad_maximum_fusion.1.refs_1_.refs_13_), channel_id=1, source_target_pairs={{0,48},{16,0},{32,16},{48,32},{1,49},{17,1},{33,17},{49,33},{2,50}... | collective-permute-start | bytes 1622024 | tf_op jit(solution)/shard_map/ppermute | solution.py:21
  73.7 7.7 %copy-start.1 = (bf16[64,4224]{1,0:T(8,128)(2,1)}, bf16[64,4224]{1,0:T(8,128)(2,1)S(1)}, u32[]{:S(2)}) copy-start(bf16[64,4224]{1,0:T(8,128)(2,1)S(1)} %collective-permute-done.16.refs_10_.refs_22_) | copy-start | bytes 1622020
  73.7 17.9 %collective-permute-start.13 = (bf16[64,4224]{1,0:T(8,128)(2,1)}, bf16[64,4224]{1,0:T(8,128)(2,1)}, u32[]{:S(2)}, u32[]{:S(2)}) collective-permute-start(bf16[64,4224]{1,0:T(8,128)(2,1)} %pad_maximum_fusion.1.refs_1_.refs_13_), channel_id=1, source_target_pairs={{0,16},{16,32},{32,48},{48,0},{1,17},{17,33},{33,49},{49,1},{2,18}... | collective-permute-start | bytes 1622024 | tf_op jit(solution)/shard_map/ppermute | solution.py:21
  78.5 3.7 %copy-start.3 = (bf16[64,4224]{1,0:T(8,128)(2,1)}, bf16[64,4224]{1,0:T(8,128)(2,1)S(1)}, u32[]{:S(2)}) copy-start(bf16[64,4224]{1,0:T(8,128)(2,1)S(1)} %collective-permute-done.12.refs_4_.refs_16_) | copy-start | bytes 1622020
  78.5 13.4 %collective-permute-start.15 = (bf16[64,4224]{1,0:T(8,128)(2,1)}, bf16[64,4224]{1,0:T(8,128)(2,1)}, u32[]{:S(2)}, u32[]{:S(2)}) collective-permute-start(bf16[64,4224]{1,0:T(8,128)(2,1)} %pad_maximum_fusion.2.refs_7_.refs_19_), channel_id=1, source_target_pairs={{0,192},{64,0},{128,64},{192,128},{1,193},{65,1},{129,65},{193,129... | collective-permute-start | bytes 1622024 | tf_op jit(solution)/shard_map/ppermute | solution.py:21
  81.4 0.8 copy-start.5
  82.2 14.9 %collective-permute-start.17 = (bf16[64,4224]{1,0:T(8,128)(2,1)}, bf16[64,4224]{1,0:T(8,128)(2,1)}, u32[]{:S(2)}, u32[]{:S(2)}) collective-permute-start(bf16[64,4224]{1,0:T(8,128)(2,1)} %pad_maximum_fusion.2.refs_7_.refs_19_), channel_id=1, source_target_pairs={{0,64},{64,128},{128,192},{192,0},{1,65},{65,129},{129,193},{193,1... | collective-permute-start | bytes 1622024 | tf_op jit(solution)/shard_map/ppermute | solution.py:21
  82.3 29.1 %collective-permute-start.20 = (bf16[64,4224]{1,0:T(8,128)(2,1)}, bf16[64,4224]{1,0:T(8,128)(2,1)}, u32[]{:S(2)}, u32[]{:S(2)}) collective-permute-start(bf16[64,4224]{1,0:T(8,128)(2,1)} %copy-done.1), channel_id=1, source_target_pairs={{0,64},{64,128},{128,192},{192,0},{1,65},{65,129},{129,193},{193,1... | collective-permute-start | bytes 1622024 | tf_op jit(solution)/shard_map/ppermute | solution.py:21
  89.8 21.5 %collective-permute-start.18 = (bf16[64,4224]{1,0:T(8,128)(2,1)}, bf16[64,4224]{1,0:T(8,128)(2,1)}, u32[]{:S(2)}, u32[]{:S(2)}) collective-permute-start(bf16[64,4224]{1,0:T(8,128)(2,1)} %copy-done.3), channel_id=1, source_target_pairs={{0,16},{16,32},{32,48},{48,0},{1,17},{17,33},{33,49},{49,1},{2,18}... | collective-permute-start | bytes 1622024 | tf_op jit(solution)/shard_map/ppermute | solution.py:21
  91.6 19.8 %collective-permute-start.19 = (bf16[64,4224]{1,0:T(8,128)(2,1)}, bf16[64,4224]{1,0:T(8,128)(2,1)}, u32[]{:S(2)}, u32[]{:S(2)}) collective-permute-start(bf16[64,4224]{1,0:T(8,128)(2,1)} %collective-permute-done.11.refs_3_.refs_15_), channel_id=1, source_target_pairs={{0,48},{16,0},{32,16},{48,32},{1,49},{17,1},{33,17},{49,33},{2,50}... | collective-permute-start | bytes 1622024 | tf_op jit(solution)/shard_map/ppermute | solution.py:21
  91.9 19.5 %collective-permute-start.21 = (bf16[64,4224]{1,0:T(8,128)(2,1)}, bf16[64,4224]{1,0:T(8,128)(2,1)}, u32[]{:S(2)}, u32[]{:S(2)}) collective-permute-start(bf16[64,4224]{1,0:T(8,128)(2,1)} %collective-permute-done.15.refs_9_.refs_21_), channel_id=1, source_target_pairs={{0,192},{64,0},{128,64},{192,128},{1,193},{65,1},{129,65},{193,129... | collective-permute-start | bytes 1622024 | tf_op jit(solution)/shard_map/ppermute | solution.py:21
  97.1 1.0 copy-start.2
  98.1 1.0 copy-start.4
  99.2 1.0 copy-start.6
  111.4 36.9 %collective-permute-start.22 = (bf16[8,192,512]{2,1,0:T(8,128)(2,1)S(1)}, bf16[8,192,512]{2,1,0:T(8,128)(2,1)}, u32[]{:S(2)}, u32[]{:S(2)}) collective-permute-start(bf16[8,192,512]{2,1,0:T(8,128)(2,1)S(1)} %bitcast.56), channel_id=1, source_target_pairs={{0,8},{8,0},{1,9},{9,1},{2,10},{10,2},{3,11},{11,3},{4,12},{12,4},... | collective-permute-start | bytes 4718600 | tf_op jit(solution)/shard_map/ppermute | solution.py:21
  118.4 30.0 %all-to-all-start.1 = ((bf16[8,96,384]{2,1,0:T(8,128)(2,1)}), bf16[8,96,384]{2,1,0:T(8,128)(2,1)S(1)}, u32[]{:S(2)}, u32[]{:S(2)}) async-start(bf16[8,96,384]{2,1,0:T(8,128)(2,1)} %broadcast_in_dim.48), calls=%async_computation.1 | async-start | bytes 1179648 | tf_op jit(solution)/shard_map/all_to_all | solution.py:26
  158.7 1.5 copy-start.7
  164.4 7.5 %copy-start.9 = (bf16[8,8,4224]{2,1,0:T(8,128)(2,1)S(1)}, bf16[8,8,4224]{2,1,0:T(8,128)(2,1)}, u32[]{:S(2)}) copy-start(bf16[8,8,4224]{2,1,0:T(8,128)(2,1)} %copy-done.8) | copy-start | bytes 1622020
  164.4 18.1 %all-to-all-start.3 = ((bf16[16,48,512]{2,1,0:T(8,128)(2,1)}), bf16[16,48,512]{2,1,0:T(8,128)(2,1)S(1)}, u32[]{:S(2)}, u32[]{:S(2)}) async-start(bf16[16,48,512]{2,1,0:T(8,128)(2,1)} %bitcast.15), calls=%async_computation.3 | async-start | bytes 1572864 | tf_op jit(solution)/shard_map/all_to_all | solution.py:314
  183.9 18.0 %all-to-all-start.4 = ((bf16[8,64,512]{2,1,0:T(8,128)(2,1)}), bf16[8,64,512]{2,1,0:T(8,128)(2,1)S(1)}, u32[]{:S(2)}, u32[]{:S(2)}) async-start(bf16[8,64,512]{2,1,0:T(8,128)(2,1)} %broadcast_in_dim.49), calls=%async_computation.4 | async-start | bytes 1048576 | tf_op jit(solution)/shard_map/all_to_all | solution.py:26
  187.9 6.4 %copy-start.16 = (s32[64]{0:T(128)S(1)}, s32[64]{0:T(128)}, u32[]{:S(2)}) copy-start(s32[64]{0:T(128)} %param.23) | copy-start | bytes 772
  204.5 4.1 %copy-start.12 = (bf16[64,1,64,128]{3,2,1,0:T(8,128)(2,1)S(1)}, bf16[64,1,64,128]{3,2,1,0:T(8,128)(2,1)}, u32[]{:S(2)}) copy-start(bf16[64,1,64,128]{3,2,1,0:T(8,128)(2,1)} %param.21) | copy-start | bytes 3145732
  208.2 2.5 %copy-start.13 = (bf16[4096,128]{1,0:T(8,128)(2,1)S(1)}, bf16[4096,128]{1,0:T(8,128)(2,1)}, u32[]{:S(2)}) copy-start(bf16[4096,128]{1,0:T(8,128)(2,1)} %param.20) | copy-start | bytes 3145732
Sparse Core Ops, SparseCore 0:
  111.5 47.1 all-gather.2
where the time goes:
time: 221 us; the launch traced here: 220 us
  waiting for transfers between devices  75 us (34%)
  starting transfers between devices  47.7 us (22%)
  blocking collectives  26.1 us (12%)
  Pallas kernels  21.3 us (10%)
  local copies, waits for them, and re-layouts  19.4 us (9%)
  between operations  14.4 us (7%)
  matrix products  9.26 us (4%)
  other arithmetic  7.03 us (3%)
    all_to_all x2, waiting for transfers between devices, copies(): lax.all_to_all(jnp.broadcast_to(values[None], (size, *values.shape)), axi...  31.6 us
    ppermute x23, starting transfers between devices, shift(): lax.ppermute(values, axis, [(i, (i - step) % size) for i in range(size)])  26.9 us
    all_to_all x1, blocking collectives, copies(): lax.all_to_all(jnp.broadcast_to(values[None], (size, *values.shape)), axi...  26.1 us
    ppermute x23, waiting for transfers between devices, shift(): lax.ppermute(values, axis, [(i, (i - step) % size) for i in range(size)])  22.9 us
    pallas_call x2, Pallas kernels, expert_slots(): pl.pallas_call(functools.partial(expert_kernel, sizes, early, steps), gri...  17.1 us
    all_gather x1, waiting for transfers between devices, per_device(): early = lax.all_gather(early, 'z', axis=0)  10.4 us
    all_to_all x1, waiting for transfers between devices, per_device(): returned = lax.all_to_all(result, ('x', 'y'), 0, 0, tiled=True)  10.1 us
    all_to_all x2, starting transfers between devices, copies(): lax.all_to_all(jnp.broadcast_to(values[None], (size, *values.shape)), axi...  9.7 us
  transfers between devices with their start and end apart: 28, of which 10 were waited for; matrix products, arithmetic and copies ran while one was open for 6% of the time, Pallas kernels for 8%

commit v1 on v0

v1 whole, which is shorter than its diff:
```python
import functools
import math

import jax
import jax.numpy as jnp
from jax import lax
from jax.experimental import pallas as pl
from jax.experimental.pallas import tpu as pltpu
from jax.sharding import Mesh
from jax.sharding import PartitionSpec as P

EPSILON = 1e-06
BF = jnp.bfloat16
F32 = jnp.float32
LANES = 128
CAP = 3


def shift(values, axis, step):
    size = lax.axis_size(axis)
    return lax.ppermute(values, axis, [(i, (i - step) % size) for i in range(size)])


def ring(block, axis):
    size = lax.axis_size(axis)
    pieces = [block] + [None] * (size - 1)
    after = before = block
    for d in range(1, size // 2):
        after, before = shift(after, axis, 1), shift(before, axis, -1)
        pieces[d], pieces[size - d] = after, before
    mid = block.shape[0] // 2
    farthest = shift(after[:mid], axis, 1), shift(before[mid:], axis, -1)
    pieces[size // 2] = jnp.concatenate(farthest, axis=0)
    return pieces


def copies(values, axis):
    size = lax.axis_size(axis)
    return lax.all_to_all(
        jnp.broadcast_to(values[None], (size, *values.shape)), axis, 0, 0, tiled=True
    )


def expert_kernel(sizes, steps, mask_ref, *refs):
    n = len(sizes)
    rows, meta = refs[:n], refs[n : 2 * n]
    w_refs = refs[2 * n : 2 * n + 4]
    out_ref, joined, totals = refs[2 * n + 4 :]
    k = pl.program_id(0)
    hidden = w_refs[0].shape[0]
    at = 0
    for m, row_ref in zip(sizes, rows):
        joined[at : at + m, :] = row_ref[...]
        at += m
    part = lax.dot_general(
        joined[...],
        jnp.concatenate([w_ref[...] for w_ref in w_refs], axis=0),
        (((1,), (1,)), ((), ())),
        preferred_element_type=F32,
    )

    @pl.when(k == 0)
    def _():
        totals[...] = part

    @pl.when(k > 0)
    def _():
        totals[...] += part

    @pl.when(k == steps - 1)
    def _():
        slots = out_ref.shape[0]
        held = lax.dot_general(
            mask_ref[...],
            jnp.concatenate([m_ref[...] for m_ref in meta], axis=0),
            (((1,), (1,)), ((), ())),
            preferred_element_type=F32,
        )
        s = lax.broadcasted_iota(jnp.int32, (slots, 1), 0)
        same = lax.broadcasted_iota(jnp.int32, (slots, at), 1) // 8 == s // CAP
        rank = (s % CAP).astype(F32)
        for j in range(2):
            base = 2 * j * hidden
            gate = totals[:, base : base + hidden]
            up = totals[:, base + hidden : base + 2 * hidden]
            active = (gate / (1.0 + jnp.exp(-gate)) * up).astype(BF)
            pick = jnp.where(same & (held[j : j + 1, :] == rank), 1.0, 0.0).astype(BF)
            packed = jnp.dot(pick, active, preferred_element_type=F32)
            out_ref[:, j * hidden : (j + 1) * hidden] = packed.astype(BF)


def expert_slots(pieces, masks, weights):
    hidden, depth = weights[0].shape
    chunk = 1024
    steps = depth // chunk
    sizes = tuple(p.shape[0] for p in pieces)
    in_specs = [pl.BlockSpec((8, LANES), lambda k: (0, 0))]
    in_specs += [pl.BlockSpec((m, chunk), lambda k: (0, k)) for m in sizes]
    in_specs += [pl.BlockSpec((m, LANES), lambda k: (0, depth // LANES)) for m in sizes]
    in_specs += [pl.BlockSpec((hidden, chunk), lambda k: (0, k))] * 4
    in_hbm = lambda arrays: [pltpu.with_memory_space_constraint(a, pltpu.HBM) for a in arrays]
    pieces, weights = in_hbm(pieces), in_hbm(weights)
    total = sum(sizes)
    slots = total // 8 * CAP
    return pl.pallas_call(
        functools.partial(expert_kernel, sizes, steps),
        grid=(steps,),
        in_specs=in_specs,
        out_specs=pl.BlockSpec((slots, 2 * hidden), lambda k: (0, 0)),
        out_shape=jax.ShapeDtypeStruct((slots, 2 * hidden), BF),
        scratch_shapes=[
            pltpu.VMEM((total, chunk), BF),
            pltpu.VMEM((total, 4 * hidden), F32),
        ],
        compiler_params=pltpu.CompilerParams(vmem_limit_bytes=20 << 20),
        cost_estimate=pl.CostEstimate(
            flops=8 * total * depth * hidden,
            bytes_accessed=8 * depth * hidden + 2 * total * depth,
            transcendentals=2 * total * hidden,
        ),
        name="expert_slots",
    )(masks, *pieces, *pieces, *weights)


PIECES = (
    *((h, 0, i) for h in (0, 1) for i in (0, 2)),
    *((h, o, 0) for h in (0, 1) for o in (1, 3)),
    *((h, o, 2) for h in (0, 1) for o in (1, 3)),
    *((h, 2, i) for h in (0, 1) for i in (0, 2)),
)


def lower_kernel(place_ref, near_ref, own_ref, other_ref, *refs):
    members, hidden, _ = own_ref.shape
    rest_refs, (out_ref, *sums, placed) = refs[:members], refs[members:]
    first = near_ref.shape[1]
    z = place_ref[2]
    for j, w_ref in enumerate((own_ref, other_ref)):
        span = slice(j * hidden, (j + 1) * hidden)
        for d in range(members):
            at = (z + d) % members
            near = jnp.dot(near_ref[d][:, span], w_ref[d], preferred_element_type=F32)
            rest = jnp.dot(rest_refs[d][:, span], w_ref[at], preferred_element_type=F32)
            if d == 0:
                sums[j][:first, :] = near
                sums[j][first:, :] = rest
            else:
                sums[j][:first, :] += near
                sums[j][first:, :] += rest
    x, y = place_ref[0], place_ref[1]
    per = placed.shape[2] // 2
    for p, (h, outer, inner) in enumerate(PIECES):
        for i in range(2):
            at = (2 * p + i) * per
            if h == 0:
                chip = (x + inner + i) % 4 * 4 + (y + outer) % 4
            else:
                chip = (x + outer) % 4 * 4 + (y + inner + i) % 4
            for j in range(2):
                placed[chip, j, h * per : (h + 1) * per, :] = sums[j][at : at + per, :]
    out_ref[...] = placed[...].astype(BF)


def lower(place, near, rest, down_own, down_other, chips):
    members, hidden, cols = down_own.shape
    slots = near.shape[1] + rest[0].shape[0]
    per_chip = slots // chips
    return pl.pallas_call(
        lower_kernel,
        in_specs=[pl.BlockSpec(memory_space=pltpu.SMEM)]
        + [pl.BlockSpec(memory_space=pltpu.VMEM)] * (3 + members),
        out_specs=pl.BlockSpec(memory_space=pltpu.VMEM),
        out_shape=jax.ShapeDtypeStruct((chips, 2, per_chip, cols), BF),
        scratch_shapes=[
            pltpu.VMEM((slots, cols), F32),
            pltpu.VMEM((slots, cols), F32),
            pltpu.VMEM((chips, 2, per_chip, cols), F32),
        ],
        compiler_params=pltpu.CompilerParams(vmem_limit_bytes=16 << 20),
        cost_estimate=pl.CostEstimate(
            flops=4 * members * slots * hidden * cols,
            bytes_accessed=4 * members * hidden * (slots + cols),
            transcendentals=0,
        ),
        name="lower",
    )(place, near, down_own, down_other, *rest)


def attend_kernel(
    stream_ref, wq_ref, wk_ref, wv_ref, keys_ref, values_ref, start_ref, out_ref, normed, spread, own, fresh
):
    members, rows, cols = stream_ref.shape
    heads, size = out_ref.shape[1] // keys_ref.shape[2], keys_ref.shape[2]
    width = members * cols
    total = jnp.zeros((rows, 1), F32)
    for i in range(members):
        block = stream_ref[i].astype(F32)
        total += jnp.sum(block * block, axis=1, keepdims=True)
    scale = lax.rsqrt(total / width + EPSILON)
    for i in range(members):
        normed[:, i * cols : (i + 1) * cols] = (stream_ref[i].astype(F32) * scale).astype(BF)
    project = lambda w_ref: jnp.dot(normed[...], w_ref[...], preferred_element_type=F32)
    queries = project(wq_ref)
    key_new = project(wk_ref).astype(BF).astype(F32)
    value_new = project(wv_ref).astype(BF).astype(F32)
    pad = spread.shape[1] // 3
    factor = 1.0 / math.sqrt(size)
    for h in range(heads):
        query = queries[:, h * size : (h + 1) * size]
        for i, part in enumerate(split3(query)):
            spread[:, pad * i + h, :] = part.astype(F32)
        mine = jnp.sum(query * key_new, axis=1, keepdims=True) * factor
        own[:, h, :] = jnp.broadcast_to(mine, (rows, size))
        fresh[:, h, :] = value_new
    for h in range(heads, pad):
        for i in range(3):
            spread[:, pad * i + h, :] = jnp.zeros((rows, size), F32)
        own[:, h, :] = jnp.zeros((rows, size), F32)
        fresh[:, h, :] = jnp.zeros((rows, size), F32)

    def parts_dot(parts, cached, dim):
        result = lax.dot_general(
            parts.astype(BF), cached, (((2,), (dim,)), ((0,), (0,))), preferred_element_type=F32
        )
        return result[:, :pad] + result[:, pad : 2 * pad] + result[:, 2 * pad :]

    scores = parts_dot(spread[...], keys_ref[...], 2) * factor
    window = scores.shape[2]
    allowed = lax.broadcasted_iota(jnp.int32, scores.shape, 2) >= start_ref[...]
    masked = jnp.where(allowed, scores, -jnp.inf)
    own_score = own[...]
    highest = jnp.maximum(jnp.max(masked, axis=2, keepdims=True), own_score[:, :, :1])
    weights = jnp.exp(masked - highest)
    own_weight = jnp.exp(own_score - highest)
    denominator = jnp.sum(weights, axis=2, keepdims=True) + own_weight[:, :, :1]
    probabilities = weights / denominator
    split = jnp.concatenate([part.astype(F32) for part in split3(probabilities)], axis=1)
    attended = parts_dot(split, values_ref[...], 1) + own_weight / denominator * fresh[...]
    own[...] = attended
    for h in range(heads):
        out_ref[:, h * size : (h + 1) * size] = own[:, h, :].astype(BF)


def attend(group_stream, w_query, w_key, w_value, cache_keys, cache_values, lengths):
    members, rows, cols = group_stream.shape
    window, size = cache_keys.shape[2:]
    pad = 8
    start = jnp.broadcast_to((window - lengths)[:, None, None], (rows, pad, window))
    return pl.pallas_call(
        attend_kernel,
        in_specs=[pl.BlockSpec(memory_space=pltpu.VMEM)] * 7,
        out_specs=pl.BlockSpec(memory_space=pltpu.VMEM),
        out_shape=jax.ShapeDtypeStruct((rows, w_query.shape[1]), BF),
        scratch_shapes=[
            pltpu.VMEM((rows, members * cols), BF),
            pltpu.VMEM((rows, 3 * pad, size), F32),
            pltpu.VMEM((rows, pad, size), F32),
            pltpu.VMEM((rows, pad, size), F32),
        ],
        compiler_params=pltpu.CompilerParams(vmem_limit_bytes=24 << 20),
        cost_estimate=pl.CostEstimate(
            flops=2 * rows * members * cols * (w_query.shape[1] + 2 * size),
            bytes_accessed=2 * members * cols * (w_query.shape[1] + 2 * size),
            transcendentals=rows * pad * window,
        ),
        name="attend",
    )(
        group_stream,
        w_query,
        w_key,
        w_value,
        cache_keys[:, 0],
        cache_values[:, 0],
        start.astype(jnp.int32),
    )


def split3(values):
    high = values.astype(BF)
    rest = values - high.astype(F32)
    middle = rest.astype(BF)
    return high, middle, (rest - middle.astype(F32)).astype(BF)


def routing_columns(expert_ids, combine, experts):
    named = expert_ids[:, :, None] == jnp.arange(experts, dtype=jnp.int32)
    chosen = jnp.any(named, axis=1)
    weight = jnp.sum(jnp.where(named, combine[:, :, None], 0.0), axis=1)
    rows = jnp.arange(expert_ids.shape[0])
    earlier = rows[None, :, None] < rows[:, None, None]
    rank = jnp.sum((earlier & chosen[None]).astype(jnp.int32), axis=1)
    rank = jnp.where(chosen, rank, CAP).astype(BF)
    return jnp.concatenate([rank, *split3(weight)], axis=1)


def per_device(
    tokens,
    expert_ids,
    combine,
    w_gate,
    w_up,
    w_down,
    w_query,
    w_key,
    w_value,
    cache_keys,
    cache_values,
    lengths,
):
    rows_n, width = tokens.shape
    x, y, c, z = (lax.axis_index(a) for a in ("x", "y", "c", "z"))
    chips = lax.axis_size("x") * lax.axis_size("y")
    experts = 2 * chips
    members = lax.axis_size("z")
    group = rows_n * members
    hidden = w_gate.shape[2]
    cols = width // members

    sent = jnp.concatenate([tokens, routing_columns(expert_ids, combine, experts)], axis=1)
    own = [w_gate[0].T, w_up[0].T]
    arrived, *other = lax.optimization_barrier(
        (copies(sent, "z"), *(shift(w, "c", 1) for w in own))
    )
    weights = own + other
    arrived = arrived.reshape(group, width + LANES)
    group_tokens, meta = arrived[:, :width], arrived[:, width:]
    widened = group_tokens.astype(F32)
    normed = (
        widened * lax.rsqrt(jnp.mean(widened * widened, axis=-1, keepdims=True) + EPSILON)
    ).astype(BF)
    dense = jnp.concatenate([normed, meta], axis=1)

    lane = jnp.arange(LANES, dtype=jnp.int32)[None, :]
    e_own = (x * 4 + y) * 2 + c
    e_other = (x * 4 + y) * 2 + 1 - c
    masks = jnp.concatenate([lane == e_own, lane == e_other] + [lane < 0] * 6, axis=0).astype(F32)
    masks = masks.astype(BF)
    half = group // 2

    def first_ring(block, axis):
        after, before, opposite = (shift(block, axis, step) for step in (1, -1, 2))
        return (
            jnp.concatenate([block, after], axis=0),
            jnp.concatenate([opposite, before], axis=0),
        )

    a_near, a_far = first_ring(dense[:half], "x")
    b_near, b_far = first_ring(dense[half:], "y")
    a_far, b_far, down = lax.optimization_barrier((a_far, b_far, w_down[0]))
    down_own = lax.all_to_all(down, "z", 1, 0, tiled=True).reshape(members, hidden, cols)
    sides = lambda part, axis: (shift(part, axis, 1), shift(part, axis, -1))
    a_near_sides, b_near_sides = sides(a_near, "y"), sides(b_near, "x")
    a_far_sides, b_far_sides = sides(a_far, "y"), sides(b_far, "x")
    near = (a_near, a_far, b_near, b_far, *a_near_sides, *b_near_sides)
    far = (*a_far_sides, *b_far_sides)
    slots = expert_slots(near, masks, weights)
    slots, *far = lax.optimization_barrier((slots, *far))
    opposite = (
        shift(a_near_sides[1], "y", -1),
        shift(far[0], "y", 1),
        shift(b_near_sides[1], "x", -1),
        shift(far[2], "x", 1),
    )
    near_active = lax.all_gather(slots, "z", axis=0)
    more, down_own = lax.optimization_barrier((expert_slots(far, masks, weights), down_own))
    down_other = shift(down_own, "c", 1)
    rest = jnp.concatenate([more, expert_slots(opposite, masks, weights)], axis=0)
    active = (near_active, ring(rest, "z"))
    place = jnp.stack([x, y, z]).astype(jnp.int32)
    result = lower(place, *active, down_own, down_other, chips)
    per_chip = result.shape[2]
    result = result.reshape(chips, 2 * per_chip, cols)
    returned = lax.all_to_all(result, ("x", "y"), 0, 0, tiled=True)

    rank = meta[:, :experts].astype(F32)
    weight = sum(meta[:, i * experts : (i + 1) * experts].astype(F32) for i in (1, 2, 3))
    by_core = lambda v: v.reshape(group, chips, 2)
    order = lambda v: jnp.where(c == 0, by_core(v), by_core(v)[:, :, ::-1])
    rank, weight = order(rank), order(weight)
    slot = jnp.arange(per_chip, dtype=jnp.int32)
    mine = (slot // CAP)[None, :] == (jnp.arange(group) // rows_n)[:, None]
    hit = mine[:, None, None, :] & (
        rank[..., None] == (slot % CAP).astype(F32)[None, None, None, :]
    )
    spread = jnp.where(hit, weight[..., None], 0.0).reshape(group, chips * 2 * per_chip)
    mixture = jnp.dot(
        spread,
        returned.reshape(chips * 2 * per_chip, cols).astype(F32),
        precision=lax.Precision.HIGHEST,
        preferred_element_type=F32,
    )
    block_tokens = lax.dynamic_slice(group_tokens, (jnp.int32(0), z * cols), (group, cols))
    stream_block = (block_tokens.astype(F32) + mixture).astype(BF)
    group_stream = copies(stream_block, "z")
    stream = lax.dynamic_slice(
        group_stream, (jnp.int32(0), z * rows_n, jnp.int32(0)), (members, rows_n, cols)
    )
    stream = stream.transpose(1, 0, 2).reshape(rows_n, width)
    guard = attend(group_stream, w_query, w_key, w_value, cache_keys, cache_values, lengths)
    return (stream, guard)


def solution(mesh):
    torus = Mesh(mesh.devices.reshape(4, 4, 2, mesh.devices.shape[1]), ("x", "y", "c", "z"))
    ep = ("x", "y", "c")
    every = (*ep, "z")
    return jax.shard_map(
        per_device,
        mesh=torus,
        in_specs=(
            P(every, None),
            P(every, None),
            P(every, None),
            P(ep, None, "z"),
            P(ep, None, "z"),
            P(ep, "z", None),
            P(None, "z"),
            P(None, "z"),
            P(None, "z"),
            P(ep, "z", None, None),
            P(ep, "z", None, None),
            P(ep),
        ),
        out_specs=(P(every, None), P(ep, "z")),
        check_vma=False,
    )
```

time: 221 us -> 207 us (0.937)
  waiting for transfers between devices: 75 us -> 56.8 us
  starting transfers between devices: 47.7 us -> 59.2 us
  matrix products: 9.26 us -> 0.49 us
  Pallas kernels: 21.3 us -> 28.2 us
  local copies, waits for them, and re-layouts: 19.4 us -> 13.6 us
    all_to_all x2 -> x1, waiting for transfers between devices: 31.6 us -> 13.3 us  [copies(): lax.all_to_all(jnp.broadcast_to(values[None], (size, *values.shape)), axi...]
    ppermute x23 -> x29, starting transfers between devices: 26.9 us -> 44.6 us  [shift(): lax.ppermute(values, axis, [(i, (i - step) % size) for i in range(size)])]
    ppermute x23 -> x29, waiting for transfers between devices: 22.9 us -> 33.8 us  [shift(): lax.ppermute(values, axis, [(i, (i - step) % size) for i in range(size)])]
    all_gather x1, waiting for transfers between devices: 10.4 us -> 0.02 us  [per_device(): near_active = lax.all_gather(slots, 'z', axis=0)]
    dot_general x6 -> x0, matrix products: 8.78 us -> none  [the longest x1 3.67 us: attend(): queries = jnp.dot(guard_norm, w_query, preferred_element_type=F32)]
    pallas_call x2 -> x4, Pallas kernels: 17.1 us -> 24.3 us  [the longest x3 20.3 us: expert_slots(): pl.pallas_call(functools.partial(expert_kernel, sizes, steps), grid=(step...]
    another operation x1 -> x0, local copies, waits for them, and re-layouts: 6.41 us -> none
    all_to_all x2 -> x1, starting transfers between devices: 9.7 us -> 3.93 us  [copies(): lax.all_to_all(jnp.broadcast_to(values[None], (size, *values.shape)), axi...]
  transfers between devices with their start and end apart: 28 -> 33, of which waited for: 10 -> 20; matrix products, arithmetic and copies ran while one was open for 6% -> 4% of each run, Pallas kernels for 8% -> 10%
where the time goes in v1:
time: 207 us; the launch traced here: 206 us
  starting transfers between devices  59.2 us (29%)
  waiting for transfers between devices  56.8 us (27%)
  Pallas kernels  28.2 us (14%)
  blocking collectives  26.4 us (13%)
  between operations  14.4 us (7%)
  local copies, waits for them, and re-layouts  13.6 us (7%)
  other arithmetic  6.56 us (3%)
    ppermute x29, starting transfers between devices, shift(): lax.ppermute(values, axis, [(i, (i - step) % size) for i in range(size)])  44.6 us
    ppermute x29, waiting for transfers between devices, shift(): lax.ppermute(values, axis, [(i, (i - step) % size) for i in range(size)])  33.8 us
    all_to_all x1, blocking collectives, copies(): lax.all_to_all(jnp.broadcast_to(values[None], (size, *values.shape)), axi...  26.4 us
    pallas_call x3, Pallas kernels, expert_slots(): pl.pallas_call(functools.partial(expert_kernel, sizes, steps), grid=(step...  20.3 us
    all_to_all x1, waiting for transfers between devices, copies(): lax.all_to_all(jnp.broadcast_to(values[None], (size, *values.shape)), axi...  13.3 us
    all_to_all x1, waiting for transfers between devices, per_device(): returned = lax.all_to_all(result, ('x', 'y'), 0, 0, tiled=True)  9.68 us
    unnamed x42, local copies, waits for them, and re-layouts  9.34 us
    all_to_all x1, starting transfers between devices, per_device(): returned = lax.all_to_all(result, ('x', 'y'), 0, 0, tiled=True)  7.01 us
  transfers between devices with their start and end apart: 33, of which 20 were waited for; matrix products, arithmetic and copies ran while one was open for 4% of the time, Pallas kernels for 10%

profile of v1, /device:TPU:8, one launch (start us, length us, event | category | flops | bytes accessed | tf_op | source)
XLA Modules:
  0.0 205.7 jit_solution(13198247937704973038)
XLA Ops:
  9.5 0.9 concatenate.27
  10.4 26.4 %all_to_all.31 = bf16[8,8,4224]{2,1,0:T(8,128)(2,1)S(1)} all-to-all(bf16[8,8,4224]{2,1,0:T(8,128)(2,1)S(1)} %broadcast_in_dim.37), channel_id=1, replica_groups=mesh['x'=4,'y'=4,'c'=2,'z'=8] {'z'}, dimensions={0} | all-to-all | bytes 1081344 | tf_op jit(solution)/shard_map/all_to_all | solution.py:39
  37.2 1.1 pad_maximum_fusion.4
  38.3 2.3 %collective-permute-start.5 = (bf16[32,4224]{1,0:T(8,128)(2,1)}, bf16[32,4224]{1,0:T(8,128)(2,1)S(1)}, u32[]{:S(2)}, u32[]{:S(2)}) collective-permute-start(bf16[32,4224]{1,0:T(8,128)(2,1)} %get-tuple-element.28), channel_id=1, source_target_pairs={{0,32},{16,48},{32,0},{48,16},{1,33},{17,49},{33,1},{49,17},{2,34}... | collective-permute-start | bytes 811016 | tf_op jit(solution)/shard_map/ppermute | solution.py:21
  40.6 3.0 %collective-permute-start.3 = (bf16[32,4224]{1,0:T(8,128)(2,1)S(1)}, bf16[32,4224]{1,0:T(8,128)(2,1)S(1)}, u32[]{:S(2)}, u32[]{:S(2)}) collective-permute-start(bf16[32,4224]{1,0:T(8,128)(2,1)S(1)} %get-tuple-element.29), channel_id=1, source_target_pairs={{0,128},{64,192},{128,0},{192,64},{1,129},{65,193},{129,1},{193,65... | collective-permute-start | bytes 811016 | tf_op jit(solution)/shard_map/ppermute | solution.py:21
  44.3 2.0 collective-permute-start.7
  46.3 1.7 collective-permute-done.5
  48.0 2.9 %collective-permute-start.2 = (bf16[32,4224]{1,0:T(8,128)(2,1)S(1)}, bf16[32,4224]{1,0:T(8,128)(2,1)}, u32[]{:S(2)}, u32[]{:S(2)}) collective-permute-start(bf16[32,4224]{1,0:T(8,128)(2,1)S(1)} %get-tuple-element.29), channel_id=1, source_target_pairs={{0,192},{64,0},{128,64},{192,128},{1,193},{65,1},{129,65},{193,129... | collective-permute-start | bytes 811016 | tf_op jit(solution)/shard_map/ppermute | solution.py:21
  50.9 2.3 %collective-permute-done.6 = bf16[32,4224]{1,0:T(8,128)(2,1)S(1)} collective-permute-done((bf16[32,4224]{1,0:T(8,128)(2,1)}, bf16[32,4224]{1,0:T(8,128)(2,1)S(1)}, u32[]{:S(2)}, u32[]{:S(2)}) %collective-permute-start.6) | collective-permute-done | bytes 270368 | tf_op jit(solution)/shard_map/ppermute | solution.py:21
  53.3 1.6 collective-permute-done.4
  54.9 1.3 copy.25
  56.2 3.6 %all-to-all-start.1 = ((bf16[192,8,512]{2,0,1:T(8,128)(2,1)}), bf16[192,8,512]{2,0,1:T(8,128)(2,1)S(1)}, u32[]{:S(2)}, u32[]{:S(2)}) async-start(bf16[192,8,512]{2,0,1:T(8,128)(2,1)} %bitcast.28), calls=%async_computation.1 | async-start | bytes 3145728 | tf_op jit(solution)/shard_map/all_to_all | solution.py:350
  59.9 1.1 pad_maximum_fusion.3.refs_2_.refs_10_
  61.0 1.6 collective-permute-start.11
  62.6 1.8 pad_maximum_fusion.refs_0_.refs_8_
  64.4 1.5 collective-permute-start.9
  65.9 1.7 collective-permute-start.10
  68.1 3.0 %collective-permute-start.12 = (bf16[64,4224]{1,0:T(8,128)(2,1)S(1)}, bf16[64,4224]{1,0:T(8,128)(2,1)}, u32[]{:S(2)}, u32[]{:S(2)}) collective-permute-start(bf16[64,4224]{1,0:T(8,128)(2,1)S(1)} %pad_maximum_fusion.1.refs_1_.refs_9_), channel_id=1, source_target_pairs={{0,48},{16,0},{32,16},{48,32},{1,49},{17,1},{33,17},{49,33},{2,50}... | collective-permute-start | bytes 1622024 | tf_op jit(solution)/shard_map/ppermute | solution.py:21
  71.1 4.6 %collective-permute-done.11.refs_7_.refs_15_ = bf16[64,4224]{1,0:T(8,128)(2,1)} collective-permute-done((bf16[64,4224]{1,0:T(8,128)(2,1)S(1)}, bf16[64,4224]{1,0:T(8,128)(2,1)}, u32[]{:S(2)}, u32[]{:S(2)}) %collective-permute-start.11) | collective-permute-done | bytes 540704 | tf_op jit(solution)/shard_map/ppermute | solution.py:21
  75.6 1.2 collective-permute-start.13
  76.9 4.7 %collective-permute-start.14 = (bf16[64,4224]{1,0:T(8,128)(2,1)S(1)}, bf16[64,4224]{1,0:T(8,128)(2,1)}, u32[]{:S(2)}, u32[]{:S(2)}) collective-permute-start(bf16[64,4224]{1,0:T(8,128)(2,1)S(1)} %pad_maximum_fusion.2.refs_3_.refs_11_), channel_id=1, source_target_pairs={{0,192},{64,0},{128,64},{192,128},{1,193},{65,1},{129,65},{193,129... | collective-permute-start | bytes 1622024 | tf_op jit(solution)/shard_map/ppermute | solution.py:21
  81.7 1.6 collective-permute-done.8.refs_4_.refs_12_
  83.3 8.5 %expert_slots.3 = bf16[192,384]{1,0:T(8,128)(2,1)} custom-call(bf16[8,128]{1,0:T(8,128)(2,1)S(1)} %convert_convert_fusion.mask_ref, bf16[64,4224]{1,0:T(8,128)(2,1)} %pad_maximum_fusion.refs_0_.refs_8_, bf16[64,4224]{1,0:T(8,128)(2,1)} %copy-done.17, bf16[64,4224]{1,0:T(8,128)(2,1)} %copy-done.18, bf16[64,4224]{1,0:T(8,128)(2,1)} %copy-done.16, ...), custom_call_target="tpu_custom_call" | custom-call | flops 3221225472 | bytes 10485760 | tf_op jit(solution)/shard_map/expert_slots/pallas_call | solution.py:105
  92.5 2.6 %collective-permute-start.18 = (bf16[64,4224]{1,0:T(8,128)(2,1)}, bf16[64,4224]{1,0:T(8,128)(2,1)}, u32[]{:S(2)}, u32[]{:S(2)}) collective-permute-start(bf16[64,4224]{1,0:T(8,128)(2,1)} %collective-permute-done.12.refs_0_.refs_4_), channel_id=1, source_target_pairs={{0,48},{16,0},{32,16},{48,32},{1,49},{17,1},{33,17},{49,33},{2,50}... | collective-permute-start | bytes 1622024 | tf_op jit(solution)/shard_map/ppermute | solution.py:21
  95.2 1.2 collective-permute-start.20
  97.2 5.9 %expert_slots.4 = bf16[96,384]{1,0:T(8,128)(2,1)S(1)} custom-call(bf16[8,128]{1,0:T(8,128)(2,1)S(1)} %convert_convert_fusion.mask_ref, bf16[64,4224]{1,0:T(8,128)(2,1)} %collective-permute-done.12.refs_0_.refs_4_, bf16[64,4224]{1,0:T(8,128)(2,1)} %collective-permute-done.13.refs_1_.refs_5_, bf16[64,4224]{1,0:T(8,128)(2,1)} %collective-permute-done.14.refs_2_.refs_6_, ...), custom_call_target="tpu_custom_call" | custom-call | flops 1610612736 | bytes 8388608 | tf_op jit(solution)/shard_map/expert_slots/pallas_call | solution.py:105
  104.8 2.4 %collective-permute-done.19.refs_2_.refs_6_ = bf16[64,4224]{1,0:T(8,128)(2,1)} collective-permute-done((bf16[64,4224]{1,0:T(8,128)(2,1)}, bf16[64,4224]{1,0:T(8,128)(2,1)}, u32[]{:S(2)}, u32[]{:S(2)}) %collective-permute-start.19) | collective-permute-done | bytes 540704 | tf_op jit(solution)/shard_map/ppermute | solution.py:21
  107.4 5.9 %expert_slots.5 = bf16[96,384]{1,0:T(8,128)(2,1)S(1)} custom-call(bf16[8,128]{1,0:T(8,128)(2,1)S(1)} %convert_convert_fusion.mask_ref, bf16[64,4224]{1,0:T(8,128)(2,1)} %collective-permute-done.17.refs_0_.refs_4_, bf16[64,4224]{1,0:T(8,128)(2,1)} %collective-permute-done.18.refs_1_.refs_5_, bf16[64,4224]{1,0:T(8,128)(2,1)} %collective-permute-done.19.refs_2_.refs_6_, ...), custom_call_target="tpu_custom_call" | custom-call | flops 1610612736 | bytes 8388608 | tf_op jit(solution)/shard_map/expert_slots/pallas_call | solution.py:105
  113.4 3.1 %collective-permute-start.21 = (bf16[192,384]{1,0:T(8,128)(2,1)S(1)}, bf16[192,384]{1,0:T(8,128)(2,1)S(1)}, u32[]{:S(2)}, u32[]{:S(2)}) collective-permute-start(bf16[192,384]{1,0:T(8,128)(2,1)S(1)} %pad_maximum_fusion.5.refs_0_), channel_id=1, source_target_pairs={{0,7},{1,0},{2,1},{3,2},{4,3},{5,4},{6,5},{7,6},{8,15},{9,8},{10,9... | collective-permute-start | bytes 442376 | tf_op jit(solution)/shard_map/ppermute | solution.py:21
  116.4 4.4 %collective-permute-done.21.refs_1_ = bf16[192,384]{1,0:T(8,128)(2,1)S(1)} collective-permute-done((bf16[192,384]{1,0:T(8,128)(2,1)S(1)}, bf16[192,384]{1,0:T(8,128)(2,1)S(1)}, u32[]{:S(2)}, u32[]{:S(2)}) %collective-permute-start.21) | collective-permute-done | bytes 147488 | tf_op jit(solution)/shard_map/ppermute | solution.py:21
  120.9 3.7 %collective-permute-start.22 = (bf16[192,384]{1,0:T(8,128)(2,1)S(1)}, bf16[192,384]{1,0:T(8,128)(2,1)}, u32[]{:S(2)}, u32[]{:S(2)}) collective-permute-start(bf16[192,384]{1,0:T(8,128)(2,1)S(1)} %collective-permute-done.21.refs_1_), channel_id=1, source_target_pairs={{0,7},{1,0},{2,1},{3,2},{4,3},{5,4},{6,5},{7,6},{8,15},{9,8},{10,9... | collective-permute-start | bytes 442376 | tf_op jit(solution)/shard_map/ppermute | solution.py:21
  125.3 2.9 %collective-permute-done.22.refs_2_ = bf16[192,384]{1,0:T(8,128)(2,1)} collective-permute-done((bf16[192,384]{1,0:T(8,128)(2,1)S(1)}, bf16[192,384]{1,0:T(8,128)(2,1)}, u32[]{:S(2)}, u32[]{:S(2)}) %collective-permute-start.22) | collective-permute-done | bytes 147488 | tf_op jit(solution)/shard_map/ppermute | solution.py:21
  128.2 3.5 %collective-permute-start.23 = (bf16[192,384]{1,0:T(8,128)(2,1)}, bf16[192,384]{1,0:T(8,128)(2,1)S(1)}, u32[]{:S(2)}, u32[]{:S(2)}) collective-permute-start(bf16[192,384]{1,0:T(8,128)(2,1)} %collective-permute-done.22.refs_2_), channel_id=1, source_target_pairs={{0,7},{1,0},{2,1},{3,2},{4,3},{5,4},{6,5},{7,6},{8,15},{9,8},{10,9... | collective-permute-start | bytes 442376 | tf_op jit(solution)/shard_map/ppermute | solution.py:21
  131.7 1.7 collective-permute-done.26.refs_6_
  133.4 2.0 collective-permute-done.23.refs_3_
  135.5 3.9 %collective-permute-start.24 = (bf16[96,384]{1,0:T(8,128)(2,1)S(1)}, bf16[96,384]{1,0:T(8,128)(2,1)S(1)}, u32[]{:S(2)}, u32[]{:S(2)}) collective-permute-start(bf16[96,384]{1,0:T(8,128)(2,1)S(1)} %slice.52), channel_id=1, source_target_pairs={{0,7},{1,0},{2,1},{3,2},{4,3},{5,4},{6,5},{7,6},{8,15},{9,8},{10,9... | collective-permute-start | bytes 221192 | tf_op jit(solution)/shard_map/ppermute | solution.py:21
  140.1 1.2 collective-permute-done.24
  141.3 4.2 %collective-permute-done.28 = bf16[96,384]{1,0:T(8,128)(2,1)S(1)} collective-permute-done((bf16[96,384]{1,0:T(8,128)(2,1)S(1)}, bf16[96,384]{1,0:T(8,128)(2,1)S(1)}, u32[]{:S(2)}, u32[]{:S(2)}) %collective-permute-start.28) | collective-permute-done | bytes 73760 | tf_op jit(solution)/shard_map/ppermute | solution.py:21
  145.7 1.3 copy-done.1
  149.7 3.9 %lower.1 = bf16[16,2,24,512]{3,2,1,0:T(8,128)(2,1)} custom-call(s32[3]{0:T(128)S(1)} %pad_add_fusion.place_ref, bf16[8,192,384]{2,1,0:T(8,128)(2,1)S(1)} %bitcast.37, bf16[8,192,512]{2,1,0:T(8,128)(2,1)S(1)} %bitcast.36, bf16[8,192,512]{2,1,0:T(8,128)(2,1)S(1)} %collective-permute-done.16.other_ref, bf16[192,384]{1,0:T(8,128)(2,1)S(1)} %pad_maximum_fusion.5.refs_0_, ...), custom_call_target="tpu_custom_call" | custom-call | flops 1207959552 | bytes 5505024 | tf_op jit(solution)/shard_map/lower/pallas_call | solution.py:168
  153.6 7.0 %all-to-all-start.2 = ((bf16[16,48,512]{2,1,0:T(8,128)(2,1)}), bf16[16,48,512]{2,1,0:T(8,128)(2,1)S(1)}, u32[]{:S(2)}, u32[]{:S(2)}) async-start(bf16[16,48,512]{2,1,0:T(8,128)(2,1)} %bitcast.16), calls=%async_computation.2 | async-start | bytes 1572864 | tf_op jit(solution)/shard_map/all_to_all | solution.py:373
  161.1 9.7 %all-to-all-done.2 = bf16[16,48,512]{2,1,0:T(8,128)(2,1)S(1)} async-done(((bf16[16,48,512]{2,1,0:T(8,128)(2,1)}), bf16[16,48,512]{2,1,0:T(8,128)(2,1)S(1)}, u32[]{:S(2)}, u32[]{:S(2)}) %all-to-all-start.2) | async-done | bytes 786464 | tf_op jit(solution)/shard_map/all_to_all | solution.py:373
  172.2 3.9 %all-to-all-start.3 = ((bf16[8,64,512]{2,1,0:T(8,128)(2,1)}), bf16[8,64,512]{2,1,0:T(8,128)(2,1)S(1)}, u32[]{:S(2)}, u32[]{:S(2)}) async-start(bf16[8,64,512]{2,1,0:T(8,128)(2,1)} %broadcast_in_dim.40), calls=%async_computation.3 | async-start | bytes 1048576 | tf_op jit(solution)/shard_map/all_to_all | solution.py:39
  176.1 13.3 %all-to-all-done.3.stream_ref = bf16[8,64,512]{2,1,0:T(8,128)(2,1)S(1)} async-done(((bf16[8,64,512]{2,1,0:T(8,128)(2,1)}), bf16[8,64,512]{2,1,0:T(8,128)(2,1)S(1)}, u32[]{:S(2)}, u32[]{:S(2)}) %all-to-all-start.3) | async-done | bytes 524320 | tf_op jit(solution)/shard_map/all_to_all | solution.py:39
  190.2 2.2 %copy-done = bf16[4096,512]{1,0:T(8,128)(2,1)S(1)} copy-done((bf16[4096,512]{1,0:T(8,128)(2,1)S(1)}, bf16[4096,512]{1,0:T(8,128)(2,1)}, u32[]{:S(2)}) %copy-start) | copy-done | bytes 4194328
  192.4 1.2 copy-done.4
  193.6 1.2 copy-done.5
  194.8 4.0 %attend.1 = bf16[64,512]{1,0:T(8,128)(2,1)} custom-call(bf16[8,64,512]{2,1,0:T(8,128)(2,1)S(1)} %all-to-all-done.3.stream_ref, bf16[4096,512]{1,0:T(8,128)(2,1)S(1)} %copy-done, bf16[4096,128]{1,0:T(8,128)(2,1)S(1)} %copy-done.2, bf16[4096,128]{1,0:T(8,128)(2,1)S(1)} %copy-done.3, bf16[64,64,128]{2,1,0:T(8,128)(2,1)S(1)} %bitcast.38, ...), custom_call_target="tpu_custom_call" | custom-call | flops 402653184 | bytes 6291456 | tf_op jit(solution)/shard_map/attend/pallas_call | solution.py:249
  (111 shorter events, 14.4 us)
Async XLA Ops:
  7.2 29.7 %collective-permute-start = (bf16[192,4096]{1,0:T(8,128)(2,1)}, bf16[192,4096]{1,0:T(8,128)(2,1)S(1)}, u32[]{:S(2)}, u32[]{:S(2)}) collective-permute-start(bf16[192,4096]{1,0:T(8,128)(2,1)} %bitcast.40), channel_id=1, source_target_pairs={{0,8},{8,0},{1,9},{9,1},{2,10},{10,2},{3,11},{11,3},{4,12},{12,4},... | collective-permute-start | bytes 4718600 | tf_op jit(solution)/shard_map/ppermute | solution.py:21
  7.3 29.6 %collective-permute-start.1 = (bf16[192,4096]{1,0:T(8,128)(2,1)}, bf16[192,4096]{1,0:T(8,128)(2,1)S(1)}, u32[]{:S(2)}, u32[]{:S(2)}) collective-permute-start(bf16[192,4096]{1,0:T(8,128)(2,1)} %bitcast.44), channel_id=1, source_target_pairs={{0,8},{8,0},{1,9},{9,1},{2,10},{10,2},{3,11},{11,3},{4,12},{12,4},... | collective-permute-start | bytes 4718600 | tf_op jit(solution)/shard_map/ppermute | solution.py:21
  36.8 1.5 copy-start.14
  36.8 1.5 copy-start.12
  36.8 19.4 %copy-start.13 = (bf16[192,4096]{1,0:T(8,128)(2,1)}, bf16[192,4096]{1,0:T(8,128)(2,1)S(1)}, u32[]{:S(2)}) copy-start(bf16[192,4096]{1,0:T(8,128)(2,1)S(1)} %collective-permute-done.1.refs_19_.refs_11_) | copy-start | bytes 4718596
  38.3 9.7 %collective-permute-start.5 = (bf16[32,4224]{1,0:T(8,128)(2,1)}, bf16[32,4224]{1,0:T(8,128)(2,1)S(1)}, u32[]{:S(2)}, u32[]{:S(2)}) collective-permute-start(bf16[32,4224]{1,0:T(8,128)(2,1)} %get-tuple-element.28), channel_id=1, source_target_pairs={{0,32},{16,48},{32,0},{48,16},{1,33},{17,49},{33,1},{49,17},{2,34}... | collective-permute-start | bytes 811016 | tf_op jit(solution)/shard_map/ppermute | solution.py:21
  40.6 12.6 %collective-permute-start.6 = (bf16[32,4224]{1,0:T(8,128)(2,1)}, bf16[32,4224]{1,0:T(8,128)(2,1)S(1)}, u32[]{:S(2)}, u32[]{:S(2)}) collective-permute-start(bf16[32,4224]{1,0:T(8,128)(2,1)} %get-tuple-element.28), channel_id=1, source_target_pairs={{0,16},{16,32},{32,48},{48,0},{1,17},{17,33},{33,49},{49,1},{2,18}... | collective-permute-start | bytes 811016 | tf_op jit(solution)/shard_map/ppermute | solution.py:21
  40.6 14.3 %copy-start.19 = (bf16[1,192,4096]{2,1,0:T(8,128)(2,1)S(1)}, bf16[1,192,4096]{2,1,0:T(8,128)(2,1)}, u32[]{:S(2)}) copy-start(bf16[1,192,4096]{2,1,0:T(8,128)(2,1)} %param.17) | copy-start | bytes 4718596
  40.6 12.6 %collective-permute-start.3 = (bf16[32,4224]{1,0:T(8,128)(2,1)S(1)}, bf16[32,4224]{1,0:T(8,128)(2,1)S(1)}, u32[]{:S(2)}, u32[]{:S(2)}) collective-permute-start(bf16[32,4224]{1,0:T(8,128)(2,1)S(1)} %get-tuple-element.29), channel_id=1, source_target_pairs={{0,128},{64,192},{128,0},{192,64},{1,129},{65,193},{129,1},{193,65... | collective-permute-start | bytes 811016 | tf_op jit(solution)/shard_map/ppermute | solution.py:21
  43.7 11.2 %collective-permute-start.4 = (bf16[32,4224]{1,0:T(8,128)(2,1)S(1)}, bf16[32,4224]{1,0:T(8,128)(2,1)S(1)}, u32[]{:S(2)}, u32[]{:S(2)}) collective-permute-start(bf16[32,4224]{1,0:T(8,128)(2,1)S(1)} %get-tuple-element.29), channel_id=1, source_target_pairs={{0,64},{64,128},{128,192},{192,0},{1,65},{65,129},{129,193},{193,1... | collective-permute-start | bytes 811016 | tf_op jit(solution)/shard_map/ppermute | solution.py:21
  44.3 15.6 %collective-permute-start.7 = (bf16[32,4224]{1,0:T(8,128)(2,1)}, bf16[32,4224]{1,0:T(8,128)(2,1)}, u32[]{:S(2)}, u32[]{:S(2)}) collective-permute-start(bf16[32,4224]{1,0:T(8,128)(2,1)} %get-tuple-element.28), channel_id=1, source_target_pairs={{0,48},{16,0},{32,16},{48,32},{1,49},{17,1},{33,17},{49,33},{2,50}... | collective-permute-start | bytes 811016 | tf_op jit(solution)/shard_map/ppermute | solution.py:21
  48.0 14.6 %collective-permute-start.2 = (bf16[32,4224]{1,0:T(8,128)(2,1)S(1)}, bf16[32,4224]{1,0:T(8,128)(2,1)}, u32[]{:S(2)}, u32[]{:S(2)}) collective-permute-start(bf16[32,4224]{1,0:T(8,128)(2,1)S(1)} %get-tuple-element.29), channel_id=1, source_target_pairs={{0,192},{64,0},{128,64},{192,128},{1,193},{65,1},{129,65},{193,129... | collective-permute-start | bytes 811016 | tf_op jit(solution)/shard_map/ppermute | solution.py:21
  53.2 28.4 %copy-start.16 = (bf16[64,4224]{1,0:T(8,128)(2,1)}, bf16[64,4224]{1,0:T(8,128)(2,1)S(1)}, u32[]{:S(2)}) copy-start(bf16[64,4224]{1,0:T(8,128)(2,1)S(1)} %pad_maximum_fusion.2.refs_3_.refs_11_) | copy-start | bytes 1622020
  54.9 20.8 %copy-start.17 = (bf16[64,4224]{1,0:T(8,128)(2,1)}, bf16[64,4224]{1,0:T(8,128)(2,1)S(1)}, u32[]{:S(2)}) copy-start(bf16[64,4224]{1,0:T(8,128)(2,1)S(1)} %pad_maximum_fusion.1.refs_1_.refs_9_) | copy-start | bytes 1622020
  56.2 46.9 %all-to-all-start.1 = ((bf16[192,8,512]{2,0,1:T(8,128)(2,1)}), bf16[192,8,512]{2,0,1:T(8,128)(2,1)S(1)}, u32[]{:S(2)}, u32[]{:S(2)}) async-start(bf16[192,8,512]{2,0,1:T(8,128)(2,1)} %bitcast.28), calls=%async_computation.1 | async-start | bytes 3145728 | tf_op jit(solution)/shard_map/all_to_all | solution.py:350
  59.8 85.8 %all-gather.3.cloned.1.call-start = ((), (), s32[]{:S(2)}) async-start(), calls=%async_computation.4 | async-start | bytes 1327104 | tf_op jit(solution)/shard_map/all_gather | solution.py:364
  61.0 20.7 %copy-start.18 = (bf16[64,4224]{1,0:T(8,128)(2,1)}, bf16[64,4224]{1,0:T(8,128)(2,1)S(1)}, u32[]{:S(2)}) copy-start(bf16[64,4224]{1,0:T(8,128)(2,1)S(1)} %pad_maximum_fusion.3.refs_2_.refs_10_) | copy-start | bytes 1622020
  61.0 14.7 %collective-permute-start.11 = (bf16[64,4224]{1,0:T(8,128)(2,1)S(1)}, bf16[64,4224]{1,0:T(8,128)(2,1)}, u32[]{:S(2)}, u32[]{:S(2)}) collective-permute-start(bf16[64,4224]{1,0:T(8,128)(2,1)S(1)} %pad_maximum_fusion.3.refs_2_.refs_10_), channel_id=1, source_target_pairs={{0,64},{64,128},{128,192},{192,0},{1,65},{65,129},{129,193},{193,1... | collective-permute-start | bytes 1622024 | tf_op jit(solution)/shard_map/ppermute | solution.py:21
  64.4 12.5 %collective-permute-start.9 = (bf16[64,4224]{1,0:T(8,128)(2,1)}, bf16[64,4224]{1,0:T(8,128)(2,1)}, u32[]{:S(2)}, u32[]{:S(2)}) collective-permute-start(bf16[64,4224]{1,0:T(8,128)(2,1)} %pad_maximum_fusion.refs_0_.refs_8_), channel_id=1, source_target_pairs={{0,16},{16,32},{32,48},{48,0},{1,17},{17,33},{33,49},{49,1},{2,18}... | collective-permute-start | bytes 1622024 | tf_op jit(solution)/shard_map/ppermute | solution.py:21
  65.9 15.7 %collective-permute-start.10 = (bf16[64,4224]{1,0:T(8,128)(2,1)S(1)}, bf16[64,4224]{1,0:T(8,128)(2,1)}, u32[]{:S(2)}, u32[]{:S(2)}) collective-permute-start(bf16[64,4224]{1,0:T(8,128)(2,1)S(1)} %pad_maximum_fusion.3.refs_2_.refs_10_), channel_id=1, source_target_pairs={{0,192},{64,0},{128,64},{192,128},{1,193},{65,1},{129,65},{193,129... | collective-permute-start | bytes 1622024 | tf_op jit(solution)/shard_map/ppermute | solution.py:21
  67.6 15.7 %collective-permute-start.8 = (bf16[64,4224]{1,0:T(8,128)(2,1)}, bf16[64,4224]{1,0:T(8,128)(2,1)}, u32[]{:S(2)}, u32[]{:S(2)}) collective-permute-start(bf16[64,4224]{1,0:T(8,128)(2,1)} %pad_maximum_fusion.refs_0_.refs_8_), channel_id=1, source_target_pairs={{0,48},{16,0},{32,16},{48,32},{1,49},{17,1},{33,17},{49,33},{2,50}... | collective-permute-start | bytes 1622024 | tf_op jit(solution)/shard_map/ppermute | solution.py:21
  68.1 24.0 %collective-permute-start.12 = (bf16[64,4224]{1,0:T(8,128)(2,1)S(1)}, bf16[64,4224]{1,0:T(8,128)(2,1)}, u32[]{:S(2)}, u32[]{:S(2)}) collective-permute-start(bf16[64,4224]{1,0:T(8,128)(2,1)S(1)} %pad_maximum_fusion.1.refs_1_.refs_9_), channel_id=1, source_target_pairs={{0,48},{16,0},{32,16},{48,32},{1,49},{17,1},{33,17},{49,33},{2,50}... | collective-permute-start | bytes 1622024 | tf_op jit(solution)/shard_map/ppermute | solution.py:21
  75.6 16.5 %collective-permute-start.13 = (bf16[64,4224]{1,0:T(8,128)(2,1)S(1)}, bf16[64,4224]{1,0:T(8,128)(2,1)}, u32[]{:S(2)}, u32[]{:S(2)}) collective-permute-start(bf16[64,4224]{1,0:T(8,128)(2,1)S(1)} %pad_maximum_fusion.1.refs_1_.refs_9_), channel_id=1, source_target_pairs={{0,16},{16,32},{32,48},{48,0},{1,17},{17,33},{33,49},{49,1},{2,18}... | collective-permute-start | bytes 1622024 | tf_op jit(solution)/shard_map/ppermute | solution.py:21
  76.9 15.2 %collective-permute-start.14 = (bf16[64,4224]{1,0:T(8,128)(2,1)S(1)}, bf16[64,4224]{1,0:T(8,128)(2,1)}, u32[]{:S(2)}, u32[]{:S(2)}) collective-permute-start(bf16[64,4224]{1,0:T(8,128)(2,1)S(1)} %pad_maximum_fusion.2.refs_3_.refs_11_), channel_id=1, source_target_pairs={{0,192},{64,0},{128,64},{192,128},{1,193},{65,1},{129,65},{193,129... | collective-permute-start | bytes 1622024 | tf_op jit(solution)/shard_map/ppermute | solution.py:21
  81.6 10.9 %collective-permute-start.15 = (bf16[64,4224]{1,0:T(8,128)(2,1)S(1)}, bf16[64,4224]{1,0:T(8,128)(2,1)}, u32[]{:S(2)}, u32[]{:S(2)}) collective-permute-start(bf16[64,4224]{1,0:T(8,128)(2,1)S(1)} %pad_maximum_fusion.2.refs_3_.refs_11_), channel_id=1, source_target_pairs={{0,64},{64,128},{128,192},{192,0},{1,65},{65,129},{129,193},{193,1... | collective-permute-start | bytes 1622024 | tf_op jit(solution)/shard_map/ppermute | solution.py:21
  92.5 11.5 %collective-permute-start.18 = (bf16[64,4224]{1,0:T(8,128)(2,1)}, bf16[64,4224]{1,0:T(8,128)(2,1)}, u32[]{:S(2)}, u32[]{:S(2)}) collective-permute-start(bf16[64,4224]{1,0:T(8,128)(2,1)} %collective-permute-done.12.refs_0_.refs_4_), channel_id=1, source_target_pairs={{0,48},{16,0},{32,16},{48,32},{1,49},{17,1},{33,17},{49,33},{2,50}... | collective-permute-start | bytes 1622024 | tf_op jit(solution)/shard_map/ppermute | solution.py:21
  95.2 9.7 %collective-permute-start.20 = (bf16[64,4224]{1,0:T(8,128)(2,1)}, bf16[64,4224]{1,0:T(8,128)(2,1)}, u32[]{:S(2)}, u32[]{:S(2)}) collective-permute-start(bf16[64,4224]{1,0:T(8,128)(2,1)} %collective-permute-done.14.refs_2_.refs_6_), channel_id=1, source_target_pairs={{0,192},{64,0},{128,64},{192,128},{1,193},{65,1},{129,65},{193,129... | collective-permute-start | bytes 1622024 | tf_op jit(solution)/shard_map/ppermute | solution.py:21
  96.4 10.9 %collective-permute-start.19 = (bf16[64,4224]{1,0:T(8,128)(2,1)}, bf16[64,4224]{1,0:T(8,128)(2,1)}, u32[]{:S(2)}, u32[]{:S(2)}) collective-permute-start(bf16[64,4224]{1,0:T(8,128)(2,1)} %collective-permute-done.11.refs_7_.refs_15_), channel_id=1, source_target_pairs={{0,64},{64,128},{128,192},{192,0},{1,65},{65,129},{129,193},{193,1... | collective-permute-start | bytes 1622024 | tf_op jit(solution)/shard_map/ppermute | solution.py:21
  97.2 10.3 %collective-permute-start.17 = (bf16[64,4224]{1,0:T(8,128)(2,1)}, bf16[64,4224]{1,0:T(8,128)(2,1)}, u32[]{:S(2)}, u32[]{:S(2)}) collective-permute-start(bf16[64,4224]{1,0:T(8,128)(2,1)} %collective-permute-done.9.refs_5_.refs_13_), channel_id=1, source_target_pairs={{0,16},{16,32},{32,48},{48,0},{1,17},{17,33},{33,49},{49,1},{2,18}... | collective-permute-start | bytes 1622024 | tf_op jit(solution)/shard_map/ppermute | solution.py:21
  103.1 42.5 %collective-permute-start.16 = (bf16[8,192,512]{2,1,0:T(8,128)(2,1)S(1)}, bf16[8,192,512]{2,1,0:T(8,128)(2,1)S(1)}, u32[]{:S(2)}, u32[]{:S(2)}) collective-permute-start(bf16[8,192,512]{2,1,0:T(8,128)(2,1)S(1)} %bitcast.35), channel_id=1, source_target_pairs={{0,8},{8,0},{1,9},{9,1},{2,10},{10,2},{3,11},{11,3},{4,12},{12,4},... | collective-permute-start | bytes 4718600 | tf_op jit(solution)/shard_map/ppermute | solution.py:21
  113.4 7.5 %collective-permute-start.21 = (bf16[192,384]{1,0:T(8,128)(2,1)S(1)}, bf16[192,384]{1,0:T(8,128)(2,1)S(1)}, u32[]{:S(2)}, u32[]{:S(2)}) collective-permute-start(bf16[192,384]{1,0:T(8,128)(2,1)S(1)} %pad_maximum_fusion.5.refs_0_), channel_id=1, source_target_pairs={{0,7},{1,0},{2,1},{3,2},{4,3},{5,4},{6,5},{7,6},{8,15},{9,8},{10,9... | collective-permute-start | bytes 442376 | tf_op jit(solution)/shard_map/ppermute | solution.py:21
  116.4 8.8 %collective-permute-start.25 = (bf16[192,384]{1,0:T(8,128)(2,1)S(1)}, bf16[192,384]{1,0:T(8,128)(2,1)}, u32[]{:S(2)}, u32[]{:S(2)}) collective-permute-start(bf16[192,384]{1,0:T(8,128)(2,1)S(1)} %pad_maximum_fusion.5.refs_0_), channel_id=1, source_target_pairs={{0,1},{1,2},{2,3},{3,4},{4,5},{5,6},{6,7},{7,0},{8,9},{9,10},{10,1... | collective-permute-start | bytes 442376 | tf_op jit(solution)/shard_map/ppermute | solution.py:21
  120.9 7.3 %collective-permute-start.22 = (bf16[192,384]{1,0:T(8,128)(2,1)S(1)}, bf16[192,384]{1,0:T(8,128)(2,1)}, u32[]{:S(2)}, u32[]{:S(2)}) collective-permute-start(bf16[192,384]{1,0:T(8,128)(2,1)S(1)} %collective-permute-done.21.refs_1_), channel_id=1, source_target_pairs={{0,7},{1,0},{2,1},{3,2},{4,3},{5,4},{6,5},{7,6},{8,15},{9,8},{10,9... | collective-permute-start | bytes 442376 | tf_op jit(solution)/shard_map/ppermute | solution.py:21
  125.2 8.1 %collective-permute-start.26 = (bf16[192,384]{1,0:T(8,128)(2,1)}, bf16[192,384]{1,0:T(8,128)(2,1)}, u32[]{:S(2)}, u32[]{:S(2)}) collective-permute-start(bf16[192,384]{1,0:T(8,128)(2,1)} %collective-permute-done.25.refs_7_), channel_id=1, source_target_pairs={{0,1},{1,2},{2,3},{3,4},{4,5},{5,6},{6,7},{7,0},{8,9},{9,10},{10,1... | collective-permute-start | bytes 442376 | tf_op jit(solution)/shard_map/ppermute | solution.py:21
  128.2 7.2 %collective-permute-start.23 = (bf16[192,384]{1,0:T(8,128)(2,1)}, bf16[192,384]{1,0:T(8,128)(2,1)S(1)}, u32[]{:S(2)}, u32[]{:S(2)}) collective-permute-start(bf16[192,384]{1,0:T(8,128)(2,1)} %collective-permute-done.22.refs_2_), channel_id=1, source_target_pairs={{0,7},{1,0},{2,1},{3,2},{4,3},{5,4},{6,5},{7,6},{8,15},{9,8},{10,9... | collective-permute-start | bytes 442376 | tf_op jit(solution)/shard_map/ppermute | solution.py:21
  133.4 6.6 %collective-permute-start.27 = (bf16[192,384]{1,0:T(8,128)(2,1)}, bf16[192,384]{1,0:T(8,128)(2,1)S(1)}, u32[]{:S(2)}, u32[]{:S(2)}) collective-permute-start(bf16[192,384]{1,0:T(8,128)(2,1)} %collective-permute-done.26.refs_6_), channel_id=1, source_target_pairs={{0,1},{1,2},{2,3},{3,4},{4,5},{5,6},{6,7},{7,0},{8,9},{9,10},{10,1... | collective-permute-start | bytes 442376 | tf_op jit(solution)/shard_map/ppermute | solution.py:21
  135.5 5.9 %copy-start.6 = (bf16[192,384]{1,0:T(8,128)(2,1)}, bf16[192,384]{1,0:T(8,128)(2,1)S(1)}, u32[]{:S(2)}) copy-start(bf16[192,384]{1,0:T(8,128)(2,1)S(1)} %collective-permute-done.23.refs_3_) | copy-start | bytes 442372
  135.5 5.9 %collective-permute-start.24 = (bf16[96,384]{1,0:T(8,128)(2,1)S(1)}, bf16[96,384]{1,0:T(8,128)(2,1)S(1)}, u32[]{:S(2)}, u32[]{:S(2)}) collective-permute-start(bf16[96,384]{1,0:T(8,128)(2,1)S(1)} %slice.52), channel_id=1, source_target_pairs={{0,7},{1,0},{2,1},{3,2},{4,3},{5,4},{6,5},{7,6},{8,15},{9,8},{10,9... | collective-permute-start | bytes 221192 | tf_op jit(solution)/shard_map/ppermute | solution.py:21
  139.9 5.7 %copy-start.8 = (bf16[192,384]{1,0:T(8,128)(2,1)}, bf16[192,384]{1,0:T(8,128)(2,1)S(1)}, u32[]{:S(2)}) copy-start(bf16[192,384]{1,0:T(8,128)(2,1)S(1)} %collective-permute-done.27.refs_5_) | copy-start | bytes 442372
  139.9 5.6 %collective-permute-start.28 = (bf16[96,384]{1,0:T(8,128)(2,1)S(1)}, bf16[96,384]{1,0:T(8,128)(2,1)S(1)}, u32[]{:S(2)}, u32[]{:S(2)}) collective-permute-start(bf16[96,384]{1,0:T(8,128)(2,1)S(1)} %slice.53), channel_id=1, source_target_pairs={{0,1},{1,2},{2,3},{3,4},{4,5},{5,6},{6,7},{7,0},{8,9},{9,10},{10,1... | collective-permute-start | bytes 221192 | tf_op jit(solution)/shard_map/ppermute | solution.py:21
  145.6 1.3 copy-start.1
  153.6 7.0 %copy-start.15 = (bf16[8,8,4224]{2,1,0:T(8,128)(2,1)S(1)}, bf16[8,8,4224]{2,1,0:T(8,128)(2,1)}, u32[]{:S(2)}) copy-start(bf16[8,8,4224]{2,1,0:T(8,128)(2,1)} %copy-done.14) | copy-start | bytes 1622020
  153.6 17.2 %all-to-all-start.2 = ((bf16[16,48,512]{2,1,0:T(8,128)(2,1)}), bf16[16,48,512]{2,1,0:T(8,128)(2,1)S(1)}, u32[]{:S(2)}, u32[]{:S(2)}) async-start(bf16[16,48,512]{2,1,0:T(8,128)(2,1)} %bitcast.16), calls=%async_computation.2 | async-start | bytes 1572864 | tf_op jit(solution)/shard_map/all_to_all | solution.py:373
  170.8 19.3 %copy-start.3 = (bf16[4096,128]{1,0:T(8,128)(2,1)S(1)}, bf16[4096,128]{1,0:T(8,128)(2,1)}, u32[]{:S(2)}) copy-start(bf16[4096,128]{1,0:T(8,128)(2,1)} %wv_ref.1) | copy-start | bytes 3145732
  171.3 4.8 %copy-start.20 = (s32[64]{0:T(128)S(1)}, s32[64]{0:T(128)}, u32[]{:S(2)}) copy-start(s32[64]{0:T(128)} %param.23) | copy-start | bytes 772
  171.3 18.9 %copy-start.2 = (bf16[4096,128]{1,0:T(8,128)(2,1)S(1)}, bf16[4096,128]{1,0:T(8,128)(2,1)}, u32[]{:S(2)}) copy-start(bf16[4096,128]{1,0:T(8,128)(2,1)} %wk_ref.1) | copy-start | bytes 3145732
  172.2 17.2 %all-to-all-start.3 = ((bf16[8,64,512]{2,1,0:T(8,128)(2,1)}), bf16[8,64,512]{2,1,0:T(8,128)(2,1)S(1)}, u32[]{:S(2)}, u32[]{:S(2)}) async-start(bf16[8,64,512]{2,1,0:T(8,128)(2,1)} %broadcast_in_dim.40), calls=%async_computation.3 | async-start | bytes 1048576 | tf_op jit(solution)/shard_map/all_to_all | solution.py:39
  190.2 2.2 %copy-start = (bf16[4096,512]{1,0:T(8,128)(2,1)S(1)}, bf16[4096,512]{1,0:T(8,128)(2,1)}, u32[]{:S(2)}) copy-start(bf16[4096,512]{1,0:T(8,128)(2,1)} %wq_ref.1) | copy-start | bytes 12582916
  (6 other events, 5.8 us)
Sparse Core Ops, SparseCore 0:
  92.7 39.5 all-gather.2

commit v2 on v1

--- a/solution.py
+++ b/solution.py
@@ -39,6 +39,10 @@
     return lax.all_to_all(
         jnp.broadcast_to(values[None], (size, *values.shape)), axis, 0, 0, tiled=True
     )
+
+
+def in_hbm(arrays):
+    return [pltpu.with_memory_space_constraint(a, pltpu.HBM) for a in arrays]
 
 
 def expert_kernel(sizes, steps, mask_ref, *refs):
@@ -98,7 +102,6 @@
     in_specs += [pl.BlockSpec((m, chunk), lambda k: (0, k)) for m in sizes]
     in_specs += [pl.BlockSpec((m, LANES), lambda k: (0, depth // LANES)) for m in sizes]
     in_specs += [pl.BlockSpec((hidden, chunk), lambda k: (0, k))] * 4
-    in_hbm = lambda arrays: [pltpu.with_memory_space_constraint(a, pltpu.HBM) for a in arrays]
     pieces, weights = in_hbm(pieces), in_hbm(weights)
     total = sum(sizes)
     slots = total // 8 * CAP
@@ -132,30 +135,48 @@
 
 def lower_kernel(place_ref, near_ref, own_ref, other_ref, *refs):
     members, hidden, _ = own_ref.shape
-    rest_refs, (out_ref, *sums, placed) = refs[:members], refs[members:]
+    rest_refs, refs = refs[:members], refs[members:]
+    out_ref, first_sum, second_sum, placed, near_held, own_held, other_held, sems = refs
+    sums = (first_sum, second_sum)
     first = near_ref.shape[1]
     z = place_ref[2]
-    for j, w_ref in enumerate((own_ref, other_ref)):
+
+    def copy(i, d):
+        source, target = ((near_ref, near_held), (own_ref, own_held), (other_ref, other_held))[i]
+        return pltpu.make_async_copy(source.at[d], target.at[d], sems.at[i, d])
+
+    for d in range(members):
+        for i in range(3):
+            copy(i, d).start()
+    for d in range(members):
+        for i in range(3):
+            copy(i, d).wait()
+        for j, held in enumerate((own_held, other_held)):
+            span = slice(j * hidden, (j + 1) * hidden)
+            part = jnp.dot(near_held[d][:, span], held[d], preferred_element_type=F32)
+            if d == 0:
+                sums[j][:first, :] = part
+            else:
+                sums[j][:first, :] += part
+    for j, held in enumerate((own_held, other_held)):
         span = slice(j * hidden, (j + 1) * hidden)
         for d in range(members):
             at = (z + d) % members
-            near = jnp.dot(near_ref[d][:, span], w_ref[d], preferred_element_type=F32)
-            rest = jnp.dot(rest_refs[d][:, span], w_ref[at], preferred_element_type=F32)
+            part = jnp.dot(rest_refs[d][:, span], held[at], preferred_element_type=F32)
             if d == 0:
-                sums[j][:first, :] = near
-                sums[j][first:, :] = rest
+                sums[j][first:, :] = part
             else:
-                sums[j][:first, :] += near
-                sums[j][first:, :] += rest
+                sums[j][first:, :] += part
     x, y = place_ref[0], place_ref[1]
     per = placed.shape[2] // 2
     for p, (h, outer, inner) in enumerate(PIECES):
         for i in range(2):
             at = (2 * p + i) * per
+            step = (0, 1, 3, 2)[inner + i]
             if h == 0:
-                chip = (x + inner + i) % 4 * 4 + (y + outer) % 4
+                chip = (x ^ step) * 4 + (y + outer) % 4
             else:
-                chip = (x + outer) % 4 * 4 + (y + inner + i) % 4
+                chip = (x + outer) % 4 * 4 + (y ^ step)
             for j in range(2):
                 placed[chip, j, h * per : (h + 1) * per, :] = sums[j][at : at + per, :]
     out_ref[...] = placed[...].astype(BF)
@@ -163,20 +184,26 @@
 
 def lower(place, near, rest, down_own, down_other, chips):
     members, hidden, cols = down_own.shape
+    near, down_own, down_other = in_hbm((near, down_own, down_other))
     slots = near.shape[1] + rest[0].shape[0]
     per_chip = slots // chips
     return pl.pallas_call(
         lower_kernel,
         in_specs=[pl.BlockSpec(memory_space=pltpu.SMEM)]
-        + [pl.BlockSpec(memory_space=pltpu.VMEM)] * (3 + members),
+        + [pl.BlockSpec(memory_space=pl.ANY)] * 3
+        + [pl.BlockSpec(memory_space=pltpu.VMEM)] * members,
         out_specs=pl.BlockSpec(memory_space=pltpu.VMEM),
         out_shape=jax.ShapeDtypeStruct((chips, 2, per_chip, cols), BF),
         scratch_shapes=[
             pltpu.VMEM((slots, cols), F32),
             pltpu.VMEM((slots, cols), F32),
             pltpu.VMEM((chips, 2, per_chip, cols), F32),
+            pltpu.VMEM(near.shape, BF),
+            pltpu.VMEM(down_own.shape, BF),
+            pltpu.VMEM(down_other.shape, BF),
+            pltpu.SemaphoreType.DMA((3, members)),
         ],
-        compiler_params=pltpu.CompilerParams(vmem_limit_bytes=16 << 20),
+        compiler_params=pltpu.CompilerParams(vmem_limit_bytes=24 << 20),
         cost_estimate=pl.CostEstimate(
             flops=4 * members * slots * hidden * cols,
             bytes_accessed=4 * members * hidden * (slots + cols),
@@ -187,22 +214,43 @@
 
 
 def attend_kernel(
-    stream_ref, wq_ref, wk_ref, wv_ref, keys_ref, values_ref, start_ref, out_ref, normed, spread, own, fresh
+    place_ref, stream_ref, wq_ref, wk_ref, wv_ref, keys_ref, values_ref, start_ref, mine_ref, out_ref, *scratch
 ):
+    normed, spread, own, fresh, wide, *held, sems, query_sems = scratch
+    sources = (wk_ref, wv_ref, keys_ref, values_ref)
+    moves = [pltpu.make_async_copy(s, t, sems.at[i]) for i, (s, t) in enumerate(zip(sources, held[1:]))]
+    members, rows, cols = stream_ref.shape
+    parts = [pl.ds(i * cols, cols) for i in range(members)]
+    query_moves = [
+        pltpu.make_async_copy(wq_ref.at[p], held[0].at[p], query_sems.at[i]) for i, p in enumerate(parts)
+    ]
+    for move in (*query_moves, *moves):
+        move.start()
     members, rows, cols = stream_ref.shape
     heads, size = out_ref.shape[1] // keys_ref.shape[2], keys_ref.shape[2]
     width = members * cols
     total = jnp.zeros((rows, 1), F32)
     for i in range(members):
         block = stream_ref[i].astype(F32)
+        wide[...] = block
+        few = mine_ref.shape[0]
+        mine = wide[pl.ds(pl.multiple_of(place_ref[2] * few, few), few), :]
+        mine_ref[:, i * cols : (i + 1) * cols] = mine.astype(BF)
         total += jnp.sum(block * block, axis=1, keepdims=True)
     scale = lax.rsqrt(total / width + EPSILON)
     for i in range(members):
         normed[:, i * cols : (i + 1) * cols] = (stream_ref[i].astype(F32) * scale).astype(BF)
-    project = lambda w_ref: jnp.dot(normed[...], w_ref[...], preferred_element_type=F32)
-    queries = project(wq_ref)
-    key_new = project(wk_ref).astype(BF).astype(F32)
-    value_new = project(wv_ref).astype(BF).astype(F32)
+    queries = jnp.zeros((rows, out_ref.shape[1]), F32)
+    for move, p in zip(query_moves, parts):
+        move.wait()
+        queries += jnp.dot(normed[:, p], held[0][p, :], preferred_element_type=F32)
+
+    def project(i):
+        moves[i].wait()
+        return jnp.dot(normed[...], held[1 + i][...], preferred_element_type=F32)
+
+    key_new = project(0).astype(BF).astype(F32)
+    value_new = project(1).astype(BF).astype(F32)
     pad = spread.shape[1] // 3
     factor = 1.0 / math.sqrt(size)
     for h in range(heads):
@@ -224,7 +272,8 @@
         )
         return result[:, :pad] + result[:, pad : 2 * pad] + result[:, 2 * pad :]
 
-    scores = parts_dot(spread[...], keys_ref[...], 2) * factor
+    moves[2].wait()
+    scores = parts_dot(spread[...], held[3][...], 2) * factor
     window = scores.shape[2]
     allowed = lax.broadcasted_iota(jnp.int32, scores.shape, 2) >= start_ref[...]
     masked = jnp.where(allowed, scores, -jnp.inf)
@@ -235,27 +284,38 @@
     denominator = jnp.sum(weights, axis=2, keepdims=True) + own_weight[:, :, :1]
     probabilities = weights / denominator
     split = jnp.concatenate([part.astype(F32) for part in split3(probabilities)], axis=1)
-    attended = parts_dot(split, values_ref[...], 1) + own_weight / denominator * fresh[...]
+    moves[3].wait()
+    attended = parts_dot(split, held[4][...], 1) + own_weight / denominator * fresh[...]
     own[...] = attended
     for h in range(heads):
         out_ref[:, h * size : (h + 1) * size] = own[:, h, :].astype(BF)
 
 
-def attend(group_stream, w_query, w_key, w_value, cache_keys, cache_values, lengths):
+def attend(place, group_stream, w_query, w_key, w_value, cache_keys, cache_values, lengths):
     members, rows, cols = group_stream.shape
-    window, size = cache_keys.shape[2:]
+    window, size = cache_keys.shape[1:]
     pad = 8
+    large = in_hbm((w_query, w_key, w_value, cache_keys, cache_values))
     start = jnp.broadcast_to((window - lengths)[:, None, None], (rows, pad, window))
     return pl.pallas_call(
         attend_kernel,
-        in_specs=[pl.BlockSpec(memory_space=pltpu.VMEM)] * 7,
-        out_specs=pl.BlockSpec(memory_space=pltpu.VMEM),
-        out_shape=jax.ShapeDtypeStruct((rows, w_query.shape[1]), BF),
+        in_specs=[pl.BlockSpec(memory_space=pltpu.SMEM), pl.BlockSpec(memory_space=pltpu.VMEM)]
+        + [pl.BlockSpec(memory_space=pl.ANY)] * 5
+        + [pl.BlockSpec(memory_space=pltpu.VMEM)],
+        out_specs=[pl.BlockSpec(memory_space=pltpu.VMEM)] * 2,
+        out_shape=[
+            jax.ShapeDtypeStruct((rows // members, members * cols), BF),
+            jax.ShapeDtypeStruct((rows, w_query.shape[1]), BF),
+        ],
         scratch_shapes=[
             pltpu.VMEM((rows, members * cols), BF),
             pltpu.VMEM((rows, 3 * pad, size), F32),
             pltpu.VMEM((rows, pad, size), F32),
             pltpu.VMEM((rows, pad, size), F32),
+            pltpu.VMEM((rows, cols), F32),
+            *(pltpu.VMEM(a.shape, a.dtype) for a in large),
+            pltpu.SemaphoreType.DMA((4,)),
+            pltpu.SemaphoreType.DMA((members,)),
         ],
         compiler_params=pltpu.CompilerParams(vmem_limit_bytes=24 << 20),
         cost_estimate=pl.CostEstimate(
@@ -265,12 +325,9 @@
         ),
         name="attend",
     )(
+        place,
         group_stream,
-        w_query,
-        w_key,
-        w_value,
-        cache_keys[:, 0],
-        cache_values[:, 0],
+        *large,
         start.astype(jnp.int32),
     )
 
@@ -318,10 +375,11 @@
 
     sent = jnp.concatenate([tokens, routing_columns(expert_ids, combine, experts)], axis=1)
     own = [w_gate[0].T, w_up[0].T]
-    arrived, *other = lax.optimization_barrier(
-        (copies(sent, "z"), *(shift(w, "c", 1) for w in own))
+    arrived, down, *other = lax.optimization_barrier(
+        (copies(sent, "z"), w_down[0], *(shift(w, "c", 1) for w in own))
     )
     weights = own + other
+    down_own = lax.all_to_all(down, "z", 1, 0, tiled=True).reshape(members, hidden, cols)
     arrived = arrived.reshape(group, width + LANES)
     group_tokens, meta = arrived[:, :width], arrived[:, width:]
     widened = group_tokens.astype(F32)
@@ -337,18 +395,15 @@
     masks = masks.astype(BF)
     half = group // 2
 
-    def first_ring(block, axis):
-        after, before, opposite = (shift(block, axis, step) for step in (1, -1, 2))
-        return (
-            jnp.concatenate([block, after], axis=0),
-            jnp.concatenate([opposite, before], axis=0),
-        )
-
-    a_near, a_far = first_ring(dense[:half], "x")
-    b_near, b_far = first_ring(dense[half:], "y")
-    a_far, b_far, down = lax.optimization_barrier((a_far, b_far, w_down[0]))
-    down_own = lax.all_to_all(down, "z", 1, 0, tiled=True).reshape(members, hidden, cols)
+    def pairs(block, axis, mask):
+        return lax.ppermute(block, axis, [(i, i ^ mask) for i in range(4)])
+
+    def near_rows(block, axis):
+        return jnp.concatenate([block, pairs(block, axis, 1)], axis=0)
+
     sides = lambda part, axis: (shift(part, axis, 1), shift(part, axis, -1))
+    a_near, b_near = near_rows(dense[:half], "x"), near_rows(dense[half:], "y")
+    a_far, b_far = pairs(a_near, "x", 3), pairs(b_near, "y", 3)
     a_near_sides, b_near_sides = sides(a_near, "y"), sides(b_near, "x")
     a_far_sides, b_far_sides = sides(a_far, "y"), sides(b_far, "x")
     near = (a_near, a_far, b_near, b_far, *a_near_sides, *b_near_sides)
@@ -391,12 +446,9 @@
     )
     block_tokens = lax.dynamic_slice(group_tokens, (jnp.int32(0), z * cols), (group, cols))
     stream_block = (block_tokens.astype(F32) + mixture).astype(BF)
+    guard_args = (w_query, w_key, w_value, cache_keys[:, 0], cache_values[:, 0])
     group_stream = copies(stream_block, "z")
-    stream = lax.dynamic_slice(
-        group_stream, (jnp.int32(0), z * rows_n, jnp.int32(0)), (members, rows_n, cols)
-    )
-    stream = stream.transpose(1, 0, 2).reshape(rows_n, width)
-    guard = attend(group_stream, w_query, w_key, w_value, cache_keys, cache_values, lengths)
+    stream, guard = attend(place, group_stream, *guard_args, lengths)
     return (stream, guard)
 
 

time: 207 us -> 199 us (0.961)
  local copies, waits for them, and re-layouts: 13.6 us -> 4.94 us
  Pallas kernels: 28.2 us -> 33.2 us
  starting transfers between devices: 59.2 us -> 55.9 us
    ppermute x29 -> x23, starting transfers between devices: 44.6 us -> 32.3 us  [shift(): lax.ppermute(values, axis, [(i, (i - step) % size) for i in range(size)])]
    unnamed x42 -> x26, local copies, waits for them, and re-layouts: 9.34 us -> 1.42 us
    ppermute x0 -> x4, waiting for transfers between devices: none -> 7.28 us  [pairs(): return lax.ppermute(block, axis, [(i, i ^ mask) for i in range(4)])]
    ppermute x29 -> x23, waiting for transfers between devices: 33.8 us -> 27.3 us  [shift(): lax.ppermute(values, axis, [(i, (i - step) % size) for i in range(size)])]
    ppermute x0 -> x4, starting transfers between devices: none -> 6.45 us  [pairs(): return lax.ppermute(block, axis, [(i, i ^ mask) for i in range(4)])]
    pallas_call x1, Pallas kernels: 4.04 us -> 7.62 us  [attend(): pl.pallas_call(attend_kernel, in_specs=[pl.BlockSpec(memory_space=pltpu.S...]
  transfers between devices with their start and end apart: 33 -> 31, of which waited for: 20 -> 15; matrix products, arithmetic and copies ran while one was open for 4% -> 3% of each run, Pallas kernels for 10% -> 10%
where the time goes in v2:
time: 199 us; the launch traced here: 198 us
  waiting for transfers between devices  57.5 us (29%)
  starting transfers between devices  55.9 us (28%)
  Pallas kernels  33.2 us (17%)
  blocking collectives  26.4 us (13%)
  between operations  14.4 us (7%)
  other arithmetic  5.32 us (3%)
  local copies, waits for them, and re-layouts  4.94 us (2%)
    ppermute x23, starting transfers between devices, shift(): lax.ppermute(values, axis, [(i, (i - step) % size) for i in range(size)])  32.3 us
    ppermute x23, waiting for transfers between devices, shift(): lax.ppermute(values, axis, [(i, (i - step) % size) for i in range(size)])  27.3 us
    all_to_all x1, blocking collectives, copies(): lax.all_to_all(jnp.broadcast_to(values[None], (size, *values.shape)), axi...  26.4 us
    pallas_call x3, Pallas kernels, expert_slots(): pl.pallas_call(functools.partial(expert_kernel, sizes, steps), grid=(step...  20.4 us
    all_to_all x1, waiting for transfers between devices, copies(): lax.all_to_all(jnp.broadcast_to(values[None], (size, *values.shape)), axi...  13.3 us
    all_to_all x1, waiting for transfers between devices, per_device(): returned = lax.all_to_all(result, ('x', 'y'), 0, 0, tiled=True)  9.58 us
    all_to_all x1, starting transfers between devices, per_device(): returned = lax.all_to_all(result, ('x', 'y'), 0, 0, tiled=True)  8.39 us
    pallas_call x1, Pallas kernels, attend(): pl.pallas_call(attend_kernel, in_specs=[pl.BlockSpec(memory_space=pltpu.S...  7.62 us
  transfers between devices with their start and end apart: 31, of which 15 were waited for; matrix products, arithmetic and copies ran while one was open for 3% of the time, Pallas kernels for 10%

profile of v2, /device:TPU:8, one launch (start us, length us, event | category | flops | bytes accessed | tf_op | source)
XLA Modules:
  0.0 198.1 jit_solution(17167480140212015488)
XLA Ops:
  7.8 0.8 fusion.4
  8.6 0.8 select_reduce_fusion
  9.5 0.9 concatenate.21
  10.4 26.4 %all_to_all.31 = bf16[8,8,4224]{2,1,0:T(8,128)(2,1)S(1)} all-to-all(bf16[8,8,4224]{2,1,0:T(8,128)(2,1)S(1)} %broadcast_in_dim.37), channel_id=1, replica_groups=mesh['x'=4,'y'=4,'c'=2,'z'=8] {'z'}, dimensions={0} | all-to-all | bytes 1081344 | tf_op jit(solution)/shard_map/all_to_all | solution.py:39
  37.1 0.6 copy-done.2
  37.8 0.8 pad_maximum_fusion.2
  39.0 1.5 collective-permute-start.2
  40.5 1.3 copy.25
  41.8 3.6 %all-to-all-start.1 = ((bf16[192,8,512]{2,0,1:T(8,128)(2,1)}), bf16[192,8,512]{2,0,1:T(8,128)(2,1)S(1)}, u32[]{:S(2)}, u32[]{:S(2)}) async-start(bf16[192,8,512]{2,0,1:T(8,128)(2,1)} %bitcast.46), calls=%async_computation.1 | async-start | bytes 3145728 | tf_op jit(solution)/shard_map/all_to_all | solution.py:382
  45.4 0.6 collective-permute-done.4
  46.1 1.1 pad_maximum_fusion.1.refs_2_.refs_10_
  47.2 1.9 collective-permute-start.5
  49.0 1.0 pad_maximum_fusion.refs_0_.refs_8_
  50.0 2.6 %collective-permute-start.3 = (bf16[64,4224]{1,0:T(8,128)(2,1)S(1)}, bf16[64,4224]{1,0:T(8,128)(2,1)}, u32[]{:S(2)}, u32[]{:S(2)}) collective-permute-start(bf16[64,4224]{1,0:T(8,128)(2,1)S(1)} %pad_maximum_fusion.refs_0_.refs_8_), channel_id=1, source_target_pairs={{0,192},{64,128},{128,64},{192,0},{1,193},{65,129},{129,65},{193,1... | collective-permute-start | bytes 1622024 | tf_op jit(solution)/shard_map/ppermute | solution.py:399
  53.3 3.0 %collective-permute-start.8 = (bf16[64,4224]{1,0:T(8,128)(2,1)S(1)}, bf16[64,4224]{1,0:T(8,128)(2,1)}, u32[]{:S(2)}, u32[]{:S(2)}) collective-permute-start(bf16[64,4224]{1,0:T(8,128)(2,1)S(1)} %pad_maximum_fusion.1.refs_2_.refs_10_), channel_id=1, source_target_pairs={{0,192},{64,0},{128,64},{192,128},{1,193},{65,1},{129,65},{193,129... | collective-permute-start | bytes 1622024 | tf_op jit(solution)/shard_map/ppermute | solution.py:21
  56.4 5.4 %collective-permute-done.5.refs_3_.refs_11_ = bf16[64,4224]{1,0:T(8,128)(2,1)S(1)} collective-permute-done((bf16[64,4224]{1,0:T(8,128)(2,1)S(1)}, bf16[64,4224]{1,0:T(8,128)(2,1)S(1)}, u32[]{:S(2)}, u32[]{:S(2)}) %collective-permute-start.5) | collective-permute-done | bytes 540704 | tf_op jit(solution)/shard_map/ppermute | solution.py:399
  61.8 0.8 copy-done.8
  62.5 2.9 %collective-permute-start.6 = (bf16[64,4224]{1,0:T(8,128)(2,1)S(1)}, bf16[64,4224]{1,0:T(8,128)(2,1)}, u32[]{:S(2)}, u32[]{:S(2)}) collective-permute-start(bf16[64,4224]{1,0:T(8,128)(2,1)S(1)} %pad_maximum_fusion.refs_0_.refs_8_), channel_id=1, source_target_pairs={{0,48},{16,0},{32,16},{48,32},{1,49},{17,1},{33,17},{49,33},{2,50}... | collective-permute-start | bytes 1622024 | tf_op jit(solution)/shard_map/ppermute | solution.py:21
  65.4 1.2 collective-permute-done.3.refs_1_.refs_9_
  66.6 2.6 %collective-permute-start.12 = (bf16[64,4224]{1,0:T(8,128)(2,1)}, bf16[64,4224]{1,0:T(8,128)(2,1)}, u32[]{:S(2)}, u32[]{:S(2)}) collective-permute-start(bf16[64,4224]{1,0:T(8,128)(2,1)} %copy-done.8), channel_id=1, source_target_pairs={{0,192},{64,0},{128,64},{192,128},{1,193},{65,1},{129,65},{193,129... | collective-permute-start | bytes 1622024 | tf_op jit(solution)/shard_map/ppermute | solution.py:21
  69.2 5.8 %collective-permute-done.9.refs_7_.refs_15_ = bf16[64,4224]{1,0:T(8,128)(2,1)S(1)} collective-permute-done((bf16[64,4224]{1,0:T(8,128)(2,1)S(1)}, bf16[64,4224]{1,0:T(8,128)(2,1)S(1)}, u32[]{:S(2)}, u32[]{:S(2)}) %collective-permute-start.9) | collective-permute-done | bytes 540704 | tf_op jit(solution)/shard_map/ppermute | solution.py:21
  75.1 1.4 collective-permute-start.10
  76.5 0.5 collective-permute-done.8.refs_6_.refs_14_
  77.5 8.5 %expert_slots.3 = bf16[192,384]{1,0:T(8,128)(2,1)} custom-call(bf16[8,128]{1,0:T(8,128)(2,1)S(1)} %convert_convert_fusion.mask_ref, bf16[64,4224]{1,0:T(8,128)(2,1)} %copy-done.6, bf16[64,4224]{1,0:T(8,128)(2,1)} %collective-permute-done.3.refs_1_.refs_9_, bf16[64,4224]{1,0:T(8,128)(2,1)} %copy-done.5, bf16[64,4224]{1,0:T(8,128)(2,1)} %copy-done.8, ...), custom_call_target="tpu_custom_call" | custom-call | flops 3221225472 | bytes 10485760 | tf_op jit(solution)/shard_map/expert_slots/pallas_call | solution.py:108
  86.1 1.7 collective-permute-done.13.refs_3_.refs_7_
  88.0 1.9 collective-permute-start.17
  89.9 0.9 collective-permute-start.15
  90.7 1.2 collective-permute-start.16
  91.9 3.5 %collective-permute-start.18 = (bf16[64,4224]{1,0:T(8,128)(2,1)}, bf16[64,4224]{1,0:T(8,128)(2,1)}, u32[]{:S(2)}, u32[]{:S(2)}) collective-permute-start(bf16[64,4224]{1,0:T(8,128)(2,1)} %collective-permute-done.12.refs_2_.refs_6_), channel_id=1, source_target_pairs={{0,192},{64,0},{128,64},{192,128},{1,193},{65,1},{129,65},{193,129... | collective-permute-start | bytes 1622024 | tf_op jit(solution)/shard_map/ppermute | solution.py:21
  95.4 5.9 %expert_slots.4 = bf16[96,384]{1,0:T(8,128)(2,1)S(1)} custom-call(bf16[8,128]{1,0:T(8,128)(2,1)S(1)} %convert_convert_fusion.mask_ref, bf16[64,4224]{1,0:T(8,128)(2,1)} %collective-permute-done.10.refs_0_.refs_4_, bf16[64,4224]{1,0:T(8,128)(2,1)} %collective-permute-done.11.refs_1_.refs_5_, bf16[64,4224]{1,0:T(8,128)(2,1)} %collective-permute-done.12.refs_2_.refs_6_, ...), custom_call_target="tpu_custom_call" | custom-call | flops 1610612736 | bytes 8388608 | tf_op jit(solution)/shard_map/expert_slots/pallas_call | solution.py:108
  101.4 1.1 collective-permute-done.18.refs_3_.refs_7_
  102.6 5.9 %expert_slots.5 = bf16[96,384]{1,0:T(8,128)(2,1)S(1)} custom-call(bf16[8,128]{1,0:T(8,128)(2,1)S(1)} %convert_convert_fusion.mask_ref, bf16[64,4224]{1,0:T(8,128)(2,1)} %copy-done.10, bf16[64,4224]{1,0:T(8,128)(2,1)} %collective-permute-done.16.refs_1_.refs_5_, bf16[64,4224]{1,0:T(8,128)(2,1)} %copy-done.9, ...), custom_call_target="tpu_custom_call" | custom-call | flops 1610612736 | bytes 8388608 | tf_op jit(solution)/shard_map/expert_slots/pallas_call | solution.py:108
  108.5 1.8 collective-permute-start.19
  110.6 5.4 %collective-permute-done.19.refs_1_ = bf16[192,384]{1,0:T(8,128)(2,1)S(1)} collective-permute-done((bf16[192,384]{1,0:T(8,128)(2,1)S(1)}, bf16[192,384]{1,0:T(8,128)(2,1)S(1)}, u32[]{:S(2)}, u32[]{:S(2)}) %collective-permute-start.19) | collective-permute-done | bytes 147488 | tf_op jit(solution)/shard_map/ppermute | solution.py:21
  116.1 3.5 %collective-permute-start.20 = (bf16[192,384]{1,0:T(8,128)(2,1)S(1)}, bf16[192,384]{1,0:T(8,128)(2,1)S(1)}, u32[]{:S(2)}, u32[]{:S(2)}) collective-permute-start(bf16[192,384]{1,0:T(8,128)(2,1)S(1)} %collective-permute-done.19.refs_1_), channel_id=1, source_target_pairs={{0,7},{1,0},{2,1},{3,2},{4,3},{5,4},{6,5},{7,6},{8,15},{9,8},{10,9... | collective-permute-start | bytes 442376 | tf_op jit(solution)/shard_map/ppermute | solution.py:21
  119.6 4.5 %collective-permute-done.20.refs_2_ = bf16[192,384]{1,0:T(8,128)(2,1)S(1)} collective-permute-done((bf16[192,384]{1,0:T(8,128)(2,1)S(1)}, bf16[192,384]{1,0:T(8,128)(2,1)S(1)}, u32[]{:S(2)}, u32[]{:S(2)}) %collective-permute-start.20) | collective-permute-done | bytes 147488 | tf_op jit(solution)/shard_map/ppermute | solution.py:21
  124.1 3.6 %collective-permute-start.21 = (bf16[192,384]{1,0:T(8,128)(2,1)S(1)}, bf16[192,384]{1,0:T(8,128)(2,1)S(1)}, u32[]{:S(2)}, u32[]{:S(2)}) collective-permute-start(bf16[192,384]{1,0:T(8,128)(2,1)S(1)} %collective-permute-done.20.refs_2_), channel_id=1, source_target_pairs={{0,7},{1,0},{2,1},{3,2},{4,3},{5,4},{6,5},{7,6},{8,15},{9,8},{10,9... | collective-permute-start | bytes 442376 | tf_op jit(solution)/shard_map/ppermute | solution.py:21
  127.7 2.6 %collective-permute-done.21.refs_3_ = bf16[192,384]{1,0:T(8,128)(2,1)S(1)} collective-permute-done((bf16[192,384]{1,0:T(8,128)(2,1)S(1)}, bf16[192,384]{1,0:T(8,128)(2,1)S(1)}, u32[]{:S(2)}, u32[]{:S(2)}) %collective-permute-start.21) | collective-permute-done | bytes 147488 | tf_op jit(solution)/shard_map/ppermute | solution.py:21
  130.3 4.0 %collective-permute-start.22 = (bf16[96,384]{1,0:T(8,128)(2,1)S(1)}, bf16[96,384]{1,0:T(8,128)(2,1)S(1)}, u32[]{:S(2)}, u32[]{:S(2)}) collective-permute-start(bf16[96,384]{1,0:T(8,128)(2,1)S(1)} %slice.52), channel_id=1, source_target_pairs={{0,7},{1,0},{2,1},{3,2},{4,3},{5,4},{6,5},{7,6},{8,15},{9,8},{10,9... | collective-permute-start | bytes 221192 | tf_op jit(solution)/shard_map/ppermute | solution.py:21
  134.5 1.8 collective-permute-done.22
  136.3 3.7 %collective-permute-done.26 = bf16[96,384]{1,0:T(8,128)(2,1)S(1)} collective-permute-done((bf16[96,384]{1,0:T(8,128)(2,1)S(1)}, bf16[96,384]{1,0:T(8,128)(2,1)S(1)}, u32[]{:S(2)}, u32[]{:S(2)}) %collective-permute-start.26) | collective-permute-done | bytes 73760 | tf_op jit(solution)/shard_map/ppermute | solution.py:21
  140.0 5.2 %lower.1 = bf16[16,2,24,512]{3,2,1,0:T(8,128)(2,1)} custom-call(s32[3]{0:T(128)S(1)} %pad_add_fusion.place_ref, bf16[8,192,384]{2,1,0:T(8,128)(2,1)} %bitcast.52, bf16[8,192,512]{2,1,0:T(8,128)(2,1)} %bitcast.48, bf16[8,192,512]{2,1,0:T(8,128)(2,1)} %collective-permute-done.14.other_ref, bf16[192,384]{1,0:T(8,128)(2,1)S(1)} %pad_maximum_fusion.3.refs_0_, ...), custom_call_target="tpu_custom_call" | custom-call | flops 1207959552 | bytes 5505024 | tf_op jit(solution)/shard_map/lower/pallas_call | solution.py:190
  145.2 8.4 %all-to-all-start.2 = ((bf16[16,48,512]{2,1,0:T(8,128)(2,1)}), bf16[16,48,512]{2,1,0:T(8,128)(2,1)S(1)}, u32[]{:S(2)}, u32[]{:S(2)}) async-start(bf16[16,48,512]{2,1,0:T(8,128)(2,1)} %bitcast.16), calls=%async_computation.2 | async-start | bytes 1572864 | tf_op jit(solution)/shard_map/all_to_all | solution.py:428
  154.1 9.6 %all-to-all-done.2 = bf16[16,48,512]{2,1,0:T(8,128)(2,1)S(1)} async-done(((bf16[16,48,512]{2,1,0:T(8,128)(2,1)}), bf16[16,48,512]{2,1,0:T(8,128)(2,1)S(1)}, u32[]{:S(2)}, u32[]{:S(2)}) %all-to-all-start.2) | async-done | bytes 786464 | tf_op jit(solution)/shard_map/all_to_all | solution.py:428
  164.2 0.8 broadcast_in_dim.40
  165.0 5.2 %all-to-all-start.3 = ((bf16[8,64,512]{2,1,0:T(8,128)(2,1)}), bf16[8,64,512]{2,1,0:T(8,128)(2,1)S(1)}, u32[]{:S(2)}, u32[]{:S(2)}) async-start(bf16[8,64,512]{2,1,0:T(8,128)(2,1)} %broadcast_in_dim.40), calls=%async_computation.3 | async-start | bytes 1048576 | tf_op jit(solution)/shard_map/all_to_all | solution.py:39
  170.2 13.3 %all-to-all-done.3.stream_ref = bf16[8,64,512]{2,1,0:T(8,128)(2,1)S(1)} async-done(((bf16[8,64,512]{2,1,0:T(8,128)(2,1)}), bf16[8,64,512]{2,1,0:T(8,128)(2,1)S(1)}, u32[]{:S(2)}, u32[]{:S(2)}) %all-to-all-start.3) | async-done | bytes 524320 | tf_op jit(solution)/shard_map/all_to_all | solution.py:39
  183.6 7.6 %attend.1 = (bf16[8,4096]{1,0:T(8,128)(2,1)}, bf16[64,512]{1,0:T(8,128)(2,1)}) custom-call(s32[3]{0:T(128)S(1)} %pad_add_fusion.place_ref, bf16[8,64,512]{2,1,0:T(8,128)(2,1)S(1)} %all-to-all-done.3.stream_ref, bf16[4096,512]{1,0:T(8,128)(2,1)} %wq_ref.1, bf16[4096,128]{1,0:T(8,128)(2,1)} %wk_ref.1, bf16[4096,128]{1,0:T(8,128)(2,1)} %wv_ref.1, ...), custom_call_target="tpu_custom_call" | custom-call | flops 402653184 | bytes 6291456 | tf_op jit(solution)/shard_map/attend/pallas_call | solution.py:300
  (89 shorter events, 4.9 us)
Async XLA Ops:
  7.2 29.7 %collective-permute-start = (bf16[192,4096]{1,0:T(8,128)(2,1)}, bf16[192,4096]{1,0:T(8,128)(2,1)S(1)}, u32[]{:S(2)}, u32[]{:S(2)}) collective-permute-start(bf16[192,4096]{1,0:T(8,128)(2,1)} %bitcast.32), channel_id=1, source_target_pairs={{0,8},{8,0},{1,9},{9,1},{2,10},{10,2},{3,11},{11,3},{4,12},{12,4},... | collective-permute-start | bytes 4718600 | tf_op jit(solution)/shard_map/ppermute | solution.py:21
  7.3 29.6 %collective-permute-start.1 = (bf16[192,4096]{1,0:T(8,128)(2,1)}, bf16[192,4096]{1,0:T(8,128)(2,1)S(1)}, u32[]{:S(2)}, u32[]{:S(2)}) collective-permute-start(bf16[192,4096]{1,0:T(8,128)(2,1)} %bitcast.36), channel_id=1, source_target_pairs={{0,8},{8,0},{1,9},{9,1},{2,10},{10,2},{3,11},{11,3},{4,12},{12,4},... | collective-permute-start | bytes 4718600 | tf_op jit(solution)/shard_map/ppermute | solution.py:21
  36.8 0.8 copy-start.2
  36.8 3.7 %copy-start.11 = (bf16[1,192,4096]{2,1,0:T(8,128)(2,1)S(1)}, bf16[1,192,4096]{2,1,0:T(8,128)(2,1)}, u32[]{:S(2)}) copy-start(bf16[1,192,4096]{2,1,0:T(8,128)(2,1)} %param.17) | copy-start | bytes 4718596
  36.8 5.0 %copy-start = (bf16[192,4096]{1,0:T(8,128)(2,1)}, bf16[192,4096]{1,0:T(8,128)(2,1)S(1)}, u32[]{:S(2)}) copy-start(bf16[192,4096]{1,0:T(8,128)(2,1)S(1)} %collective-permute-done.refs_18_.refs_10_) | copy-start | bytes 4718596
  36.8 5.0 %copy-start.1 = (bf16[192,4096]{1,0:T(8,128)(2,1)}, bf16[192,4096]{1,0:T(8,128)(2,1)S(1)}, u32[]{:S(2)}) copy-start(bf16[192,4096]{1,0:T(8,128)(2,1)S(1)} %collective-permute-done.1.refs_19_.refs_11_) | copy-start | bytes 4718596
  38.6 7.5 %collective-permute-start.4 = (bf16[32,4224]{1,0:T(8,128)(2,1)}, bf16[32,4224]{1,0:T(8,128)(2,1)}, u32[]{:S(2)}, u32[]{:S(2)}) collective-permute-start(bf16[32,4224]{1,0:T(8,128)(2,1)} %get-tuple-element.24), channel_id=1, source_target_pairs={{0,16},{16,0},{32,48},{48,32},{1,17},{17,1},{33,49},{49,33},{2,18}... | collective-permute-start | bytes 811016 | tf_op jit(solution)/shard_map/ppermute | solution.py:399
  39.0 10.0 %collective-permute-start.2 = (bf16[32,4224]{1,0:T(8,128)(2,1)S(1)}, bf16[32,4224]{1,0:T(8,128)(2,1)}, u32[]{:S(2)}, u32[]{:S(2)}) collective-permute-start(bf16[32,4224]{1,0:T(8,128)(2,1)S(1)} %get-tuple-element.25), channel_id=1, source_target_pairs={{0,64},{64,0},{128,192},{192,128},{1,65},{65,1},{129,193},{193,129... | collective-permute-start | bytes 811016 | tf_op jit(solution)/shard_map/ppermute | solution.py:399
  41.8 59.5 %all-to-all-start.1 = ((bf16[192,8,512]{2,0,1:T(8,128)(2,1)}), bf16[192,8,512]{2,0,1:T(8,128)(2,1)S(1)}, u32[]{:S(2)}, u32[]{:S(2)}) async-start(bf16[192,8,512]{2,0,1:T(8,128)(2,1)} %bitcast.46), calls=%async_computation.1 | async-start | bytes 3145728 | tf_op jit(solution)/shard_map/all_to_all | solution.py:382
  45.4 94.6 %all-gather.3.cloned.1.call-start = ((), (), s32[]{:S(2)}) async-start(), calls=%async_computation.4 | async-start | bytes 1327104 | tf_op jit(solution)/shard_map/all_gather | solution.py:419
  47.1 30.4 %copy-start.5 = (bf16[64,4224]{1,0:T(8,128)(2,1)}, bf16[64,4224]{1,0:T(8,128)(2,1)S(1)}, u32[]{:S(2)}) copy-start(bf16[64,4224]{1,0:T(8,128)(2,1)S(1)} %pad_maximum_fusion.1.refs_2_.refs_10_) | copy-start | bytes 1622020
  47.2 14.6 %collective-permute-start.5 = (bf16[64,4224]{1,0:T(8,128)(2,1)S(1)}, bf16[64,4224]{1,0:T(8,128)(2,1)S(1)}, u32[]{:S(2)}, u32[]{:S(2)}) collective-permute-start(bf16[64,4224]{1,0:T(8,128)(2,1)S(1)} %pad_maximum_fusion.1.refs_2_.refs_10_), channel_id=1, source_target_pairs={{0,48},{16,32},{32,16},{48,0},{1,49},{17,33},{33,17},{49,1},{2,50}... | collective-permute-start | bytes 1622024 | tf_op jit(solution)/shard_map/ppermute | solution.py:399
  50.0 27.5 %copy-start.6 = (bf16[64,4224]{1,0:T(8,128)(2,1)}, bf16[64,4224]{1,0:T(8,128)(2,1)S(1)}, u32[]{:S(2)}) copy-start(bf16[64,4224]{1,0:T(8,128)(2,1)S(1)} %pad_maximum_fusion.refs_0_.refs_8_) | copy-start | bytes 1622020
  50.0 16.6 %collective-permute-start.3 = (bf16[64,4224]{1,0:T(8,128)(2,1)S(1)}, bf16[64,4224]{1,0:T(8,128)(2,1)}, u32[]{:S(2)}, u32[]{:S(2)}) collective-permute-start(bf16[64,4224]{1,0:T(8,128)(2,1)S(1)} %pad_maximum_fusion.refs_0_.refs_8_), channel_id=1, source_target_pairs={{0,192},{64,128},{128,64},{192,0},{1,193},{65,129},{129,65},{193,1... | collective-permute-start | bytes 1622024 | tf_op jit(solution)/shard_map/ppermute | solution.py:399
  52.7 22.4 %collective-permute-start.9 = (bf16[64,4224]{1,0:T(8,128)(2,1)S(1)}, bf16[64,4224]{1,0:T(8,128)(2,1)S(1)}, u32[]{:S(2)}, u32[]{:S(2)}) collective-permute-start(bf16[64,4224]{1,0:T(8,128)(2,1)S(1)} %pad_maximum_fusion.1.refs_2_.refs_10_), channel_id=1, source_target_pairs={{0,64},{64,128},{128,192},{192,0},{1,65},{65,129},{129,193},{193,1... | collective-permute-start | bytes 1622024 | tf_op jit(solution)/shard_map/ppermute | solution.py:21
  52.9 22.2 %collective-permute-start.7 = (bf16[64,4224]{1,0:T(8,128)(2,1)S(1)}, bf16[64,4224]{1,0:T(8,128)(2,1)}, u32[]{:S(2)}, u32[]{:S(2)}) collective-permute-start(bf16[64,4224]{1,0:T(8,128)(2,1)S(1)} %pad_maximum_fusion.refs_0_.refs_8_), channel_id=1, source_target_pairs={{0,16},{16,32},{32,48},{48,0},{1,17},{17,33},{33,49},{49,1},{2,18}... | collective-permute-start | bytes 1622024 | tf_op jit(solution)/shard_map/ppermute | solution.py:21
  53.3 23.6 %collective-permute-start.8 = (bf16[64,4224]{1,0:T(8,128)(2,1)S(1)}, bf16[64,4224]{1,0:T(8,128)(2,1)}, u32[]{:S(2)}, u32[]{:S(2)}) collective-permute-start(bf16[64,4224]{1,0:T(8,128)(2,1)S(1)} %pad_maximum_fusion.1.refs_2_.refs_10_), channel_id=1, source_target_pairs={{0,192},{64,0},{128,64},{192,128},{1,193},{65,1},{129,65},{193,129... | collective-permute-start | bytes 1622024 | tf_op jit(solution)/shard_map/ppermute | solution.py:21
  61.8 0.8 copy-start.8
  62.5 15.0 %collective-permute-start.6 = (bf16[64,4224]{1,0:T(8,128)(2,1)S(1)}, bf16[64,4224]{1,0:T(8,128)(2,1)}, u32[]{:S(2)}, u32[]{:S(2)}) collective-permute-start(bf16[64,4224]{1,0:T(8,128)(2,1)S(1)} %pad_maximum_fusion.refs_0_.refs_8_), channel_id=1, source_target_pairs={{0,48},{16,0},{32,16},{48,32},{1,49},{17,1},{33,17},{49,33},{2,50}... | collective-permute-start | bytes 1622024 | tf_op jit(solution)/shard_map/ppermute | solution.py:21
  66.6 19.4 %collective-permute-start.12 = (bf16[64,4224]{1,0:T(8,128)(2,1)}, bf16[64,4224]{1,0:T(8,128)(2,1)}, u32[]{:S(2)}, u32[]{:S(2)}) collective-permute-start(bf16[64,4224]{1,0:T(8,128)(2,1)} %copy-done.8), channel_id=1, source_target_pairs={{0,192},{64,0},{128,64},{192,128},{1,193},{65,1},{129,65},{193,129... | collective-permute-start | bytes 1622024 | tf_op jit(solution)/shard_map/ppermute | solution.py:21
  75.0 2.5 %copy-start.7 = (bf16[64,4224]{1,0:T(8,128)(2,1)}, bf16[64,4224]{1,0:T(8,128)(2,1)S(1)}, u32[]{:S(2)}) copy-start(bf16[64,4224]{1,0:T(8,128)(2,1)S(1)} %collective-permute-done.9.refs_7_.refs_15_) | copy-start | bytes 1622020
  75.1 12.7 %collective-permute-start.13 = (bf16[64,4224]{1,0:T(8,128)(2,1)}, bf16[64,4224]{1,0:T(8,128)(2,1)}, u32[]{:S(2)}, u32[]{:S(2)}) collective-permute-start(bf16[64,4224]{1,0:T(8,128)(2,1)} %copy-done.8), channel_id=1, source_target_pairs={{0,64},{64,128},{128,192},{192,0},{1,65},{65,129},{129,193},{193,1... | collective-permute-start | bytes 1622024 | tf_op jit(solution)/shard_map/ppermute | solution.py:21
  75.1 12.7 %collective-permute-start.10 = (bf16[64,4224]{1,0:T(8,128)(2,1)}, bf16[64,4224]{1,0:T(8,128)(2,1)}, u32[]{:S(2)}, u32[]{:S(2)}) collective-permute-start(bf16[64,4224]{1,0:T(8,128)(2,1)} %collective-permute-done.3.refs_1_.refs_9_), channel_id=1, source_target_pairs={{0,48},{16,0},{32,16},{48,32},{1,49},{17,1},{33,17},{49,33},{2,50}... | collective-permute-start | bytes 1622024 | tf_op jit(solution)/shard_map/ppermute | solution.py:21
  77.0 10.9 %collective-permute-start.11 = (bf16[64,4224]{1,0:T(8,128)(2,1)}, bf16[64,4224]{1,0:T(8,128)(2,1)}, u32[]{:S(2)}, u32[]{:S(2)}) collective-permute-start(bf16[64,4224]{1,0:T(8,128)(2,1)} %collective-permute-done.3.refs_1_.refs_9_), channel_id=1, source_target_pairs={{0,16},{16,32},{32,48},{48,0},{1,17},{17,33},{33,49},{49,1},{2,18}... | collective-permute-start | bytes 1622024 | tf_op jit(solution)/shard_map/ppermute | solution.py:21
  88.0 13.4 %collective-permute-start.17 = (bf16[64,4224]{1,0:T(8,128)(2,1)}, bf16[64,4224]{1,0:T(8,128)(2,1)S(1)}, u32[]{:S(2)}, u32[]{:S(2)}) collective-permute-start(bf16[64,4224]{1,0:T(8,128)(2,1)} %copy-done.7), channel_id=1, source_target_pairs={{0,64},{64,128},{128,192},{192,0},{1,65},{65,129},{129,193},{193,1... | collective-permute-start | bytes 1622024 | tf_op jit(solution)/shard_map/ppermute | solution.py:21
  89.9 11.5 %collective-permute-start.15 = (bf16[64,4224]{1,0:T(8,128)(2,1)}, bf16[64,4224]{1,0:T(8,128)(2,1)S(1)}, u32[]{:S(2)}, u32[]{:S(2)}) collective-permute-start(bf16[64,4224]{1,0:T(8,128)(2,1)} %collective-permute-done.7.refs_5_.refs_13_), channel_id=1, source_target_pairs={{0,16},{16,32},{32,48},{48,0},{1,17},{17,33},{33,49},{49,1},{2,18}... | collective-permute-start | bytes 1622024 | tf_op jit(solution)/shard_map/ppermute | solution.py:21
  90.7 10.7 %collective-permute-start.16 = (bf16[64,4224]{1,0:T(8,128)(2,1)}, bf16[64,4224]{1,0:T(8,128)(2,1)}, u32[]{:S(2)}, u32[]{:S(2)}) collective-permute-start(bf16[64,4224]{1,0:T(8,128)(2,1)} %collective-permute-done.10.refs_0_.refs_4_), channel_id=1, source_target_pairs={{0,48},{16,0},{32,16},{48,32},{1,49},{17,1},{33,17},{49,33},{2,50}... | collective-permute-start | bytes 1622024 | tf_op jit(solution)/shard_map/ppermute | solution.py:21
  91.9 10.7 %collective-permute-start.18 = (bf16[64,4224]{1,0:T(8,128)(2,1)}, bf16[64,4224]{1,0:T(8,128)(2,1)}, u32[]{:S(2)}, u32[]{:S(2)}) collective-permute-start(bf16[64,4224]{1,0:T(8,128)(2,1)} %collective-permute-done.12.refs_2_.refs_6_), channel_id=1, source_target_pairs={{0,192},{64,0},{128,64},{192,128},{1,193},{65,1},{129,65},{193,129... | collective-permute-start | bytes 1622024 | tf_op jit(solution)/shard_map/ppermute | solution.py:21
  101.3 7.2 %copy-start.4 = (bf16[192,8,512]{2,0,1:T(8,128)(2,1)}, bf16[192,8,512]{2,0,1:T(8,128)(2,1)S(1)}, u32[]{:S(2)}) copy-start(bf16[192,8,512]{2,0,1:T(8,128)(2,1)S(1)} %all-to-all-done.1) | copy-start | bytes 4718596
  101.3 38.7 %collective-permute-start.14 = (bf16[8,192,512]{2,1,0:T(8,128)(2,1)S(1)}, bf16[8,192,512]{2,1,0:T(8,128)(2,1)}, u32[]{:S(2)}, u32[]{:S(2)}) collective-permute-start(bf16[8,192,512]{2,1,0:T(8,128)(2,1)S(1)} %bitcast.47), channel_id=1, source_target_pairs={{0,8},{8,0},{1,9},{9,1},{2,10},{10,2},{3,11},{11,3},{4,12},{12,4},... | collective-permute-start | bytes 4718600 | tf_op jit(solution)/shard_map/ppermute | solution.py:21
  101.4 1.2 copy-start.9
  101.4 1.1 copy-start.10
  108.5 7.5 %collective-permute-start.19 = (bf16[192,384]{1,0:T(8,128)(2,1)S(1)}, bf16[192,384]{1,0:T(8,128)(2,1)S(1)}, u32[]{:S(2)}, u32[]{:S(2)}) collective-permute-start(bf16[192,384]{1,0:T(8,128)(2,1)S(1)} %pad_maximum_fusion.3.refs_0_), channel_id=1, source_target_pairs={{0,7},{1,0},{2,1},{3,2},{4,3},{5,4},{6,5},{7,6},{8,15},{9,8},{10,9... | collective-permute-start | bytes 442376 | tf_op jit(solution)/shard_map/ppermute | solution.py:21
  110.3 9.3 %collective-permute-start.23 = (bf16[192,384]{1,0:T(8,128)(2,1)S(1)}, bf16[192,384]{1,0:T(8,128)(2,1)S(1)}, u32[]{:S(2)}, u32[]{:S(2)}) collective-permute-start(bf16[192,384]{1,0:T(8,128)(2,1)S(1)} %pad_maximum_fusion.3.refs_0_), channel_id=1, source_target_pairs={{0,1},{1,2},{2,3},{3,4},{4,5},{5,6},{6,7},{7,0},{8,9},{9,10},{10,1... | collective-permute-start | bytes 442376 | tf_op jit(solution)/shard_map/ppermute | solution.py:21
  116.1 8.0 %collective-permute-start.20 = (bf16[192,384]{1,0:T(8,128)(2,1)S(1)}, bf16[192,384]{1,0:T(8,128)(2,1)S(1)}, u32[]{:S(2)}, u32[]{:S(2)}) collective-permute-start(bf16[192,384]{1,0:T(8,128)(2,1)S(1)} %collective-permute-done.19.refs_1_), channel_id=1, source_target_pairs={{0,7},{1,0},{2,1},{3,2},{4,3},{5,4},{6,5},{7,6},{8,15},{9,8},{10,9... | collective-permute-start | bytes 442376 | tf_op jit(solution)/shard_map/ppermute | solution.py:21
  119.6 8.0 %collective-permute-start.24 = (bf16[192,384]{1,0:T(8,128)(2,1)S(1)}, bf16[192,384]{1,0:T(8,128)(2,1)S(1)}, u32[]{:S(2)}, u32[]{:S(2)}) collective-permute-start(bf16[192,384]{1,0:T(8,128)(2,1)S(1)} %collective-permute-done.23.refs_7_), channel_id=1, source_target_pairs={{0,1},{1,2},{2,3},{3,4},{4,5},{5,6},{6,7},{7,0},{8,9},{9,10},{10,1... | collective-permute-start | bytes 442376 | tf_op jit(solution)/shard_map/ppermute | solution.py:21
  124.1 6.2 %collective-permute-start.21 = (bf16[192,384]{1,0:T(8,128)(2,1)S(1)}, bf16[192,384]{1,0:T(8,128)(2,1)S(1)}, u32[]{:S(2)}, u32[]{:S(2)}) collective-permute-start(bf16[192,384]{1,0:T(8,128)(2,1)S(1)} %collective-permute-done.20.refs_2_), channel_id=1, source_target_pairs={{0,7},{1,0},{2,1},{3,2},{4,3},{5,4},{6,5},{7,6},{8,15},{9,8},{10,9... | collective-permute-start | bytes 442376 | tf_op jit(solution)/shard_map/ppermute | solution.py:21
  127.6 6.7 %collective-permute-start.25 = (bf16[192,384]{1,0:T(8,128)(2,1)S(1)}, bf16[192,384]{1,0:T(8,128)(2,1)S(1)}, u32[]{:S(2)}, u32[]{:S(2)}) collective-permute-start(bf16[192,384]{1,0:T(8,128)(2,1)S(1)} %collective-permute-done.24.refs_6_), channel_id=1, source_target_pairs={{0,1},{1,2},{2,3},{3,4},{4,5},{5,6},{6,7},{7,0},{8,9},{9,10},{10,1... | collective-permute-start | bytes 442376 | tf_op jit(solution)/shard_map/ppermute | solution.py:21
  130.3 6.0 %collective-permute-start.22 = (bf16[96,384]{1,0:T(8,128)(2,1)S(1)}, bf16[96,384]{1,0:T(8,128)(2,1)S(1)}, u32[]{:S(2)}, u32[]{:S(2)}) collective-permute-start(bf16[96,384]{1,0:T(8,128)(2,1)S(1)} %slice.52), channel_id=1, source_target_pairs={{0,7},{1,0},{2,1},{3,2},{4,3},{5,4},{6,5},{7,6},{8,15},{9,8},{10,9... | collective-permute-start | bytes 221192 | tf_op jit(solution)/shard_map/ppermute | solution.py:21
  134.3 5.6 %collective-permute-start.26 = (bf16[96,384]{1,0:T(8,128)(2,1)S(1)}, bf16[96,384]{1,0:T(8,128)(2,1)S(1)}, u32[]{:S(2)}, u32[]{:S(2)}) collective-permute-start(bf16[96,384]{1,0:T(8,128)(2,1)S(1)} %slice.53), channel_id=1, source_target_pairs={{0,1},{1,2},{2,3},{3,4},{4,5},{5,6},{6,7},{7,0},{8,9},{9,10},{10,1... | collective-permute-start | bytes 221192 | tf_op jit(solution)/shard_map/ppermute | solution.py:21
  145.2 8.4 %copy-start.3 = (bf16[8,8,4224]{2,1,0:T(8,128)(2,1)S(1)}, bf16[8,8,4224]{2,1,0:T(8,128)(2,1)}, u32[]{:S(2)}) copy-start(bf16[8,8,4224]{2,1,0:T(8,128)(2,1)} %copy-done.2) | copy-start | bytes 1622020
  145.2 18.5 %all-to-all-start.2 = ((bf16[16,48,512]{2,1,0:T(8,128)(2,1)}), bf16[16,48,512]{2,1,0:T(8,128)(2,1)S(1)}, u32[]{:S(2)}, u32[]{:S(2)}) async-start(bf16[16,48,512]{2,1,0:T(8,128)(2,1)} %bitcast.16), calls=%async_computation.2 | async-start | bytes 1572864 | tf_op jit(solution)/shard_map/all_to_all | solution.py:428
  154.1 16.1 %copy-start.12 = (s32[64]{0:T(128)S(1)}, s32[64]{0:T(128)}, u32[]{:S(2)}) copy-start(s32[64]{0:T(128)} %param.23) | copy-start | bytes 772
  165.0 18.5 %all-to-all-start.3 = ((bf16[8,64,512]{2,1,0:T(8,128)(2,1)}), bf16[8,64,512]{2,1,0:T(8,128)(2,1)S(1)}, u32[]{:S(2)}, u32[]{:S(2)}) async-start(bf16[8,64,512]{2,1,0:T(8,128)(2,1)} %broadcast_in_dim.40), calls=%async_computation.3 | async-start | bytes 1048576 | tf_op jit(solution)/shard_map/all_to_all | solution.py:39
Sparse Core Ops, SparseCore 0:
  88.1 40.9 all-gather.2

commit v3 on v2

--- a/solution.py
+++ b/solution.py
@@ -133,40 +133,30 @@
 )
 
 
-def lower_kernel(place_ref, near_ref, own_ref, other_ref, *refs):
+def lower_kernel(place_ref, own_ref, other_ref, *refs):
     members, hidden, _ = own_ref.shape
-    rest_refs, refs = refs[:members], refs[members:]
-    out_ref, first_sum, second_sum, placed, near_held, own_held, other_held, sems = refs
+    active_refs, refs = refs[:members], refs[members:]
+    out_ref, first_sum, second_sum, placed, own_held, other_held, sems = refs
     sums = (first_sum, second_sum)
-    first = near_ref.shape[1]
+    pairs = ((own_ref, own_held), (other_ref, other_held))
     z = place_ref[2]
-
-    def copy(i, d):
-        source, target = ((near_ref, near_held), (own_ref, own_held), (other_ref, other_held))[i]
-        return pltpu.make_async_copy(source.at[d], target.at[d], sems.at[i, d])
-
+    moves = []
     for d in range(members):
-        for i in range(3):
-            copy(i, d).start()
+        at = (z + d) % members
+        moves.append(
+            [pltpu.make_async_copy(s.at[at], t.at[d], sems.at[i, d]) for i, (s, t) in enumerate(pairs)]
+        )
+        for move in moves[d]:
+            move.start()
     for d in range(members):
-        for i in range(3):
-            copy(i, d).wait()
         for j, held in enumerate((own_held, other_held)):
+            moves[d][j].wait()
             span = slice(j * hidden, (j + 1) * hidden)
-            part = jnp.dot(near_held[d][:, span], held[d], preferred_element_type=F32)
+            part = jnp.dot(active_refs[d][:, span], held[d], preferred_element_type=F32)
             if d == 0:
-                sums[j][:first, :] = part
+                sums[j][...] = part
             else:
-                sums[j][:first, :] += part
-    for j, held in enumerate((own_held, other_held)):
-        span = slice(j * hidden, (j + 1) * hidden)
-        for d in range(members):
-            at = (z + d) % members
-            part = jnp.dot(rest_refs[d][:, span], held[at], preferred_element_type=F32)
-            if d == 0:
-                sums[j][first:, :] = part
-            else:
-                sums[j][first:, :] += part
+                sums[j][...] += part
     x, y = place_ref[0], place_ref[1]
     per = placed.shape[2] // 2
     for p, (h, outer, inner) in enumerate(PIECES):
@@ -182,15 +172,15 @@
     out_ref[...] = placed[...].astype(BF)
 
 
-def lower(place, near, rest, down_own, down_other, chips):
+def lower(place, active, down_own, down_other, chips):
     members, hidden, cols = down_own.shape
-    near, down_own, down_other = in_hbm((near, down_own, down_other))
-    slots = near.shape[1] + rest[0].shape[0]
+    down_own, down_other = in_hbm((down_own, down_other))
+    slots = active[0].shape[0]
     per_chip = slots // chips
     return pl.pallas_call(
         lower_kernel,
         in_specs=[pl.BlockSpec(memory_space=pltpu.SMEM)]
-        + [pl.BlockSpec(memory_space=pl.ANY)] * 3
+        + [pl.BlockSpec(memory_space=pl.ANY)] * 2
         + [pl.BlockSpec(memory_space=pltpu.VMEM)] * members,
         out_specs=pl.BlockSpec(memory_space=pltpu.VMEM),
         out_shape=jax.ShapeDtypeStruct((chips, 2, per_chip, cols), BF),
@@ -198,10 +188,9 @@
             pltpu.VMEM((slots, cols), F32),
             pltpu.VMEM((slots, cols), F32),
             pltpu.VMEM((chips, 2, per_chip, cols), F32),
-            pltpu.VMEM(near.shape, BF),
             pltpu.VMEM(down_own.shape, BF),
             pltpu.VMEM(down_other.shape, BF),
-            pltpu.SemaphoreType.DMA((3, members)),
+            pltpu.SemaphoreType.DMA((2, members)),
         ],
         compiler_params=pltpu.CompilerParams(vmem_limit_bytes=24 << 20),
         cost_estimate=pl.CostEstimate(
@@ -210,7 +199,7 @@
             transcendentals=0,
         ),
         name="lower",
-    )(place, near, down_own, down_other, *rest)
+    )(place, down_own, down_other, *active)
 
 
 def attend_kernel(
@@ -226,7 +215,8 @@
     ]
     for move in (*query_moves, *moves):
         move.start()
-    members, rows, cols = stream_ref.shape
+    for ref in (spread, own, fresh):
+        ref[...] = jnp.zeros(ref.shape, F32)
     heads, size = out_ref.shape[1] // keys_ref.shape[2], keys_ref.shape[2]
     width = members * cols
     total = jnp.zeros((rows, 1), F32)
@@ -260,11 +250,6 @@
         mine = jnp.sum(query * key_new, axis=1, keepdims=True) * factor
         own[:, h, :] = jnp.broadcast_to(mine, (rows, size))
         fresh[:, h, :] = value_new
-    for h in range(heads, pad):
-        for i in range(3):
-            spread[:, pad * i + h, :] = jnp.zeros((rows, size), F32)
-        own[:, h, :] = jnp.zeros((rows, size), F32)
-        fresh[:, h, :] = jnp.zeros((rows, size), F32)
 
     def parts_dot(parts, cached, dim):
         result = lax.dot_general(
@@ -339,15 +324,55 @@
     return high, middle, (rest - middle.astype(F32)).astype(BF)
 
 
-def routing_columns(expert_ids, combine, experts):
-    named = expert_ids[:, :, None] == jnp.arange(experts, dtype=jnp.int32)
-    chosen = jnp.any(named, axis=1)
-    weight = jnp.sum(jnp.where(named, combine[:, :, None], 0.0), axis=1)
-    rows = jnp.arange(expert_ids.shape[0])
-    earlier = rows[None, :, None] < rows[:, None, None]
-    rank = jnp.sum((earlier & chosen[None]).astype(jnp.int32), axis=1)
-    rank = jnp.where(chosen, rank, CAP).astype(BF)
-    return jnp.concatenate([rank, *split3(weight)], axis=1)
+def prepare_kernel(*refs):
+    sources, out_ref, held, sems = refs[:3], refs[3], refs[4:7], refs[7]
+    moves = [pltpu.make_async_copy(s, t, sems.at[i]) for i, (s, t) in enumerate(zip(sources, held))]
+    for move in moves:
+        move.start()
+    for move in moves:
+        move.wait()
+    tokens_ref, ids_ref, combine_ref = held
+    rows, width = tokens_ref.shape
+    experts = LANES // 4
+    lane = lax.broadcasted_iota(jnp.int32, (rows, LANES), 1)
+    expert = lane % experts
+    chosen = jnp.zeros((rows, LANES), F32)
+    weight = jnp.zeros((rows, LANES), F32)
+    for k in range(ids_ref.shape[1]):
+        named = ids_ref[:, k : k + 1] == expert
+        chosen = jnp.where(named, 1.0, chosen)
+        weight = jnp.where(named, combine_ref[:, k : k + 1], weight)
+    row = lax.broadcasted_iota(jnp.int32, (rows, LANES), 0)
+    rank = jnp.zeros((rows, LANES), F32)
+    for r in range(rows - 1):
+        rank += jnp.where(row > r, chosen[r : r + 1, :], 0.0)
+    rank = jnp.where(chosen > 0.0, rank, float(CAP))
+    terms = [part.astype(F32) for part in split3(weight)]
+    columns = rank
+    for i, term in enumerate(terms):
+        columns = jnp.where(lane >= (i + 1) * experts, term, columns)
+    for i in range(out_ref.shape[0]):
+        out_ref[i, :, :width] = tokens_ref[...]
+        out_ref[i, :, width:] = columns.astype(BF)
+
+
+def prepare(tokens, expert_ids, combine, members):
+    rows, width = tokens.shape
+    return pl.pallas_call(
+        prepare_kernel,
+        in_specs=[pl.BlockSpec(memory_space=pl.ANY)] * 3,
+        out_specs=pl.BlockSpec(memory_space=pltpu.VMEM),
+        out_shape=jax.ShapeDtypeStruct((members, rows, width + LANES), BF),
+        scratch_shapes=[
+            *(pltpu.VMEM(a.shape, a.dtype) for a in (tokens, expert_ids, combine)),
+            pltpu.SemaphoreType.DMA((3,)),
+        ],
+        compiler_params=pltpu.CompilerParams(vmem_limit_bytes=4 << 20),
+        cost_estimate=pl.CostEstimate(
+            flops=0, bytes_accessed=2 * members * rows * width, transcendentals=0
+        ),
+        name="prepare",
+    )(*in_hbm((tokens, expert_ids, combine)))
 
 
 def per_device(
@@ -373,10 +398,10 @@
     hidden = w_gate.shape[2]
     cols = width // members
 
-    sent = jnp.concatenate([tokens, routing_columns(expert_ids, combine, experts)], axis=1)
+    sent = prepare(tokens, expert_ids, combine, members)
     own = [w_gate[0].T, w_up[0].T]
     arrived, down, *other = lax.optimization_barrier(
-        (copies(sent, "z"), w_down[0], *(shift(w, "c", 1) for w in own))
+        (lax.all_to_all(sent, "z", 0, 0, tiled=True), w_down[0], *(shift(w, "c", 1) for w in own))
     )
     weights = own + other
     down_own = lax.all_to_all(down, "z", 1, 0, tiled=True).reshape(members, hidden, cols)
@@ -416,13 +441,12 @@
         shift(b_near_sides[1], "x", -1),
         shift(far[2], "x", 1),
     )
-    near_active = lax.all_gather(slots, "z", axis=0)
     more, down_own = lax.optimization_barrier((expert_slots(far, masks, weights), down_own))
     down_other = shift(down_own, "c", 1)
-    rest = jnp.concatenate([more, expert_slots(opposite, masks, weights)], axis=0)
-    active = (near_active, ring(rest, "z"))
+    slots = jnp.concatenate([slots, more, expert_slots(opposite, masks, weights)], axis=0)
+    active = ring(slots, "z")
     place = jnp.stack([x, y, z]).astype(jnp.int32)
-    result = lower(place, *active, down_own, down_other, chips)
+    result = lower(place, active, down_own, down_other, chips)
     per_chip = result.shape[2]
     result = result.reshape(chips, 2 * per_chip, cols)
     returned = lax.all_to_all(result, ("x", "y"), 0, 0, tiled=True)

time: 199 us -> 184 us (0.925)
  between operations: 14.4 us -> 1.16 us
  waiting for transfers between devices: 57.5 us -> 64.2 us
  other arithmetic: 5.32 us -> 0.98 us
  starting transfers between devices: 55.9 us -> 53 us
    ppermute x23, waiting for transfers between devices: 27.3 us -> 33.3 us  [shift(): lax.ppermute(values, axis, [(i, (i - step) % size) for i in range(size)])]
  transfers between devices with their start and end apart: 31 -> 30, of which waited for: 15 -> 13; matrix products, arithmetic and copies ran while one was open for 3% -> 1% of each run, Pallas kernels for 10% -> 11%
where the time goes in v3:
time: 184 us; the launch traced here: 183 us
  waiting for transfers between devices  64.2 us (35%)
  starting transfers between devices  53 us (29%)
  Pallas kernels  33.4 us (18%)
  blocking collectives  26.4 us (14%)
  local copies, waits for them, and re-layouts  3.48 us (2%)
    ppermute x23, waiting for transfers between devices, shift(): lax.ppermute(values, axis, [(i, (i - step) % size) for i in range(size)])  33.3 us
    ppermute x23, starting transfers between devices, shift(): lax.ppermute(values, axis, [(i, (i - step) % size) for i in range(size)])  30.4 us
    all_to_all x1, blocking collectives, per_device(): lax.all_to_all(sent, 'z', 0, 0, tiled=True)  26.4 us
    pallas_call x3, Pallas kernels, expert_slots(): pl.pallas_call(functools.partial(expert_kernel, sizes, steps), grid=(step...  19.7 us
    all_to_all x1, waiting for transfers between devices, copies(): lax.all_to_all(jnp.broadcast_to(values[None], (size, *values.shape)), axi...  13.3 us
    all_to_all x1, waiting for transfers between devices, per_device(): returned = lax.all_to_all(result, ('x', 'y'), 0, 0, tiled=True)  9.59 us
    ppermute x4, waiting for transfers between devices, pairs(): return lax.ppermute(block, axis, [(i, i ^ mask) for i in range(4)])  8.07 us
    pallas_call x1, Pallas kernels, attend(): pl.pallas_call(attend_kernel, in_specs=[pl.BlockSpec(memory_space=pltpu.S...  7.29 us
  transfers between devices with their start and end apart: 30, of which 13 were waited for; matrix products, arithmetic and copies ran while one was open for 1% of the time, Pallas kernels for 11%

profile of v3, /device:TPU:8, one launch (start us, length us, event | category | flops | bytes accessed | tf_op | source)
XLA Modules:
  0.0 183.1 jit_solution(3720712371270324041)
XLA Ops:
  0.7 0.5 collective-permute-start.1
  1.2 1.0 prepare.1
  2.2 26.4 %all_to_all.31 = bf16[8,8,4224]{2,1,0:T(8,128)(2,1)S(1)} all-to-all(bf16[8,8,4224]{2,1,0:T(8,128)(2,1)S(1)} %prepare.1), channel_id=1, replica_groups=mesh['x'=4,'y'=4,'c'=2,'z'=8] {'z'}, dimensions={0} | all-to-all | bytes 1081344 | tf_op jit(solution)/shard_map/all_to_all | solution.py:404
  28.6 0.2 fusion.1
  29.0 0.5 collective-permute-start.4
  29.6 1.5 collective-permute-start.2
  31.1 1.3 copy.22
  32.4 4.3 %all-to-all-start.1 = ((bf16[192,8,512]{2,0,1:T(8,128)(2,1)}), bf16[192,8,512]{2,0,1:T(8,128)(2,1)}, u32[]{:S(2)}, u32[]{:S(2)}) async-start(bf16[192,8,512]{2,0,1:T(8,128)(2,1)} %bitcast.24), calls=%async_computation.1 | async-start | bytes 3145728 | tf_op jit(solution)/shard_map/all_to_all | solution.py:407
  36.8 2.5 %collective-permute-start.5 = (bf16[64,4224]{1,0:T(8,128)(2,1)S(1)}, bf16[64,4224]{1,0:T(8,128)(2,1)S(1)}, u32[]{:S(2)}, u32[]{:S(2)}) collective-permute-start(bf16[64,4224]{1,0:T(8,128)(2,1)S(1)} %pad_maximum_fusion.1.refs_2_.refs_10_), channel_id=1, source_target_pairs={{0,48},{16,32},{32,16},{48,0},{1,49},{17,33},{33,17},{49,1},{2,50}... | collective-permute-start | bytes 1622024 | tf_op jit(solution)/shard_map/ppermute | solution.py:424
  39.3 2.2 %collective-permute-start.3 = (bf16[64,4224]{1,0:T(8,128)(2,1)S(1)}, bf16[64,4224]{1,0:T(8,128)(2,1)}, u32[]{:S(2)}, u32[]{:S(2)}) collective-permute-start(bf16[64,4224]{1,0:T(8,128)(2,1)S(1)} %pad_maximum_fusion.refs_0_.refs_8_), channel_id=1, source_target_pairs={{0,192},{64,128},{128,64},{192,0},{1,193},{65,129},{129,65},{193,1... | collective-permute-start | bytes 1622024 | tf_op jit(solution)/shard_map/ppermute | solution.py:424
  41.5 0.6 collective-permute-start.9
  42.1 2.9 %collective-permute-start.8 = (bf16[64,4224]{1,0:T(8,128)(2,1)S(1)}, bf16[64,4224]{1,0:T(8,128)(2,1)}, u32[]{:S(2)}, u32[]{:S(2)}) collective-permute-start(bf16[64,4224]{1,0:T(8,128)(2,1)S(1)} %pad_maximum_fusion.1.refs_2_.refs_10_), channel_id=1, source_target_pairs={{0,192},{64,0},{128,64},{192,128},{1,193},{65,1},{129,65},{193,129... | collective-permute-start | bytes 1622024 | tf_op jit(solution)/shard_map/ppermute | solution.py:21
  45.0 7.0 %collective-permute-done.5.refs_3_.refs_11_ = bf16[64,4224]{1,0:T(8,128)(2,1)S(1)} collective-permute-done((bf16[64,4224]{1,0:T(8,128)(2,1)S(1)}, bf16[64,4224]{1,0:T(8,128)(2,1)S(1)}, u32[]{:S(2)}, u32[]{:S(2)}) %collective-permute-start.5) | collective-permute-done | bytes 540704 | tf_op jit(solution)/shard_map/ppermute | solution.py:424
  52.0 2.9 %collective-permute-start.6 = (bf16[64,4224]{1,0:T(8,128)(2,1)S(1)}, bf16[64,4224]{1,0:T(8,128)(2,1)}, u32[]{:S(2)}, u32[]{:S(2)}) collective-permute-start(bf16[64,4224]{1,0:T(8,128)(2,1)S(1)} %pad_maximum_fusion.refs_0_.refs_8_), channel_id=1, source_target_pairs={{0,48},{16,0},{32,16},{48,32},{1,49},{17,1},{33,17},{49,33},{2,50}... | collective-permute-start | bytes 1622024 | tf_op jit(solution)/shard_map/ppermute | solution.py:21
  54.9 1.1 collective-permute-done.3.refs_1_.refs_9_
  55.9 2.1 %collective-permute-start.12 = (bf16[64,4224]{1,0:T(8,128)(2,1)S(1)}, bf16[64,4224]{1,0:T(8,128)(2,1)}, u32[]{:S(2)}, u32[]{:S(2)}) collective-permute-start(bf16[64,4224]{1,0:T(8,128)(2,1)S(1)} %collective-permute-done.5.refs_3_.refs_11_), channel_id=1, source_target_pairs={{0,192},{64,0},{128,64},{192,128},{1,193},{65,1},{129,65},{193,129... | collective-permute-start | bytes 1622024 | tf_op jit(solution)/shard_map/ppermute | solution.py:21
  58.0 6.3 %collective-permute-done.9.refs_7_.refs_15_ = bf16[64,4224]{1,0:T(8,128)(2,1)S(1)} collective-permute-done((bf16[64,4224]{1,0:T(8,128)(2,1)S(1)}, bf16[64,4224]{1,0:T(8,128)(2,1)S(1)}, u32[]{:S(2)}, u32[]{:S(2)}) %collective-permute-start.9) | collective-permute-done | bytes 540704 | tf_op jit(solution)/shard_map/ppermute | solution.py:21
  64.4 1.4 collective-permute-start.10
  65.8 0.6 collective-permute-start.11
  66.5 1.8 %collective-permute-start.17 = (bf16[64,4224]{1,0:T(8,128)(2,1)S(1)}, bf16[64,4224]{1,0:T(8,128)(2,1)}, u32[]{:S(2)}, u32[]{:S(2)}) collective-permute-start(bf16[64,4224]{1,0:T(8,128)(2,1)S(1)} %collective-permute-done.9.refs_7_.refs_15_), channel_id=1, source_target_pairs={{0,64},{64,128},{128,192},{192,0},{1,65},{65,129},{129,193},{193,1... | collective-permute-start | bytes 1622024 | tf_op jit(solution)/shard_map/ppermute | solution.py:21
  68.4 7.9 %expert_slots.3 = bf16[192,384]{1,0:T(8,128)(2,1)S(1)} custom-call(bf16[8,128]{1,0:T(8,128)(2,1)S(1)} %convert_convert_fusion.mask_ref, bf16[64,4224]{1,0:T(8,128)(2,1)} %copy-done.2, bf16[64,4224]{1,0:T(8,128)(2,1)} %collective-permute-done.3.refs_1_.refs_9_, bf16[64,4224]{1,0:T(8,128)(2,1)} %copy-done.1, bf16[64,4224]{1,0:T(8,128)(2,1)} %copy-done.5, ...), custom_call_target="tpu_custom_call" | custom-call | flops 3221225472 | bytes 10485760 | tf_op jit(solution)/shard_map/expert_slots/pallas_call | solution.py:108
  76.3 0.8 collective-permute-start.15
  77.1 3.8 %collective-permute-done.13.refs_3_.refs_7_ = bf16[64,4224]{1,0:T(8,128)(2,1)} collective-permute-done((bf16[64,4224]{1,0:T(8,128)(2,1)S(1)}, bf16[64,4224]{1,0:T(8,128)(2,1)}, u32[]{:S(2)}, u32[]{:S(2)}) %collective-permute-start.13) | collective-permute-done | bytes 540704 | tf_op jit(solution)/shard_map/ppermute | solution.py:21
  80.9 1.4 collective-permute-start.16
  82.2 0.8 collective-permute-start.18
  83.0 5.9 %expert_slots.4 = bf16[96,384]{1,0:T(8,128)(2,1)S(1)} custom-call(bf16[8,128]{1,0:T(8,128)(2,1)S(1)} %convert_convert_fusion.mask_ref, bf16[64,4224]{1,0:T(8,128)(2,1)} %collective-permute-done.10.refs_0_.refs_4_, bf16[64,4224]{1,0:T(8,128)(2,1)} %collective-permute-done.11.refs_1_.refs_5_, bf16[64,4224]{1,0:T(8,128)(2,1)} %collective-permute-done.12.refs_2_.refs_6_, ...), custom_call_target="tpu_custom_call" | custom-call | flops 1610612736 | bytes 8388608 | tf_op jit(solution)/shard_map/expert_slots/pallas_call | solution.py:108
  89.1 1.4 collective-permute-done.16.refs_1_.refs_5_
  90.5 1.3 collective-permute-done.18.refs_3_.refs_7_
  91.8 0.8 copy-done.8
  92.6 5.9 %expert_slots.5 = bf16[96,384]{1,0:T(8,128)(2,1)S(1)} custom-call(bf16[8,128]{1,0:T(8,128)(2,1)S(1)} %convert_convert_fusion.mask_ref, bf16[64,4224]{1,0:T(8,128)(2,1)} %copy-done.6, bf16[64,4224]{1,0:T(8,128)(2,1)} %copy-done.7, bf16[64,4224]{1,0:T(8,128)(2,1)} %collective-permute-done.17.refs_2_.refs_6_, bf16[64,4224]{1,0:T(8,128)(2,1)} %copy-done.8, ...), custom_call_target="tpu_custom_call" | custom-call | flops 1610612736 | bytes 8388608 | tf_op jit(solution)/shard_map/expert_slots/pallas_call | solution.py:108
  98.5 2.9 %collective-permute-start.19 = (bf16[384,384]{1,0:T(8,128)(2,1)S(1)}, bf16[384,384]{1,0:T(8,128)(2,1)S(1)}, u32[]{:S(2)}, u32[]{:S(2)}) collective-permute-start(bf16[384,384]{1,0:T(8,128)(2,1)S(1)} %pad_maximum_fusion.2.refs_0_), channel_id=1, source_target_pairs={{0,7},{1,0},{2,1},{3,2},{4,3},{5,4},{6,5},{7,6},{8,15},{9,8},{10,9... | collective-permute-start | bytes 884744 | tf_op jit(solution)/shard_map/ppermute | solution.py:21
  101.5 5.2 %collective-permute-done.19.refs_1_ = bf16[384,384]{1,0:T(8,128)(2,1)S(1)} collective-permute-done((bf16[384,384]{1,0:T(8,128)(2,1)S(1)}, bf16[384,384]{1,0:T(8,128)(2,1)S(1)}, u32[]{:S(2)}, u32[]{:S(2)}) %collective-permute-start.19) | collective-permute-done | bytes 294944 | tf_op jit(solution)/shard_map/ppermute | solution.py:21
  106.7 3.7 %collective-permute-start.20 = (bf16[384,384]{1,0:T(8,128)(2,1)S(1)}, bf16[384,384]{1,0:T(8,128)(2,1)S(1)}, u32[]{:S(2)}, u32[]{:S(2)}) collective-permute-start(bf16[384,384]{1,0:T(8,128)(2,1)S(1)} %collective-permute-done.19.refs_1_), channel_id=1, source_target_pairs={{0,7},{1,0},{2,1},{3,2},{4,3},{5,4},{6,5},{7,6},{8,15},{9,8},{10,9... | collective-permute-start | bytes 884744 | tf_op jit(solution)/shard_map/ppermute | solution.py:21
  110.4 4.3 %collective-permute-done.20.refs_2_ = bf16[384,384]{1,0:T(8,128)(2,1)S(1)} collective-permute-done((bf16[384,384]{1,0:T(8,128)(2,1)S(1)}, bf16[384,384]{1,0:T(8,128)(2,1)S(1)}, u32[]{:S(2)}, u32[]{:S(2)}) %collective-permute-start.20) | collective-permute-done | bytes 294944 | tf_op jit(solution)/shard_map/ppermute | solution.py:21
  114.7 3.7 %collective-permute-start.21 = (bf16[384,384]{1,0:T(8,128)(2,1)S(1)}, bf16[384,384]{1,0:T(8,128)(2,1)S(1)}, u32[]{:S(2)}, u32[]{:S(2)}) collective-permute-start(bf16[384,384]{1,0:T(8,128)(2,1)S(1)} %collective-permute-done.20.refs_2_), channel_id=1, source_target_pairs={{0,7},{1,0},{2,1},{3,2},{4,3},{5,4},{6,5},{7,6},{8,15},{9,8},{10,9... | collective-permute-start | bytes 884744 | tf_op jit(solution)/shard_map/ppermute | solution.py:21
  118.4 4.7 %collective-permute-done.21.refs_3_ = bf16[384,384]{1,0:T(8,128)(2,1)S(1)} collective-permute-done((bf16[384,384]{1,0:T(8,128)(2,1)S(1)}, bf16[384,384]{1,0:T(8,128)(2,1)S(1)}, u32[]{:S(2)}, u32[]{:S(2)}) %collective-permute-start.21) | collective-permute-done | bytes 294944 | tf_op jit(solution)/shard_map/ppermute | solution.py:21
  123.1 3.8 %collective-permute-start.22 = (bf16[192,384]{1,0:T(8,128)(2,1)S(1)}, bf16[192,384]{1,0:T(8,128)(2,1)S(1)}, u32[]{:S(2)}, u32[]{:S(2)}) collective-permute-start(bf16[192,384]{1,0:T(8,128)(2,1)S(1)} %slice.52), channel_id=1, source_target_pairs={{0,7},{1,0},{2,1},{3,2},{4,3},{5,4},{6,5},{7,6},{8,15},{9,8},{10,9... | collective-permute-start | bytes 442376 | tf_op jit(solution)/shard_map/ppermute | solution.py:21
  126.9 0.3 collective-permute-start.26
  127.3 2.2 %collective-permute-done.22 = bf16[192,384]{1,0:T(8,128)(2,1)S(1)} collective-permute-done((bf16[192,384]{1,0:T(8,128)(2,1)S(1)}, bf16[192,384]{1,0:T(8,128)(2,1)S(1)}, u32[]{:S(2)}, u32[]{:S(2)}) %collective-permute-start.22) | collective-permute-done | bytes 147488 | tf_op jit(solution)/shard_map/ppermute | solution.py:21
  129.6 4.0 %collective-permute-done.26 = bf16[192,384]{1,0:T(8,128)(2,1)S(1)} collective-permute-done((bf16[192,384]{1,0:T(8,128)(2,1)S(1)}, bf16[192,384]{1,0:T(8,128)(2,1)S(1)}, u32[]{:S(2)}, u32[]{:S(2)}) %collective-permute-start.26) | collective-permute-done | bytes 147488 | tf_op jit(solution)/shard_map/ppermute | solution.py:21
  133.6 5.5 %lower.1 = bf16[16,2,24,512]{3,2,1,0:T(8,128)(2,1)} custom-call(s32[3]{0:T(128)S(1)} %pad_add_fusion.place_ref, bf16[8,192,512]{2,1,0:T(8,128)(2,1)} %bitcast.14.own_ref, bf16[8,192,512]{2,1,0:T(8,128)(2,1)} %collective-permute-done.14.other_ref, bf16[384,384]{1,0:T(8,128)(2,1)S(1)} %pad_maximum_fusion.2.refs_0_, ...), custom_call_target="tpu_custom_call" | custom-call | flops 1207959552 | bytes 5505024 | tf_op jit(solution)/shard_map/lower/pallas_call | solution.py:180
  139.1 7.1 %all-to-all-start.2 = ((bf16[16,48,512]{2,1,0:T(8,128)(2,1)}), bf16[16,48,512]{2,1,0:T(8,128)(2,1)S(1)}, u32[]{:S(2)}, u32[]{:S(2)}) async-start(bf16[16,48,512]{2,1,0:T(8,128)(2,1)} %bitcast.15), calls=%async_computation.2 | async-start | bytes 1572864 | tf_op jit(solution)/shard_map/all_to_all | solution.py:452
  146.8 9.6 %all-to-all-done.2 = bf16[16,48,512]{2,1,0:T(8,128)(2,1)S(1)} async-done(((bf16[16,48,512]{2,1,0:T(8,128)(2,1)}), bf16[16,48,512]{2,1,0:T(8,128)(2,1)S(1)}, u32[]{:S(2)}, u32[]{:S(2)}) %all-to-all-start.2) | async-done | bytes 786464 | tf_op jit(solution)/shard_map/all_to_all | solution.py:452
  156.4 0.5 fusion
  156.9 0.8 broadcast_in_dim.18
  157.8 4.5 %all-to-all-start.3 = ((bf16[8,64,512]{2,1,0:T(8,128)(2,1)}), bf16[8,64,512]{2,1,0:T(8,128)(2,1)S(1)}, u32[]{:S(2)}, u32[]{:S(2)}) async-start(bf16[8,64,512]{2,1,0:T(8,128)(2,1)} %broadcast_in_dim.18), calls=%async_computation.3 | async-start | bytes 1048576 | tf_op jit(solution)/shard_map/all_to_all | solution.py:39
  162.3 13.3 %all-to-all-done.3.stream_ref = bf16[8,64,512]{2,1,0:T(8,128)(2,1)S(1)} async-done(((bf16[8,64,512]{2,1,0:T(8,128)(2,1)}), bf16[8,64,512]{2,1,0:T(8,128)(2,1)S(1)}, u32[]{:S(2)}, u32[]{:S(2)}) %all-to-all-start.3) | async-done | bytes 524320 | tf_op jit(solution)/shard_map/all_to_all | solution.py:39
  175.7 7.3 %attend.1 = (bf16[8,4096]{1,0:T(8,128)(2,1)}, bf16[64,512]{1,0:T(8,128)(2,1)}) custom-call(s32[3]{0:T(128)S(1)} %pad_add_fusion.place_ref, bf16[8,64,512]{2,1,0:T(8,128)(2,1)S(1)} %all-to-all-done.3.stream_ref, bf16[4096,512]{1,0:T(8,128)(2,1)} %wq_ref.1, bf16[4096,128]{1,0:T(8,128)(2,1)} %wk_ref.1, bf16[4096,128]{1,0:T(8,128)(2,1)} %wv_ref.1, ...), custom_call_target="tpu_custom_call" | custom-call | flops 402653184 | bytes 6291456 | tf_op jit(solution)/shard_map/attend/pallas_call | solution.py:285
  (75 shorter events, 1.6 us)
Async XLA Ops:
  0.6 28.0 %collective-permute-start = (bf16[192,4096]{1,0:T(8,128)(2,1)}, bf16[192,4096]{1,0:T(8,128)(2,1)S(1)}, u32[]{:S(2)}, u32[]{:S(2)}) collective-permute-start(bf16[192,4096]{1,0:T(8,128)(2,1)} %bitcast.31), channel_id=1, source_target_pairs={{0,8},{8,0},{1,9},{9,1},{2,10},{10,2},{3,11},{11,3},{4,12},{12,4},... | collective-permute-start | bytes 4718600 | tf_op jit(solution)/shard_map/ppermute | solution.py:21
  0.7 27.9 %collective-permute-start.1 = (bf16[192,4096]{1,0:T(8,128)(2,1)}, bf16[192,4096]{1,0:T(8,128)(2,1)}, u32[]{:S(2)}, u32[]{:S(2)}) collective-permute-start(bf16[192,4096]{1,0:T(8,128)(2,1)} %bitcast.35), channel_id=1, source_target_pairs={{0,8},{8,0},{1,9},{9,1},{2,10},{10,2},{3,11},{11,3},{4,12},{12,4},... | collective-permute-start | bytes 4718600 | tf_op jit(solution)/shard_map/ppermute | solution.py:21
  28.6 2.5 %copy-start.9 = (bf16[1,192,4096]{2,1,0:T(8,128)(2,1)S(1)}, bf16[1,192,4096]{2,1,0:T(8,128)(2,1)}, u32[]{:S(2)}) copy-start(bf16[1,192,4096]{2,1,0:T(8,128)(2,1)} %param.17) | copy-start | bytes 4718596
  28.6 3.8 %copy-start = (bf16[192,4096]{1,0:T(8,128)(2,1)}, bf16[192,4096]{1,0:T(8,128)(2,1)S(1)}, u32[]{:S(2)}) copy-start(bf16[192,4096]{1,0:T(8,128)(2,1)S(1)} %collective-permute-done.refs_18_.refs_10_) | copy-start | bytes 4718596
  29.0 7.7 %collective-permute-start.4 = (bf16[32,4224]{1,0:T(8,128)(2,1)S(1)}, bf16[32,4224]{1,0:T(8,128)(2,1)S(1)}, u32[]{:S(2)}, u32[]{:S(2)}) collective-permute-start(bf16[32,4224]{1,0:T(8,128)(2,1)S(1)} %get-tuple-element.24), channel_id=1, source_target_pairs={{0,16},{16,0},{32,48},{48,32},{1,17},{17,1},{33,49},{49,33},{2,18}... | collective-permute-start | bytes 811016 | tf_op jit(solution)/shard_map/ppermute | solution.py:424
  29.6 9.7 %collective-permute-start.2 = (bf16[32,4224]{1,0:T(8,128)(2,1)S(1)}, bf16[32,4224]{1,0:T(8,128)(2,1)S(1)}, u32[]{:S(2)}, u32[]{:S(2)}) collective-permute-start(bf16[32,4224]{1,0:T(8,128)(2,1)S(1)} %get-tuple-element.25), channel_id=1, source_target_pairs={{0,64},{64,0},{128,192},{192,128},{1,65},{65,1},{129,193},{193,129... | collective-permute-start | bytes 811016 | tf_op jit(solution)/shard_map/ppermute | solution.py:424
  32.4 56.5 %all-to-all-start.1 = ((bf16[192,8,512]{2,0,1:T(8,128)(2,1)}), bf16[192,8,512]{2,0,1:T(8,128)(2,1)}, u32[]{:S(2)}, u32[]{:S(2)}) async-start(bf16[192,8,512]{2,0,1:T(8,128)(2,1)} %bitcast.24), calls=%async_computation.1 | async-start | bytes 3145728 | tf_op jit(solution)/shard_map/all_to_all | solution.py:407
  36.8 31.6 %copy-start.1 = (bf16[64,4224]{1,0:T(8,128)(2,1)}, bf16[64,4224]{1,0:T(8,128)(2,1)S(1)}, u32[]{:S(2)}) copy-start(bf16[64,4224]{1,0:T(8,128)(2,1)S(1)} %pad_maximum_fusion.1.refs_2_.refs_10_) | copy-start | bytes 1622020
  36.8 15.2 %collective-permute-start.5 = (bf16[64,4224]{1,0:T(8,128)(2,1)S(1)}, bf16[64,4224]{1,0:T(8,128)(2,1)S(1)}, u32[]{:S(2)}, u32[]{:S(2)}) collective-permute-start(bf16[64,4224]{1,0:T(8,128)(2,1)S(1)} %pad_maximum_fusion.1.refs_2_.refs_10_), channel_id=1, source_target_pairs={{0,48},{16,32},{32,16},{48,0},{1,49},{17,33},{33,17},{49,1},{2,50}... | collective-permute-start | bytes 1622024 | tf_op jit(solution)/shard_map/ppermute | solution.py:424
  39.3 29.1 %copy-start.2 = (bf16[64,4224]{1,0:T(8,128)(2,1)}, bf16[64,4224]{1,0:T(8,128)(2,1)S(1)}, u32[]{:S(2)}) copy-start(bf16[64,4224]{1,0:T(8,128)(2,1)S(1)} %pad_maximum_fusion.refs_0_.refs_8_) | copy-start | bytes 1622020
  39.3 16.6 %collective-permute-start.3 = (bf16[64,4224]{1,0:T(8,128)(2,1)S(1)}, bf16[64,4224]{1,0:T(8,128)(2,1)}, u32[]{:S(2)}, u32[]{:S(2)}) collective-permute-start(bf16[64,4224]{1,0:T(8,128)(2,1)S(1)} %pad_maximum_fusion.refs_0_.refs_8_), channel_id=1, source_target_pairs={{0,192},{64,128},{128,64},{192,0},{1,193},{65,129},{129,65},{193,1... | collective-permute-start | bytes 1622024 | tf_op jit(solution)/shard_map/ppermute | solution.py:424
  41.5 22.8 %collective-permute-start.9 = (bf16[64,4224]{1,0:T(8,128)(2,1)S(1)}, bf16[64,4224]{1,0:T(8,128)(2,1)S(1)}, u32[]{:S(2)}, u32[]{:S(2)}) collective-permute-start(bf16[64,4224]{1,0:T(8,128)(2,1)S(1)} %pad_maximum_fusion.1.refs_2_.refs_10_), channel_id=1, source_target_pairs={{0,64},{64,128},{128,192},{192,0},{1,65},{65,129},{129,193},{193,1... | collective-permute-start | bytes 1622024 | tf_op jit(solution)/shard_map/ppermute | solution.py:21
  42.1 22.3 %collective-permute-start.7 = (bf16[64,4224]{1,0:T(8,128)(2,1)S(1)}, bf16[64,4224]{1,0:T(8,128)(2,1)S(1)}, u32[]{:S(2)}, u32[]{:S(2)}) collective-permute-start(bf16[64,4224]{1,0:T(8,128)(2,1)S(1)} %pad_maximum_fusion.refs_0_.refs_8_), channel_id=1, source_target_pairs={{0,16},{16,32},{32,48},{48,0},{1,17},{17,33},{33,49},{49,1},{2,18}... | collective-permute-start | bytes 1622024 | tf_op jit(solution)/shard_map/ppermute | solution.py:21
  42.1 23.7 %collective-permute-start.8 = (bf16[64,4224]{1,0:T(8,128)(2,1)S(1)}, bf16[64,4224]{1,0:T(8,128)(2,1)}, u32[]{:S(2)}, u32[]{:S(2)}) collective-permute-start(bf16[64,4224]{1,0:T(8,128)(2,1)S(1)} %pad_maximum_fusion.1.refs_2_.refs_10_), channel_id=1, source_target_pairs={{0,192},{64,0},{128,64},{192,128},{1,193},{65,1},{129,65},{193,129... | collective-permute-start | bytes 1622024 | tf_op jit(solution)/shard_map/ppermute | solution.py:21
  52.0 16.4 %copy-start.5 = (bf16[64,4224]{1,0:T(8,128)(2,1)}, bf16[64,4224]{1,0:T(8,128)(2,1)S(1)}, u32[]{:S(2)}) copy-start(bf16[64,4224]{1,0:T(8,128)(2,1)S(1)} %collective-permute-done.5.refs_3_.refs_11_) | copy-start | bytes 1622020
  52.0 14.5 %collective-permute-start.6 = (bf16[64,4224]{1,0:T(8,128)(2,1)S(1)}, bf16[64,4224]{1,0:T(8,128)(2,1)}, u32[]{:S(2)}, u32[]{:S(2)}) collective-permute-start(bf16[64,4224]{1,0:T(8,128)(2,1)S(1)} %pad_maximum_fusion.refs_0_.refs_8_), channel_id=1, source_target_pairs={{0,48},{16,0},{32,16},{48,32},{1,49},{17,1},{33,17},{49,33},{2,50}... | collective-permute-start | bytes 1622024 | tf_op jit(solution)/shard_map/ppermute | solution.py:21
  55.9 20.4 %collective-permute-start.12 = (bf16[64,4224]{1,0:T(8,128)(2,1)S(1)}, bf16[64,4224]{1,0:T(8,128)(2,1)}, u32[]{:S(2)}, u32[]{:S(2)}) collective-permute-start(bf16[64,4224]{1,0:T(8,128)(2,1)S(1)} %collective-permute-done.5.refs_3_.refs_11_), channel_id=1, source_target_pairs={{0,192},{64,0},{128,64},{192,128},{1,193},{65,1},{129,65},{193,129... | collective-permute-start | bytes 1622024 | tf_op jit(solution)/shard_map/ppermute | solution.py:21
  64.4 4.0 %copy-start.3 = (bf16[64,4224]{1,0:T(8,128)(2,1)}, bf16[64,4224]{1,0:T(8,128)(2,1)S(1)}, u32[]{:S(2)}) copy-start(bf16[64,4224]{1,0:T(8,128)(2,1)S(1)} %collective-permute-done.9.refs_7_.refs_15_) | copy-start | bytes 1622020
  64.4 16.5 %collective-permute-start.13 = (bf16[64,4224]{1,0:T(8,128)(2,1)S(1)}, bf16[64,4224]{1,0:T(8,128)(2,1)}, u32[]{:S(2)}, u32[]{:S(2)}) collective-permute-start(bf16[64,4224]{1,0:T(8,128)(2,1)S(1)} %collective-permute-done.5.refs_3_.refs_11_), channel_id=1, source_target_pairs={{0,64},{64,128},{128,192},{192,0},{1,65},{65,129},{129,193},{193,1... | collective-permute-start | bytes 1622024 | tf_op jit(solution)/shard_map/ppermute | solution.py:21
  64.4 4.0 %copy-start.4 = (bf16[64,4224]{1,0:T(8,128)(2,1)}, bf16[64,4224]{1,0:T(8,128)(2,1)S(1)}, u32[]{:S(2)}) copy-start(bf16[64,4224]{1,0:T(8,128)(2,1)S(1)} %collective-permute-done.7.refs_5_.refs_13_) | copy-start | bytes 1622020
  64.4 16.5 %collective-permute-start.10 = (bf16[64,4224]{1,0:T(8,128)(2,1)}, bf16[64,4224]{1,0:T(8,128)(2,1)}, u32[]{:S(2)}, u32[]{:S(2)}) collective-permute-start(bf16[64,4224]{1,0:T(8,128)(2,1)} %collective-permute-done.3.refs_1_.refs_9_), channel_id=1, source_target_pairs={{0,48},{16,0},{32,16},{48,32},{1,49},{17,1},{33,17},{49,33},{2,50}... | collective-permute-start | bytes 1622024 | tf_op jit(solution)/shard_map/ppermute | solution.py:21
  65.8 15.1 %collective-permute-start.11 = (bf16[64,4224]{1,0:T(8,128)(2,1)}, bf16[64,4224]{1,0:T(8,128)(2,1)}, u32[]{:S(2)}, u32[]{:S(2)}) collective-permute-start(bf16[64,4224]{1,0:T(8,128)(2,1)} %collective-permute-done.3.refs_1_.refs_9_), channel_id=1, source_target_pairs={{0,16},{16,32},{32,48},{48,0},{1,17},{17,33},{33,49},{49,1},{2,18}... | collective-permute-start | bytes 1622024 | tf_op jit(solution)/shard_map/ppermute | solution.py:21
  66.5 22.5 %collective-permute-start.17 = (bf16[64,4224]{1,0:T(8,128)(2,1)S(1)}, bf16[64,4224]{1,0:T(8,128)(2,1)}, u32[]{:S(2)}, u32[]{:S(2)}) collective-permute-start(bf16[64,4224]{1,0:T(8,128)(2,1)S(1)} %collective-permute-done.9.refs_7_.refs_15_), channel_id=1, source_target_pairs={{0,64},{64,128},{128,192},{192,0},{1,65},{65,129},{129,193},{193,1... | collective-permute-start | bytes 1622024 | tf_op jit(solution)/shard_map/ppermute | solution.py:21
  76.3 12.7 %collective-permute-start.15 = (bf16[64,4224]{1,0:T(8,128)(2,1)}, bf16[64,4224]{1,0:T(8,128)(2,1)S(1)}, u32[]{:S(2)}, u32[]{:S(2)}) collective-permute-start(bf16[64,4224]{1,0:T(8,128)(2,1)} %copy-done.4), channel_id=1, source_target_pairs={{0,16},{16,32},{32,48},{48,0},{1,17},{17,33},{33,49},{49,1},{2,18}... | collective-permute-start | bytes 1622024 | tf_op jit(solution)/shard_map/ppermute | solution.py:21
  80.9 9.6 %collective-permute-start.16 = (bf16[64,4224]{1,0:T(8,128)(2,1)}, bf16[64,4224]{1,0:T(8,128)(2,1)S(1)}, u32[]{:S(2)}, u32[]{:S(2)}) collective-permute-start(bf16[64,4224]{1,0:T(8,128)(2,1)} %collective-permute-done.10.refs_0_.refs_4_), channel_id=1, source_target_pairs={{0,48},{16,0},{32,16},{48,32},{1,49},{17,1},{33,17},{49,33},{2,50}... | collective-permute-start | bytes 1622024 | tf_op jit(solution)/shard_map/ppermute | solution.py:21
  82.2 9.6 %collective-permute-start.18 = (bf16[64,4224]{1,0:T(8,128)(2,1)}, bf16[64,4224]{1,0:T(8,128)(2,1)S(1)}, u32[]{:S(2)}, u32[]{:S(2)}) collective-permute-start(bf16[64,4224]{1,0:T(8,128)(2,1)} %collective-permute-done.12.refs_2_.refs_6_), channel_id=1, source_target_pairs={{0,192},{64,0},{128,64},{192,128},{1,193},{65,1},{129,65},{193,129... | collective-permute-start | bytes 1622024 | tf_op jit(solution)/shard_map/ppermute | solution.py:21
  88.9 44.7 %collective-permute-start.14 = (bf16[8,192,512]{2,1,0:T(8,128)(2,1)}, bf16[8,192,512]{2,1,0:T(8,128)(2,1)}, u32[]{:S(2)}, u32[]{:S(2)}) collective-permute-start(bf16[8,192,512]{2,1,0:T(8,128)(2,1)} %bitcast.14.own_ref), channel_id=1, source_target_pairs={{0,8},{8,0},{1,9},{9,1},{2,10},{10,2},{3,11},{11,3},{4,12},{12,4},... | collective-permute-start | bytes 4718600 | tf_op jit(solution)/shard_map/ppermute | solution.py:21
  89.1 2.8 %copy-start.6 = (bf16[64,4224]{1,0:T(8,128)(2,1)}, bf16[64,4224]{1,0:T(8,128)(2,1)S(1)}, u32[]{:S(2)}) copy-start(bf16[64,4224]{1,0:T(8,128)(2,1)S(1)} %collective-permute-done.15.refs_0_.refs_4_) | copy-start | bytes 1622020
  90.5 1.4 copy-start.7
  91.8 0.8 copy-start.8
  98.5 8.1 %collective-permute-start.19 = (bf16[384,384]{1,0:T(8,128)(2,1)S(1)}, bf16[384,384]{1,0:T(8,128)(2,1)S(1)}, u32[]{:S(2)}, u32[]{:S(2)}) collective-permute-start(bf16[384,384]{1,0:T(8,128)(2,1)S(1)} %pad_maximum_fusion.2.refs_0_), channel_id=1, source_target_pairs={{0,7},{1,0},{2,1},{3,2},{4,3},{5,4},{6,5},{7,6},{8,15},{9,8},{10,9... | collective-permute-start | bytes 884744 | tf_op jit(solution)/shard_map/ppermute | solution.py:21
  101.5 8.9 %collective-permute-start.23 = (bf16[384,384]{1,0:T(8,128)(2,1)S(1)}, bf16[384,384]{1,0:T(8,128)(2,1)S(1)}, u32[]{:S(2)}, u32[]{:S(2)}) collective-permute-start(bf16[384,384]{1,0:T(8,128)(2,1)S(1)} %pad_maximum_fusion.2.refs_0_), channel_id=1, source_target_pairs={{0,1},{1,2},{2,3},{3,4},{4,5},{5,6},{6,7},{7,0},{8,9},{9,10},{10,1... | collective-permute-start | bytes 884744 | tf_op jit(solution)/shard_map/ppermute | solution.py:21
  106.7 8.0 %collective-permute-start.20 = (bf16[384,384]{1,0:T(8,128)(2,1)S(1)}, bf16[384,384]{1,0:T(8,128)(2,1)S(1)}, u32[]{:S(2)}, u32[]{:S(2)}) collective-permute-start(bf16[384,384]{1,0:T(8,128)(2,1)S(1)} %collective-permute-done.19.refs_1_), channel_id=1, source_target_pairs={{0,7},{1,0},{2,1},{3,2},{4,3},{5,4},{6,5},{7,6},{8,15},{9,8},{10,9... | collective-permute-start | bytes 884744 | tf_op jit(solution)/shard_map/ppermute | solution.py:21
  110.4 8.0 %collective-permute-start.24 = (bf16[384,384]{1,0:T(8,128)(2,1)S(1)}, bf16[384,384]{1,0:T(8,128)(2,1)S(1)}, u32[]{:S(2)}, u32[]{:S(2)}) collective-permute-start(bf16[384,384]{1,0:T(8,128)(2,1)S(1)} %collective-permute-done.23.refs_7_), channel_id=1, source_target_pairs={{0,1},{1,2},{2,3},{3,4},{4,5},{5,6},{6,7},{7,0},{8,9},{9,10},{10,1... | collective-permute-start | bytes 884744 | tf_op jit(solution)/shard_map/ppermute | solution.py:21
  114.7 8.5 %collective-permute-start.21 = (bf16[384,384]{1,0:T(8,128)(2,1)S(1)}, bf16[384,384]{1,0:T(8,128)(2,1)S(1)}, u32[]{:S(2)}, u32[]{:S(2)}) collective-permute-start(bf16[384,384]{1,0:T(8,128)(2,1)S(1)} %collective-permute-done.20.refs_2_), channel_id=1, source_target_pairs={{0,7},{1,0},{2,1},{3,2},{4,3},{5,4},{6,5},{7,6},{8,15},{9,8},{10,9... | collective-permute-start | bytes 884744 | tf_op jit(solution)/shard_map/ppermute | solution.py:21
  118.3 8.6 %collective-permute-start.25 = (bf16[384,384]{1,0:T(8,128)(2,1)S(1)}, bf16[384,384]{1,0:T(8,128)(2,1)S(1)}, u32[]{:S(2)}, u32[]{:S(2)}) collective-permute-start(bf16[384,384]{1,0:T(8,128)(2,1)S(1)} %collective-permute-done.24.refs_6_), channel_id=1, source_target_pairs={{0,1},{1,2},{2,3},{3,4},{4,5},{5,6},{6,7},{7,0},{8,9},{9,10},{10,1... | collective-permute-start | bytes 884744 | tf_op jit(solution)/shard_map/ppermute | solution.py:21
  123.1 6.4 %collective-permute-start.22 = (bf16[192,384]{1,0:T(8,128)(2,1)S(1)}, bf16[192,384]{1,0:T(8,128)(2,1)S(1)}, u32[]{:S(2)}, u32[]{:S(2)}) collective-permute-start(bf16[192,384]{1,0:T(8,128)(2,1)S(1)} %slice.52), channel_id=1, source_target_pairs={{0,7},{1,0},{2,1},{3,2},{4,3},{5,4},{6,5},{7,6},{8,15},{9,8},{10,9... | collective-permute-start | bytes 442376 | tf_op jit(solution)/shard_map/ppermute | solution.py:21
  126.9 6.7 %collective-permute-start.26 = (bf16[192,384]{1,0:T(8,128)(2,1)S(1)}, bf16[192,384]{1,0:T(8,128)(2,1)S(1)}, u32[]{:S(2)}, u32[]{:S(2)}) collective-permute-start(bf16[192,384]{1,0:T(8,128)(2,1)S(1)} %slice.53), channel_id=1, source_target_pairs={{0,1},{1,2},{2,3},{3,4},{4,5},{5,6},{6,7},{7,0},{8,9},{9,10},{10,1... | collective-permute-start | bytes 442376 | tf_op jit(solution)/shard_map/ppermute | solution.py:21
  139.1 17.2 %all-to-all-start.2 = ((bf16[16,48,512]{2,1,0:T(8,128)(2,1)}), bf16[16,48,512]{2,1,0:T(8,128)(2,1)S(1)}, u32[]{:S(2)}, u32[]{:S(2)}) async-start(bf16[16,48,512]{2,1,0:T(8,128)(2,1)} %bitcast.15), calls=%async_computation.2 | async-start | bytes 1572864 | tf_op jit(solution)/shard_map/all_to_all | solution.py:452
  146.8 15.5 %copy-start.10 = (s32[64]{0:T(128)S(1)}, s32[64]{0:T(128)}, u32[]{:S(2)}) copy-start(s32[64]{0:T(128)} %param.23) | copy-start | bytes 772
  157.8 17.8 %all-to-all-start.3 = ((bf16[8,64,512]{2,1,0:T(8,128)(2,1)}), bf16[8,64,512]{2,1,0:T(8,128)(2,1)S(1)}, u32[]{:S(2)}, u32[]{:S(2)}) async-start(bf16[8,64,512]{2,1,0:T(8,128)(2,1)} %broadcast_in_dim.18), calls=%async_computation.3 | async-start | bytes 1048576 | tf_op jit(solution)/shard_map/all_to_all | solution.py:39

commit v4 on v3

--- a/solution.py
+++ b/solution.py
@@ -93,7 +93,7 @@
             out_ref[:, j * hidden : (j + 1) * hidden] = packed.astype(BF)
 
 
-def expert_slots(pieces, masks, weights):
+def expert_slots(pieces, masks, weights, on_chip=False):
     hidden, depth = weights[0].shape
     chunk = 1024
     steps = depth // chunk
@@ -102,7 +102,7 @@
     in_specs += [pl.BlockSpec((m, chunk), lambda k: (0, k)) for m in sizes]
     in_specs += [pl.BlockSpec((m, LANES), lambda k: (0, depth // LANES)) for m in sizes]
     in_specs += [pl.BlockSpec((hidden, chunk), lambda k: (0, k))] * 4
-    pieces, weights = in_hbm(pieces), in_hbm(weights)
+    pieces, weights = pieces if on_chip else in_hbm(pieces), in_hbm(weights)
     total = sum(sizes)
     slots = total // 8 * CAP
     return pl.pallas_call(
@@ -129,7 +129,7 @@
     *((h, 0, i) for h in (0, 1) for i in (0, 2)),
     *((h, o, 0) for h in (0, 1) for o in (1, 3)),
     *((h, o, 2) for h in (0, 1) for o in (1, 3)),
-    *((h, 2, i) for h in (0, 1) for i in (0, 2)),
+    *((h, 2, i) for i in (0, 2) for h in (0, 1)),
 )
 
 
@@ -435,15 +435,11 @@
     far = (*a_far_sides, *b_far_sides)
     slots = expert_slots(near, masks, weights)
     slots, *far = lax.optimization_barrier((slots, *far))
-    opposite = (
-        shift(a_near_sides[1], "y", -1),
-        shift(far[0], "y", 1),
-        shift(b_near_sides[1], "x", -1),
-        shift(far[2], "x", 1),
-    )
+    far += [shift(a_near_sides[1], "y", -1), shift(b_near_sides[1], "x", -1)]
+    opposite = (shift(far[0], "y", 1), shift(far[2], "x", 1))
     more, down_own = lax.optimization_barrier((expert_slots(far, masks, weights), down_own))
     down_other = shift(down_own, "c", 1)
-    slots = jnp.concatenate([slots, more, expert_slots(opposite, masks, weights)], axis=0)
+    slots = jnp.concatenate([slots, more, expert_slots(opposite, masks, weights, on_chip=True)], axis=0)
     active = ring(slots, "z")
     place = jnp.stack([x, y, z]).astype(jnp.int32)
     result = lower(place, active, down_own, down_other, chips)

time: 184 us -> 191 us (1.038)
  waiting for transfers between devices: 64.2 us -> 68.6 us
    ppermute x23, waiting for transfers between devices: 33.3 us -> 37.8 us  [shift(): lax.ppermute(values, axis, [(i, (i - step) % size) for i in range(size)])]
    ppermute x23, starting transfers between devices: 30.4 us -> 32.7 us  [shift(): lax.ppermute(values, axis, [(i, (i - step) % size) for i in range(size)])]
  transfers between devices with their start and end apart: 30 -> 30, of which waited for: 13 -> 12; matrix products, arithmetic and copies ran while one was open for 1% -> 1% of each run, Pallas kernels for 11% -> 11%
where the time goes in v4:
time: 191 us; the launch traced here: 190 us
  waiting for transfers between devices  68.6 us (36%)
  starting transfers between devices  54.4 us (28%)
  Pallas kernels  34.1 us (18%)
  blocking collectives  26.4 us (14%)
  local copies, waits for them, and re-layouts  4.28 us (2%)
    ppermute x23, waiting for transfers between devices, shift(): lax.ppermute(values, axis, [(i, (i - step) % size) for i in range(size)])  37.8 us
    ppermute x23, starting transfers between devices, shift(): lax.ppermute(values, axis, [(i, (i - step) % size) for i in range(size)])  32.7 us
    all_to_all x1, blocking collectives, per_device(): lax.all_to_all(sent, 'z', 0, 0, tiled=True)  26.4 us
    pallas_call x3, Pallas kernels, expert_slots(): pl.pallas_call(functools.partial(expert_kernel, sizes, steps), grid=(step...  20.4 us
    all_to_all x1, waiting for transfers between devices, copies(): lax.all_to_all(jnp.broadcast_to(values[None], (size, *values.shape)), axi...  13.3 us
    all_to_all x1, waiting for transfers between devices, per_device(): returned = lax.all_to_all(result, ('x', 'y'), 0, 0, tiled=True)  9.68 us
    ppermute x4, waiting for transfers between devices, pairs(): return lax.ppermute(block, axis, [(i, i ^ mask) for i in range(4)])  7.86 us
    pallas_call x1, Pallas kernels, attend(): pl.pallas_call(attend_kernel, in_specs=[pl.BlockSpec(memory_space=pltpu.S...  7.29 us
  transfers between devices with their start and end apart: 30, of which 12 were waited for; matrix products, arithmetic and copies ran while one was open for 1% of the time, Pallas kernels for 11%

profile of v4, /device:TPU:8, one launch (start us, length us, event | category | flops | bytes accessed | tf_op | source)
XLA Modules:
  0.0 190.5 jit_solution(13193190455020783164)
XLA Ops:
  0.7 0.5 collective-permute-start.1
  1.2 1.0 prepare.1
  2.2 26.4 %all_to_all.31 = bf16[8,8,4224]{2,1,0:T(8,128)(2,1)S(1)} all-to-all(bf16[8,8,4224]{2,1,0:T(8,128)(2,1)S(1)} %prepare.1), channel_id=1, replica_groups=mesh['x'=4,'y'=4,'c'=2,'z'=8] {'z'}, dimensions={0} | all-to-all | bytes 1081344 | tf_op jit(solution)/shard_map/all_to_all | solution.py:404
  28.6 0.2 fusion.1
  29.0 0.5 collective-permute-start.4
  29.6 1.5 collective-permute-start.2
  31.1 1.3 copy.22
  32.4 4.3 %all-to-all-start.1 = ((bf16[192,8,512]{2,0,1:T(8,128)(2,1)}), bf16[192,8,512]{2,0,1:T(8,128)(2,1)}, u32[]{:S(2)}, u32[]{:S(2)}) async-start(bf16[192,8,512]{2,0,1:T(8,128)(2,1)} %bitcast.24), calls=%async_computation.1 | async-start | bytes 3145728 | tf_op jit(solution)/shard_map/all_to_all | solution.py:407
  36.8 2.5 %collective-permute-start.5 = (bf16[64,4224]{1,0:T(8,128)(2,1)S(1)}, bf16[64,4224]{1,0:T(8,128)(2,1)}, u32[]{:S(2)}, u32[]{:S(2)}) collective-permute-start(bf16[64,4224]{1,0:T(8,128)(2,1)S(1)} %pad_maximum_fusion.1.refs_2_.refs_10_), channel_id=1, source_target_pairs={{0,48},{16,32},{32,16},{48,0},{1,49},{17,33},{33,17},{49,1},{2,50}... | collective-permute-start | bytes 1622024 | tf_op jit(solution)/shard_map/ppermute | solution.py:424
  39.3 2.2 %collective-permute-start.3 = (bf16[64,4224]{1,0:T(8,128)(2,1)S(1)}, bf16[64,4224]{1,0:T(8,128)(2,1)S(1)}, u32[]{:S(2)}, u32[]{:S(2)}) collective-permute-start(bf16[64,4224]{1,0:T(8,128)(2,1)S(1)} %pad_maximum_fusion.refs_0_.refs_8_), channel_id=1, source_target_pairs={{0,192},{64,128},{128,64},{192,0},{1,193},{65,129},{129,65},{193,1... | collective-permute-start | bytes 1622024 | tf_op jit(solution)/shard_map/ppermute | solution.py:424
  41.5 0.6 collective-permute-start.9
  42.1 2.9 %collective-permute-start.8 = (bf16[64,4224]{1,0:T(8,128)(2,1)S(1)}, bf16[64,4224]{1,0:T(8,128)(2,1)}, u32[]{:S(2)}, u32[]{:S(2)}) collective-permute-start(bf16[64,4224]{1,0:T(8,128)(2,1)S(1)} %pad_maximum_fusion.1.refs_2_.refs_10_), channel_id=1, source_target_pairs={{0,192},{64,0},{128,64},{192,128},{1,193},{65,1},{129,65},{193,129... | collective-permute-start | bytes 1622024 | tf_op jit(solution)/shard_map/ppermute | solution.py:21
  45.0 7.0 %collective-permute-done.5.refs_3_.refs_11_ = bf16[64,4224]{1,0:T(8,128)(2,1)} collective-permute-done((bf16[64,4224]{1,0:T(8,128)(2,1)S(1)}, bf16[64,4224]{1,0:T(8,128)(2,1)}, u32[]{:S(2)}, u32[]{:S(2)}) %collective-permute-start.5) | collective-permute-done | bytes 540704 | tf_op jit(solution)/shard_map/ppermute | solution.py:424
  52.0 3.0 %collective-permute-start.6 = (bf16[64,4224]{1,0:T(8,128)(2,1)S(1)}, bf16[64,4224]{1,0:T(8,128)(2,1)}, u32[]{:S(2)}, u32[]{:S(2)}) collective-permute-start(bf16[64,4224]{1,0:T(8,128)(2,1)S(1)} %pad_maximum_fusion.refs_0_.refs_8_), channel_id=1, source_target_pairs={{0,48},{16,0},{32,16},{48,32},{1,49},{17,1},{33,17},{49,33},{2,50}... | collective-permute-start | bytes 1622024 | tf_op jit(solution)/shard_map/ppermute | solution.py:21
  55.0 0.9 collective-permute-done.3.refs_1_.refs_9_
  55.8 2.1 %collective-permute-start.12 = (bf16[64,4224]{1,0:T(8,128)(2,1)}, bf16[64,4224]{1,0:T(8,128)(2,1)}, u32[]{:S(2)}, u32[]{:S(2)}) collective-permute-start(bf16[64,4224]{1,0:T(8,128)(2,1)} %collective-permute-done.5.refs_3_.refs_11_), channel_id=1, source_target_pairs={{0,192},{64,0},{128,64},{192,128},{1,193},{65,1},{129,65},{193,129... | collective-permute-start | bytes 1622024 | tf_op jit(solution)/shard_map/ppermute | solution.py:21
  57.9 6.4 %collective-permute-done.9.refs_7_.refs_15_ = bf16[64,4224]{1,0:T(8,128)(2,1)S(1)} collective-permute-done((bf16[64,4224]{1,0:T(8,128)(2,1)S(1)}, bf16[64,4224]{1,0:T(8,128)(2,1)S(1)}, u32[]{:S(2)}, u32[]{:S(2)}) %collective-permute-start.9) | collective-permute-done | bytes 540704 | tf_op jit(solution)/shard_map/ppermute | solution.py:21
  64.4 1.4 collective-permute-start.10
  65.8 0.6 collective-permute-start.11
  66.5 1.5 collective-permute-start.15
  68.0 6.4 %collective-permute-done.12.refs_2_.refs_8_ = bf16[64,4224]{1,0:T(8,128)(2,1)} collective-permute-done((bf16[64,4224]{1,0:T(8,128)(2,1)}, bf16[64,4224]{1,0:T(8,128)(2,1)}, u32[]{:S(2)}, u32[]{:S(2)}) %collective-permute-start.12) | collective-permute-done | bytes 540704 | tf_op jit(solution)/shard_map/ppermute | solution.py:21
  74.4 0.3 collective-permute-start.14
  74.8 7.9 %expert_slots.3 = bf16[192,384]{1,0:T(8,128)(2,1)S(1)} custom-call(bf16[8,128]{1,0:T(8,128)(2,1)S(1)} %convert_convert_fusion.mask_ref, bf16[64,4224]{1,0:T(8,128)(2,1)} %copy-done.2, bf16[64,4224]{1,0:T(8,128)(2,1)} %copy-done.5, bf16[64,4224]{1,0:T(8,128)(2,1)} %copy-done.1, bf16[64,4224]{1,0:T(8,128)(2,1)} %collective-permute-done.5.refs_3_.refs_11_, ...), custom_call_target="tpu_custom_call" | custom-call | flops 3221225472 | bytes 10485760 | tf_op jit(solution)/shard_map/expert_slots/pallas_call | solution.py:108
  82.7 1.8 collective-permute-start.17
  84.5 3.7 %collective-permute-start.18 = (bf16[64,4224]{1,0:T(8,128)(2,1)}, bf16[64,4224]{1,0:T(8,128)(2,1)S(1)}, u32[]{:S(2)}, u32[]{:S(2)}) collective-permute-start(bf16[64,4224]{1,0:T(8,128)(2,1)} %collective-permute-done.12.refs_2_.refs_8_), channel_id=1, source_target_pairs={{0,192},{64,0},{128,64},{192,128},{1,193},{65,1},{129,65},{193,129... | collective-permute-start | bytes 1622024 | tf_op jit(solution)/shard_map/ppermute | solution.py:21
  88.2 0.5 collective-permute-done.15.refs_5_.refs_11_
  88.7 0.8 copy-done.6
  89.5 0.8 copy-done.7
  90.3 6.9 %expert_slots.4 = bf16[144,384]{1,0:T(8,128)(2,1)S(1)} custom-call(bf16[8,128]{1,0:T(8,128)(2,1)S(1)} %convert_convert_fusion.mask_ref, bf16[64,4224]{1,0:T(8,128)(2,1)} %collective-permute-done.10.refs_0_.refs_6_, bf16[64,4224]{1,0:T(8,128)(2,1)} %collective-permute-done.11.refs_1_.refs_7_, bf16[64,4224]{1,0:T(8,128)(2,1)} %collective-permute-done.12.refs_2_.refs_8_, ...), custom_call_target="tpu_custom_call" | custom-call | flops 2415919104 | bytes 9437184 | tf_op jit(solution)/shard_map/expert_slots/pallas_call | solution.py:108
  97.3 5.6 %expert_slots.5 = bf16[48,384]{1,0:T(8,128)(2,1)S(1)} custom-call(bf16[8,128]{1,0:T(8,128)(2,1)S(1)} %convert_convert_fusion.mask_ref, bf16[64,4224]{1,0:T(8,128)(2,1)S(1)} %collective-permute-done.17.refs_0_.refs_2_, bf16[64,4224]{1,0:T(8,128)(2,1)S(1)} %collective-permute-done.18.refs_1_.refs_3_, ...), custom_call_target="tpu_custom_call" | custom-call | flops 805306368 | bytes 7340032 | tf_op jit(solution)/shard_map/expert_slots/pallas_call | solution.py:108
  102.9 2.6 %collective-permute-start.19 = (bf16[384,384]{1,0:T(8,128)(2,1)S(1)}, bf16[384,384]{1,0:T(8,128)(2,1)S(1)}, u32[]{:S(2)}, u32[]{:S(2)}) collective-permute-start(bf16[384,384]{1,0:T(8,128)(2,1)S(1)} %pad_maximum_fusion.2.refs_0_), channel_id=1, source_target_pairs={{0,7},{1,0},{2,1},{3,2},{4,3},{5,4},{6,5},{7,6},{8,15},{9,8},{10,9... | collective-permute-start | bytes 884744 | tf_op jit(solution)/shard_map/ppermute | solution.py:21
  105.6 6.9 %collective-permute-done.19.refs_1_ = bf16[384,384]{1,0:T(8,128)(2,1)S(1)} collective-permute-done((bf16[384,384]{1,0:T(8,128)(2,1)S(1)}, bf16[384,384]{1,0:T(8,128)(2,1)S(1)}, u32[]{:S(2)}, u32[]{:S(2)}) %collective-permute-start.19) | collective-permute-done | bytes 294944 | tf_op jit(solution)/shard_map/ppermute | solution.py:21
  112.5 3.7 %collective-permute-start.20 = (bf16[384,384]{1,0:T(8,128)(2,1)S(1)}, bf16[384,384]{1,0:T(8,128)(2,1)S(1)}, u32[]{:S(2)}, u32[]{:S(2)}) collective-permute-start(bf16[384,384]{1,0:T(8,128)(2,1)S(1)} %collective-permute-done.19.refs_1_), channel_id=1, source_target_pairs={{0,7},{1,0},{2,1},{3,2},{4,3},{5,4},{6,5},{7,6},{8,15},{9,8},{10,9... | collective-permute-start | bytes 884744 | tf_op jit(solution)/shard_map/ppermute | solution.py:21
  116.2 6.1 %collective-permute-done.20.refs_2_ = bf16[384,384]{1,0:T(8,128)(2,1)S(1)} collective-permute-done((bf16[384,384]{1,0:T(8,128)(2,1)S(1)}, bf16[384,384]{1,0:T(8,128)(2,1)S(1)}, u32[]{:S(2)}, u32[]{:S(2)}) %collective-permute-start.20) | collective-permute-done | bytes 294944 | tf_op jit(solution)/shard_map/ppermute | solution.py:21
  122.3 3.7 %collective-permute-start.21 = (bf16[384,384]{1,0:T(8,128)(2,1)S(1)}, bf16[384,384]{1,0:T(8,128)(2,1)S(1)}, u32[]{:S(2)}, u32[]{:S(2)}) collective-permute-start(bf16[384,384]{1,0:T(8,128)(2,1)S(1)} %collective-permute-done.20.refs_2_), channel_id=1, source_target_pairs={{0,7},{1,0},{2,1},{3,2},{4,3},{5,4},{6,5},{7,6},{8,15},{9,8},{10,9... | collective-permute-start | bytes 884744 | tf_op jit(solution)/shard_map/ppermute | solution.py:21
  126.1 5.1 %collective-permute-done.21.refs_3_ = bf16[384,384]{1,0:T(8,128)(2,1)S(1)} collective-permute-done((bf16[384,384]{1,0:T(8,128)(2,1)S(1)}, bf16[384,384]{1,0:T(8,128)(2,1)S(1)}, u32[]{:S(2)}, u32[]{:S(2)}) %collective-permute-start.21) | collective-permute-done | bytes 294944 | tf_op jit(solution)/shard_map/ppermute | solution.py:21
  131.3 3.8 %collective-permute-start.22 = (bf16[192,384]{1,0:T(8,128)(2,1)S(1)}, bf16[192,384]{1,0:T(8,128)(2,1)S(1)}, u32[]{:S(2)}, u32[]{:S(2)}) collective-permute-start(bf16[192,384]{1,0:T(8,128)(2,1)S(1)} %slice.52), channel_id=1, source_target_pairs={{0,7},{1,0},{2,1},{3,2},{4,3},{5,4},{6,5},{7,6},{8,15},{9,8},{10,9... | collective-permute-start | bytes 442376 | tf_op jit(solution)/shard_map/ppermute | solution.py:21
  135.1 0.3 collective-permute-start.26
  135.5 2.2 %collective-permute-done.22 = bf16[192,384]{1,0:T(8,128)(2,1)S(1)} collective-permute-done((bf16[192,384]{1,0:T(8,128)(2,1)S(1)}, bf16[192,384]{1,0:T(8,128)(2,1)S(1)}, u32[]{:S(2)}, u32[]{:S(2)}) %collective-permute-start.22) | collective-permute-done | bytes 147488 | tf_op jit(solution)/shard_map/ppermute | solution.py:21
  137.7 4.0 %collective-permute-done.26 = bf16[192,384]{1,0:T(8,128)(2,1)S(1)} collective-permute-done((bf16[192,384]{1,0:T(8,128)(2,1)S(1)}, bf16[192,384]{1,0:T(8,128)(2,1)S(1)}, u32[]{:S(2)}, u32[]{:S(2)}) %collective-permute-start.26) | collective-permute-done | bytes 147488 | tf_op jit(solution)/shard_map/ppermute | solution.py:21
  141.8 5.5 %lower.1 = bf16[16,2,24,512]{3,2,1,0:T(8,128)(2,1)} custom-call(s32[3]{0:T(128)S(1)} %pad_add_fusion.place_ref, bf16[8,192,512]{2,1,0:T(8,128)(2,1)} %bitcast.14.own_ref, bf16[8,192,512]{2,1,0:T(8,128)(2,1)} %collective-permute-done.16.other_ref, bf16[384,384]{1,0:T(8,128)(2,1)S(1)} %pad_maximum_fusion.2.refs_0_, ...), custom_call_target="tpu_custom_call" | custom-call | flops 1207959552 | bytes 5505024 | tf_op jit(solution)/shard_map/lower/pallas_call | solution.py:180
  147.3 6.2 %all-to-all-start.2 = ((bf16[16,48,512]{2,1,0:T(8,128)(2,1)}), bf16[16,48,512]{2,1,0:T(8,128)(2,1)S(1)}, u32[]{:S(2)}, u32[]{:S(2)}) async-start(bf16[16,48,512]{2,1,0:T(8,128)(2,1)} %bitcast.15), calls=%async_computation.2 | async-start | bytes 1572864 | tf_op jit(solution)/shard_map/all_to_all | solution.py:448
  154.0 9.7 %all-to-all-done.2 = bf16[16,48,512]{2,1,0:T(8,128)(2,1)S(1)} async-done(((bf16[16,48,512]{2,1,0:T(8,128)(2,1)}), bf16[16,48,512]{2,1,0:T(8,128)(2,1)S(1)}, u32[]{:S(2)}, u32[]{:S(2)}) %all-to-all-start.2) | async-done | bytes 786464 | tf_op jit(solution)/shard_map/all_to_all | solution.py:448
  163.7 0.5 fusion
  164.2 0.8 broadcast_in_dim.18
  165.1 4.5 %all-to-all-start.3 = ((bf16[8,64,512]{2,1,0:T(8,128)(2,1)}), bf16[8,64,512]{2,1,0:T(8,128)(2,1)S(1)}, u32[]{:S(2)}, u32[]{:S(2)}) async-start(bf16[8,64,512]{2,1,0:T(8,128)(2,1)} %broadcast_in_dim.18), calls=%async_computation.3 | async-start | bytes 1048576 | tf_op jit(solution)/shard_map/all_to_all | solution.py:39
  169.6 13.3 %all-to-all-done.3.stream_ref = bf16[8,64,512]{2,1,0:T(8,128)(2,1)S(1)} async-done(((bf16[8,64,512]{2,1,0:T(8,128)(2,1)}), bf16[8,64,512]{2,1,0:T(8,128)(2,1)S(1)}, u32[]{:S(2)}, u32[]{:S(2)}) %all-to-all-start.3) | async-done | bytes 524320 | tf_op jit(solution)/shard_map/all_to_all | solution.py:39
  183.0 7.3 %attend.1 = (bf16[8,4096]{1,0:T(8,128)(2,1)}, bf16[64,512]{1,0:T(8,128)(2,1)}) custom-call(s32[3]{0:T(128)S(1)} %pad_add_fusion.place_ref, bf16[8,64,512]{2,1,0:T(8,128)(2,1)S(1)} %all-to-all-done.3.stream_ref, bf16[4096,512]{1,0:T(8,128)(2,1)} %wq_ref.1, bf16[4096,128]{1,0:T(8,128)(2,1)} %wk_ref.1, bf16[4096,128]{1,0:T(8,128)(2,1)} %wv_ref.1, ...), custom_call_target="tpu_custom_call" | custom-call | flops 402653184 | bytes 6291456 | tf_op jit(solution)/shard_map/attend/pallas_call | solution.py:285
  (73 shorter events, 1.6 us)
Async XLA Ops:
  0.6 28.0 %collective-permute-start = (bf16[192,4096]{1,0:T(8,128)(2,1)}, bf16[192,4096]{1,0:T(8,128)(2,1)S(1)}, u32[]{:S(2)}, u32[]{:S(2)}) collective-permute-start(bf16[192,4096]{1,0:T(8,128)(2,1)} %bitcast.31), channel_id=1, source_target_pairs={{0,8},{8,0},{1,9},{9,1},{2,10},{10,2},{3,11},{11,3},{4,12},{12,4},... | collective-permute-start | bytes 4718600 | tf_op jit(solution)/shard_map/ppermute | solution.py:21
  0.7 27.9 %collective-permute-start.1 = (bf16[192,4096]{1,0:T(8,128)(2,1)}, bf16[192,4096]{1,0:T(8,128)(2,1)}, u32[]{:S(2)}, u32[]{:S(2)}) collective-permute-start(bf16[192,4096]{1,0:T(8,128)(2,1)} %bitcast.35), channel_id=1, source_target_pairs={{0,8},{8,0},{1,9},{9,1},{2,10},{10,2},{3,11},{11,3},{4,12},{12,4},... | collective-permute-start | bytes 4718600 | tf_op jit(solution)/shard_map/ppermute | solution.py:21
  28.6 2.5 %copy-start.8 = (bf16[1,192,4096]{2,1,0:T(8,128)(2,1)S(1)}, bf16[1,192,4096]{2,1,0:T(8,128)(2,1)}, u32[]{:S(2)}) copy-start(bf16[1,192,4096]{2,1,0:T(8,128)(2,1)} %param.17) | copy-start | bytes 4718596
  28.6 3.8 %copy-start = (bf16[192,4096]{1,0:T(8,128)(2,1)}, bf16[192,4096]{1,0:T(8,128)(2,1)S(1)}, u32[]{:S(2)}) copy-start(bf16[192,4096]{1,0:T(8,128)(2,1)S(1)} %collective-permute-done.refs_18_.refs_14_.refs_6_) | copy-start | bytes 4718596
  29.0 7.7 %collective-permute-start.4 = (bf16[32,4224]{1,0:T(8,128)(2,1)S(1)}, bf16[32,4224]{1,0:T(8,128)(2,1)S(1)}, u32[]{:S(2)}, u32[]{:S(2)}) collective-permute-start(bf16[32,4224]{1,0:T(8,128)(2,1)S(1)} %get-tuple-element.24), channel_id=1, source_target_pairs={{0,16},{16,0},{32,48},{48,32},{1,17},{17,1},{33,49},{49,33},{2,18}... | collective-permute-start | bytes 811016 | tf_op jit(solution)/shard_map/ppermute | solution.py:424
  29.6 9.7 %collective-permute-start.2 = (bf16[32,4224]{1,0:T(8,128)(2,1)S(1)}, bf16[32,4224]{1,0:T(8,128)(2,1)S(1)}, u32[]{:S(2)}, u32[]{:S(2)}) collective-permute-start(bf16[32,4224]{1,0:T(8,128)(2,1)S(1)} %get-tuple-element.25), channel_id=1, source_target_pairs={{0,64},{64,0},{128,192},{192,128},{1,65},{65,1},{129,193},{193,129... | collective-permute-start | bytes 811016 | tf_op jit(solution)/shard_map/ppermute | solution.py:424
  32.4 64.8 %all-to-all-start.1 = ((bf16[192,8,512]{2,0,1:T(8,128)(2,1)}), bf16[192,8,512]{2,0,1:T(8,128)(2,1)}, u32[]{:S(2)}, u32[]{:S(2)}) async-start(bf16[192,8,512]{2,0,1:T(8,128)(2,1)} %bitcast.24), calls=%async_computation.1 | async-start | bytes 3145728 | tf_op jit(solution)/shard_map/all_to_all | solution.py:407
  36.8 38.0 %copy-start.1 = (bf16[64,4224]{1,0:T(8,128)(2,1)}, bf16[64,4224]{1,0:T(8,128)(2,1)S(1)}, u32[]{:S(2)}) copy-start(bf16[64,4224]{1,0:T(8,128)(2,1)S(1)} %pad_maximum_fusion.1.refs_2_.refs_10_) | copy-start | bytes 1622020
  36.8 15.2 %collective-permute-start.5 = (bf16[64,4224]{1,0:T(8,128)(2,1)S(1)}, bf16[64,4224]{1,0:T(8,128)(2,1)}, u32[]{:S(2)}, u32[]{:S(2)}) collective-permute-start(bf16[64,4224]{1,0:T(8,128)(2,1)S(1)} %pad_maximum_fusion.1.refs_2_.refs_10_), channel_id=1, source_target_pairs={{0,48},{16,32},{32,16},{48,0},{1,49},{17,33},{33,17},{49,1},{2,50}... | collective-permute-start | bytes 1622024 | tf_op jit(solution)/shard_map/ppermute | solution.py:424
  39.3 35.5 %copy-start.2 = (bf16[64,4224]{1,0:T(8,128)(2,1)}, bf16[64,4224]{1,0:T(8,128)(2,1)S(1)}, u32[]{:S(2)}) copy-start(bf16[64,4224]{1,0:T(8,128)(2,1)S(1)} %pad_maximum_fusion.refs_0_.refs_8_) | copy-start | bytes 1622020
  39.3 16.5 %collective-permute-start.3 = (bf16[64,4224]{1,0:T(8,128)(2,1)S(1)}, bf16[64,4224]{1,0:T(8,128)(2,1)S(1)}, u32[]{:S(2)}, u32[]{:S(2)}) collective-permute-start(bf16[64,4224]{1,0:T(8,128)(2,1)S(1)} %pad_maximum_fusion.refs_0_.refs_8_), channel_id=1, source_target_pairs={{0,192},{64,128},{128,64},{192,0},{1,193},{65,129},{129,65},{193,1... | collective-permute-start | bytes 1622024 | tf_op jit(solution)/shard_map/ppermute | solution.py:424
  41.5 22.8 %collective-permute-start.9 = (bf16[64,4224]{1,0:T(8,128)(2,1)S(1)}, bf16[64,4224]{1,0:T(8,128)(2,1)S(1)}, u32[]{:S(2)}, u32[]{:S(2)}) collective-permute-start(bf16[64,4224]{1,0:T(8,128)(2,1)S(1)} %pad_maximum_fusion.1.refs_2_.refs_10_), channel_id=1, source_target_pairs={{0,64},{64,128},{128,192},{192,0},{1,65},{65,129},{129,193},{193,1... | collective-permute-start | bytes 1622024 | tf_op jit(solution)/shard_map/ppermute | solution.py:21
  42.1 22.3 %collective-permute-start.7 = (bf16[64,4224]{1,0:T(8,128)(2,1)S(1)}, bf16[64,4224]{1,0:T(8,128)(2,1)S(1)}, u32[]{:S(2)}, u32[]{:S(2)}) collective-permute-start(bf16[64,4224]{1,0:T(8,128)(2,1)S(1)} %pad_maximum_fusion.refs_0_.refs_8_), channel_id=1, source_target_pairs={{0,16},{16,32},{32,48},{48,0},{1,17},{17,33},{33,49},{49,1},{2,18}... | collective-permute-start | bytes 1622024 | tf_op jit(solution)/shard_map/ppermute | solution.py:21
  42.1 23.7 %collective-permute-start.8 = (bf16[64,4224]{1,0:T(8,128)(2,1)S(1)}, bf16[64,4224]{1,0:T(8,128)(2,1)}, u32[]{:S(2)}, u32[]{:S(2)}) collective-permute-start(bf16[64,4224]{1,0:T(8,128)(2,1)S(1)} %pad_maximum_fusion.1.refs_2_.refs_10_), channel_id=1, source_target_pairs={{0,192},{64,0},{128,64},{192,128},{1,193},{65,1},{129,65},{193,129... | collective-permute-start | bytes 1622024 | tf_op jit(solution)/shard_map/ppermute | solution.py:21
  52.0 14.5 %collective-permute-start.6 = (bf16[64,4224]{1,0:T(8,128)(2,1)S(1)}, bf16[64,4224]{1,0:T(8,128)(2,1)}, u32[]{:S(2)}, u32[]{:S(2)}) collective-permute-start(bf16[64,4224]{1,0:T(8,128)(2,1)S(1)} %pad_maximum_fusion.refs_0_.refs_8_), channel_id=1, source_target_pairs={{0,48},{16,0},{32,16},{48,32},{1,49},{17,1},{33,17},{49,33},{2,50}... | collective-permute-start | bytes 1622024 | tf_op jit(solution)/shard_map/ppermute | solution.py:21
  55.8 19.0 %copy-start.5 = (bf16[64,4224]{1,0:T(8,128)(2,1)}, bf16[64,4224]{1,0:T(8,128)(2,1)S(1)}, u32[]{:S(2)}) copy-start(bf16[64,4224]{1,0:T(8,128)(2,1)S(1)} %collective-permute-done.3.refs_1_.refs_9_) | copy-start | bytes 1622020
  55.8 18.6 %collective-permute-start.12 = (bf16[64,4224]{1,0:T(8,128)(2,1)}, bf16[64,4224]{1,0:T(8,128)(2,1)}, u32[]{:S(2)}, u32[]{:S(2)}) collective-permute-start(bf16[64,4224]{1,0:T(8,128)(2,1)} %collective-permute-done.5.refs_3_.refs_11_), channel_id=1, source_target_pairs={{0,192},{64,0},{128,64},{192,128},{1,193},{65,1},{129,65},{193,129... | collective-permute-start | bytes 1622024 | tf_op jit(solution)/shard_map/ppermute | solution.py:21
  64.3 10.5 %copy-start.3 = (bf16[64,4224]{1,0:T(8,128)(2,1)}, bf16[64,4224]{1,0:T(8,128)(2,1)S(1)}, u32[]{:S(2)}) copy-start(bf16[64,4224]{1,0:T(8,128)(2,1)S(1)} %collective-permute-done.9.refs_7_.refs_15_) | copy-start | bytes 1622020
  64.3 18.4 %collective-permute-start.13 = (bf16[64,4224]{1,0:T(8,128)(2,1)}, bf16[64,4224]{1,0:T(8,128)(2,1)}, u32[]{:S(2)}, u32[]{:S(2)}) collective-permute-start(bf16[64,4224]{1,0:T(8,128)(2,1)} %collective-permute-done.5.refs_3_.refs_11_), channel_id=1, source_target_pairs={{0,64},{64,128},{128,192},{192,0},{1,65},{65,129},{129,193},{193,1... | collective-permute-start | bytes 1622024 | tf_op jit(solution)/shard_map/ppermute | solution.py:21
  64.4 10.5 %copy-start.4 = (bf16[64,4224]{1,0:T(8,128)(2,1)}, bf16[64,4224]{1,0:T(8,128)(2,1)S(1)}, u32[]{:S(2)}) copy-start(bf16[64,4224]{1,0:T(8,128)(2,1)S(1)} %collective-permute-done.7.refs_5_.refs_13_) | copy-start | bytes 1622020
  64.4 18.4 %collective-permute-start.10 = (bf16[64,4224]{1,0:T(8,128)(2,1)S(1)}, bf16[64,4224]{1,0:T(8,128)(2,1)}, u32[]{:S(2)}, u32[]{:S(2)}) collective-permute-start(bf16[64,4224]{1,0:T(8,128)(2,1)S(1)} %collective-permute-done.3.refs_1_.refs_9_), channel_id=1, source_target_pairs={{0,48},{16,0},{32,16},{48,32},{1,49},{17,1},{33,17},{49,33},{2,50}... | collective-permute-start | bytes 1622024 | tf_op jit(solution)/shard_map/ppermute | solution.py:21
  65.8 16.9 %collective-permute-start.11 = (bf16[64,4224]{1,0:T(8,128)(2,1)S(1)}, bf16[64,4224]{1,0:T(8,128)(2,1)}, u32[]{:S(2)}, u32[]{:S(2)}) collective-permute-start(bf16[64,4224]{1,0:T(8,128)(2,1)S(1)} %collective-permute-done.3.refs_1_.refs_9_), channel_id=1, source_target_pairs={{0,16},{16,32},{32,48},{48,0},{1,17},{17,33},{33,49},{49,1},{2,18}... | collective-permute-start | bytes 1622024 | tf_op jit(solution)/shard_map/ppermute | solution.py:21
  66.5 22.1 %collective-permute-start.15 = (bf16[64,4224]{1,0:T(8,128)(2,1)S(1)}, bf16[64,4224]{1,0:T(8,128)(2,1)S(1)}, u32[]{:S(2)}, u32[]{:S(2)}) collective-permute-start(bf16[64,4224]{1,0:T(8,128)(2,1)S(1)} %collective-permute-done.9.refs_7_.refs_15_), channel_id=1, source_target_pairs={{0,64},{64,128},{128,192},{192,0},{1,65},{65,129},{129,193},{193,1... | collective-permute-start | bytes 1622024 | tf_op jit(solution)/shard_map/ppermute | solution.py:21
  74.4 14.2 %collective-permute-start.14 = (bf16[64,4224]{1,0:T(8,128)(2,1)S(1)}, bf16[64,4224]{1,0:T(8,128)(2,1)S(1)}, u32[]{:S(2)}, u32[]{:S(2)}) collective-permute-start(bf16[64,4224]{1,0:T(8,128)(2,1)S(1)} %collective-permute-done.7.refs_5_.refs_13_), channel_id=1, source_target_pairs={{0,16},{16,32},{32,48},{48,0},{1,17},{17,33},{33,49},{49,1},{2,18}... | collective-permute-start | bytes 1622024 | tf_op jit(solution)/shard_map/ppermute | solution.py:21
  82.7 14.5 %collective-permute-start.17 = (bf16[64,4224]{1,0:T(8,128)(2,1)}, bf16[64,4224]{1,0:T(8,128)(2,1)S(1)}, u32[]{:S(2)}, u32[]{:S(2)}) collective-permute-start(bf16[64,4224]{1,0:T(8,128)(2,1)} %collective-permute-done.10.refs_0_.refs_6_), channel_id=1, source_target_pairs={{0,48},{16,0},{32,16},{48,32},{1,49},{17,1},{33,17},{49,33},{2,50}... | collective-permute-start | bytes 1622024 | tf_op jit(solution)/shard_map/ppermute | solution.py:21
  84.5 12.8 %collective-permute-start.18 = (bf16[64,4224]{1,0:T(8,128)(2,1)}, bf16[64,4224]{1,0:T(8,128)(2,1)S(1)}, u32[]{:S(2)}, u32[]{:S(2)}) collective-permute-start(bf16[64,4224]{1,0:T(8,128)(2,1)} %collective-permute-done.12.refs_2_.refs_8_), channel_id=1, source_target_pairs={{0,192},{64,0},{128,64},{192,128},{1,193},{65,1},{129,65},{193,129... | collective-permute-start | bytes 1622024 | tf_op jit(solution)/shard_map/ppermute | solution.py:21
  88.7 0.8 copy-start.6
  89.5 0.8 copy-start.7
  97.2 44.6 %collective-permute-start.16 = (bf16[8,192,512]{2,1,0:T(8,128)(2,1)}, bf16[8,192,512]{2,1,0:T(8,128)(2,1)}, u32[]{:S(2)}, u32[]{:S(2)}) collective-permute-start(bf16[8,192,512]{2,1,0:T(8,128)(2,1)} %bitcast.14.own_ref), channel_id=1, source_target_pairs={{0,8},{8,0},{1,9},{9,1},{2,10},{10,2},{3,11},{11,3},{4,12},{12,4},... | collective-permute-start | bytes 4718600 | tf_op jit(solution)/shard_map/ppermute | solution.py:21
  102.9 9.6 %collective-permute-start.19 = (bf16[384,384]{1,0:T(8,128)(2,1)S(1)}, bf16[384,384]{1,0:T(8,128)(2,1)S(1)}, u32[]{:S(2)}, u32[]{:S(2)}) collective-permute-start(bf16[384,384]{1,0:T(8,128)(2,1)S(1)} %pad_maximum_fusion.2.refs_0_), channel_id=1, source_target_pairs={{0,7},{1,0},{2,1},{3,2},{4,3},{5,4},{6,5},{7,6},{8,15},{9,8},{10,9... | collective-permute-start | bytes 884744 | tf_op jit(solution)/shard_map/ppermute | solution.py:21
  105.6 10.6 %collective-permute-start.23 = (bf16[384,384]{1,0:T(8,128)(2,1)S(1)}, bf16[384,384]{1,0:T(8,128)(2,1)S(1)}, u32[]{:S(2)}, u32[]{:S(2)}) collective-permute-start(bf16[384,384]{1,0:T(8,128)(2,1)S(1)} %pad_maximum_fusion.2.refs_0_), channel_id=1, source_target_pairs={{0,1},{1,2},{2,3},{3,4},{4,5},{5,6},{6,7},{7,0},{8,9},{9,10},{10,1... | collective-permute-start | bytes 884744 | tf_op jit(solution)/shard_map/ppermute | solution.py:21
  112.5 9.8 %collective-permute-start.20 = (bf16[384,384]{1,0:T(8,128)(2,1)S(1)}, bf16[384,384]{1,0:T(8,128)(2,1)S(1)}, u32[]{:S(2)}, u32[]{:S(2)}) collective-permute-start(bf16[384,384]{1,0:T(8,128)(2,1)S(1)} %collective-permute-done.19.refs_1_), channel_id=1, source_target_pairs={{0,7},{1,0},{2,1},{3,2},{4,3},{5,4},{6,5},{7,6},{8,15},{9,8},{10,9... | collective-permute-start | bytes 884744 | tf_op jit(solution)/shard_map/ppermute | solution.py:21
  116.2 9.8 %collective-permute-start.24 = (bf16[384,384]{1,0:T(8,128)(2,1)S(1)}, bf16[384,384]{1,0:T(8,128)(2,1)S(1)}, u32[]{:S(2)}, u32[]{:S(2)}) collective-permute-start(bf16[384,384]{1,0:T(8,128)(2,1)S(1)} %collective-permute-done.23.refs_7_), channel_id=1, source_target_pairs={{0,1},{1,2},{2,3},{3,4},{4,5},{5,6},{6,7},{7,0},{8,9},{9,10},{10,1... | collective-permute-start | bytes 884744 | tf_op jit(solution)/shard_map/ppermute | solution.py:21
  122.3 8.9 %collective-permute-start.21 = (bf16[384,384]{1,0:T(8,128)(2,1)S(1)}, bf16[384,384]{1,0:T(8,128)(2,1)S(1)}, u32[]{:S(2)}, u32[]{:S(2)}) collective-permute-start(bf16[384,384]{1,0:T(8,128)(2,1)S(1)} %collective-permute-done.20.refs_2_), channel_id=1, source_target_pairs={{0,7},{1,0},{2,1},{3,2},{4,3},{5,4},{6,5},{7,6},{8,15},{9,8},{10,9... | collective-permute-start | bytes 884744 | tf_op jit(solution)/shard_map/ppermute | solution.py:21
  126.0 9.0 %collective-permute-start.25 = (bf16[384,384]{1,0:T(8,128)(2,1)S(1)}, bf16[384,384]{1,0:T(8,128)(2,1)S(1)}, u32[]{:S(2)}, u32[]{:S(2)}) collective-permute-start(bf16[384,384]{1,0:T(8,128)(2,1)S(1)} %collective-permute-done.24.refs_6_), channel_id=1, source_target_pairs={{0,1},{1,2},{2,3},{3,4},{4,5},{5,6},{6,7},{7,0},{8,9},{9,10},{10,1... | collective-permute-start | bytes 884744 | tf_op jit(solution)/shard_map/ppermute | solution.py:21
  131.3 6.4 %collective-permute-start.22 = (bf16[192,384]{1,0:T(8,128)(2,1)S(1)}, bf16[192,384]{1,0:T(8,128)(2,1)S(1)}, u32[]{:S(2)}, u32[]{:S(2)}) collective-permute-start(bf16[192,384]{1,0:T(8,128)(2,1)S(1)} %slice.52), channel_id=1, source_target_pairs={{0,7},{1,0},{2,1},{3,2},{4,3},{5,4},{6,5},{7,6},{8,15},{9,8},{10,9... | collective-permute-start | bytes 442376 | tf_op jit(solution)/shard_map/ppermute | solution.py:21
  135.1 6.7 %collective-permute-start.26 = (bf16[192,384]{1,0:T(8,128)(2,1)S(1)}, bf16[192,384]{1,0:T(8,128)(2,1)S(1)}, u32[]{:S(2)}, u32[]{:S(2)}) collective-permute-start(bf16[192,384]{1,0:T(8,128)(2,1)S(1)} %slice.53), channel_id=1, source_target_pairs={{0,1},{1,2},{2,3},{3,4},{4,5},{5,6},{6,7},{7,0},{8,9},{9,10},{10,1... | collective-permute-start | bytes 442376 | tf_op jit(solution)/shard_map/ppermute | solution.py:21
  147.3 16.4 %all-to-all-start.2 = ((bf16[16,48,512]{2,1,0:T(8,128)(2,1)}), bf16[16,48,512]{2,1,0:T(8,128)(2,1)S(1)}, u32[]{:S(2)}, u32[]{:S(2)}) async-start(bf16[16,48,512]{2,1,0:T(8,128)(2,1)} %bitcast.15), calls=%async_computation.2 | async-start | bytes 1572864 | tf_op jit(solution)/shard_map/all_to_all | solution.py:448
  154.0 15.6 %copy-start.9 = (s32[64]{0:T(128)S(1)}, s32[64]{0:T(128)}, u32[]{:S(2)}) copy-start(s32[64]{0:T(128)} %param.23) | copy-start | bytes 772
  165.1 17.8 %all-to-all-start.3 = ((bf16[8,64,512]{2,1,0:T(8,128)(2,1)}), bf16[8,64,512]{2,1,0:T(8,128)(2,1)S(1)}, u32[]{:S(2)}, u32[]{:S(2)}) async-start(bf16[8,64,512]{2,1,0:T(8,128)(2,1)} %broadcast_in_dim.18), calls=%async_computation.3 | async-start | bytes 1048576 | tf_op jit(solution)/shard_map/all_to_all | solution.py:39

commit v5 on v3

--- a/solution.py
+++ b/solution.py
@@ -93,16 +93,16 @@
             out_ref[:, j * hidden : (j + 1) * hidden] = packed.astype(BF)
 
 
-def expert_slots(pieces, masks, weights):
+def expert_slots(pieces, masks, weights, on_chip=False):
     hidden, depth = weights[0].shape
-    chunk = 1024
+    chunk = 2048
     steps = depth // chunk
     sizes = tuple(p.shape[0] for p in pieces)
     in_specs = [pl.BlockSpec((8, LANES), lambda k: (0, 0))]
     in_specs += [pl.BlockSpec((m, chunk), lambda k: (0, k)) for m in sizes]
     in_specs += [pl.BlockSpec((m, LANES), lambda k: (0, depth // LANES)) for m in sizes]
     in_specs += [pl.BlockSpec((hidden, chunk), lambda k: (0, k))] * 4
-    pieces, weights = in_hbm(pieces), in_hbm(weights)
+    pieces, weights = pieces if on_chip else in_hbm(pieces), in_hbm(weights)
     total = sum(sizes)
     slots = total // 8 * CAP
     return pl.pallas_call(
@@ -115,7 +115,7 @@
             pltpu.VMEM((total, chunk), BF),
             pltpu.VMEM((total, 4 * hidden), F32),
         ],
-        compiler_params=pltpu.CompilerParams(vmem_limit_bytes=20 << 20),
+        compiler_params=pltpu.CompilerParams(vmem_limit_bytes=28 << 20),
         cost_estimate=pl.CostEstimate(
             flops=8 * total * depth * hidden,
             bytes_accessed=8 * depth * hidden + 2 * total * depth,
@@ -443,7 +443,7 @@
     )
     more, down_own = lax.optimization_barrier((expert_slots(far, masks, weights), down_own))
     down_other = shift(down_own, "c", 1)
-    slots = jnp.concatenate([slots, more, expert_slots(opposite, masks, weights)], axis=0)
+    slots = jnp.concatenate([slots, more, expert_slots(opposite, masks, weights, on_chip=True)], axis=0)
     active = ring(slots, "z")
     place = jnp.stack([x, y, z]).astype(jnp.int32)
     result = lower(place, active, down_own, down_other, chips)

time: 184 us -> 183 us (level)
  waiting for transfers between devices: 64.2 us -> 69.6 us
  Pallas kernels: 33.4 us -> 30.5 us
  starting transfers between devices: 53 us -> 50.9 us
    ppermute x23, waiting for transfers between devices: 33.3 us -> 38.8 us  [shift(): lax.ppermute(values, axis, [(i, (i - step) % size) for i in range(size)])]
    pallas_call x3, Pallas kernels: 19.7 us -> 16.8 us  [expert_slots(): pl.pallas_call(functools.partial(expert_kernel, sizes, steps), grid=(step...]
  transfers between devices with their start and end apart: 30 -> 30, of which waited for: 13 -> 17; matrix products, arithmetic and copies ran while one was open for 1% -> 1% of each run, Pallas kernels for 11% -> 10%
where the time goes in v5:
time: 183 us
  waiting for transfers between devices  69.6 us (38%)
  starting transfers between devices  50.9 us (28%)
  Pallas kernels  30.5 us (17%)
  blocking collectives  26.4 us (14%)
  local copies, waits for them, and re-layouts  2.86 us (2%)
    ppermute x23, waiting for transfers between devices, shift(): lax.ppermute(values, axis, [(i, (i - step) % size) for i in range(size)])  38.8 us
    ppermute x23, starting transfers between devices, shift(): lax.ppermute(values, axis, [(i, (i - step) % size) for i in range(size)])  29.6 us
    all_to_all x1, blocking collectives, per_device(): lax.all_to_all(sent, 'z', 0, 0, tiled=True)  26.4 us
    pallas_call x3, Pallas kernels, expert_slots(): pl.pallas_call(functools.partial(expert_kernel, sizes, steps), grid=(step...  16.8 us
    all_to_all x1, waiting for transfers between devices, copies(): lax.all_to_all(jnp.broadcast_to(values[None], (size, *values.shape)), axi...  13.3 us
    all_to_all x1, waiting for transfers between devices, per_device(): returned = lax.all_to_all(result, ('x', 'y'), 0, 0, tiled=True)  9.59 us
    ppermute x4, waiting for transfers between devices, pairs(): return lax.ppermute(block, axis, [(i, i ^ mask) for i in range(4)])  7.96 us
    pallas_call x1, Pallas kernels, attend(): pl.pallas_call(attend_kernel, in_specs=[pl.BlockSpec(memory_space=pltpu.S...  7.29 us
  transfers between devices with their start and end apart: 30, of which 17 were waited for; matrix products, arithmetic and copies ran while one was open for 1% of the time, Pallas kernels for 10%

profile of v5, /device:TPU:8, one launch (start us, length us, event | category | flops | bytes accessed | tf_op | source)
XLA Modules:
  0.0 182.9 jit_solution(13461293232509454294)
XLA Ops:
  0.7 0.5 collective-permute-start.1
  1.2 1.0 prepare.1
  2.2 26.4 %all_to_all.31 = bf16[8,8,4224]{2,1,0:T(8,128)(2,1)S(1)} all-to-all(bf16[8,8,4224]{2,1,0:T(8,128)(2,1)S(1)} %prepare.1), channel_id=1, replica_groups=mesh['x'=4,'y'=4,'c'=2,'z'=8] {'z'}, dimensions={0} | all-to-all | bytes 1081344 | tf_op jit(solution)/shard_map/all_to_all | solution.py:404
  29.0 0.5 collective-permute-start.4
  29.6 1.5 collective-permute-start.2
  31.1 1.3 copy.22
  32.4 4.3 %all-to-all-start.1 = ((bf16[192,8,512]{2,0,1:T(8,128)(2,1)}), bf16[192,8,512]{2,0,1:T(8,128)(2,1)}, u32[]{:S(2)}, u32[]{:S(2)}) async-start(bf16[192,8,512]{2,0,1:T(8,128)(2,1)} %bitcast.24), calls=%async_computation.1 | async-start | bytes 3145728 | tf_op jit(solution)/shard_map/all_to_all | solution.py:407
  36.8 2.5 %collective-permute-start.5 = (bf16[64,4224]{1,0:T(8,128)(2,1)S(1)}, bf16[64,4224]{1,0:T(8,128)(2,1)}, u32[]{:S(2)}, u32[]{:S(2)}) collective-permute-start(bf16[64,4224]{1,0:T(8,128)(2,1)S(1)} %pad_maximum_fusion.1.refs_2_.refs_10_), channel_id=1, source_target_pairs={{0,48},{16,32},{32,16},{48,0},{1,49},{17,33},{33,17},{49,1},{2,50}... | collective-permute-start | bytes 1622024 | tf_op jit(solution)/shard_map/ppermute | solution.py:424
  39.3 2.2 %collective-permute-start.3 = (bf16[64,4224]{1,0:T(8,128)(2,1)S(1)}, bf16[64,4224]{1,0:T(8,128)(2,1)}, u32[]{:S(2)}, u32[]{:S(2)}) collective-permute-start(bf16[64,4224]{1,0:T(8,128)(2,1)S(1)} %pad_maximum_fusion.refs_0_.refs_8_), channel_id=1, source_target_pairs={{0,192},{64,128},{128,64},{192,0},{1,193},{65,129},{129,65},{193,1... | collective-permute-start | bytes 1622024 | tf_op jit(solution)/shard_map/ppermute | solution.py:424
  41.5 0.6 collective-permute-start.9
  42.1 2.9 %collective-permute-start.8 = (bf16[64,4224]{1,0:T(8,128)(2,1)S(1)}, bf16[64,4224]{1,0:T(8,128)(2,1)S(1)}, u32[]{:S(2)}, u32[]{:S(2)}) collective-permute-start(bf16[64,4224]{1,0:T(8,128)(2,1)S(1)} %pad_maximum_fusion.1.refs_2_.refs_10_), channel_id=1, source_target_pairs={{0,192},{64,0},{128,64},{192,128},{1,193},{65,1},{129,65},{193,129... | collective-permute-start | bytes 1622024 | tf_op jit(solution)/shard_map/ppermute | solution.py:21
  45.0 7.0 %collective-permute-done.5.refs_3_.refs_11_ = bf16[64,4224]{1,0:T(8,128)(2,1)} collective-permute-done((bf16[64,4224]{1,0:T(8,128)(2,1)S(1)}, bf16[64,4224]{1,0:T(8,128)(2,1)}, u32[]{:S(2)}, u32[]{:S(2)}) %collective-permute-start.5) | collective-permute-done | bytes 540704 | tf_op jit(solution)/shard_map/ppermute | solution.py:424
  52.0 3.0 %collective-permute-start.6 = (bf16[64,4224]{1,0:T(8,128)(2,1)S(1)}, bf16[64,4224]{1,0:T(8,128)(2,1)}, u32[]{:S(2)}, u32[]{:S(2)}) collective-permute-start(bf16[64,4224]{1,0:T(8,128)(2,1)S(1)} %pad_maximum_fusion.refs_0_.refs_8_), channel_id=1, source_target_pairs={{0,48},{16,0},{32,16},{48,32},{1,49},{17,1},{33,17},{49,33},{2,50}... | collective-permute-start | bytes 1622024 | tf_op jit(solution)/shard_map/ppermute | solution.py:21
  55.0 1.0 collective-permute-done.3.refs_1_.refs_9_
  55.9 2.1 %collective-permute-start.12 = (bf16[64,4224]{1,0:T(8,128)(2,1)}, bf16[64,4224]{1,0:T(8,128)(2,1)}, u32[]{:S(2)}, u32[]{:S(2)}) collective-permute-start(bf16[64,4224]{1,0:T(8,128)(2,1)} %collective-permute-done.5.refs_3_.refs_11_), channel_id=1, source_target_pairs={{0,192},{64,0},{128,64},{192,128},{1,193},{65,1},{129,65},{193,129... | collective-permute-start | bytes 1622024 | tf_op jit(solution)/shard_map/ppermute | solution.py:21
  58.0 6.3 %collective-permute-done.9.refs_7_.refs_15_ = bf16[64,4224]{1,0:T(8,128)(2,1)S(1)} collective-permute-done((bf16[64,4224]{1,0:T(8,128)(2,1)S(1)}, bf16[64,4224]{1,0:T(8,128)(2,1)S(1)}, u32[]{:S(2)}, u32[]{:S(2)}) %collective-permute-start.9) | collective-permute-done | bytes 540704 | tf_op jit(solution)/shard_map/ppermute | solution.py:21
  64.4 1.4 collective-permute-start.10
  65.8 0.6 collective-permute-start.11
  66.7 1.7 collective-permute-start.17
  68.4 7.2 %expert_slots.3 = bf16[192,384]{1,0:T(8,128)(2,1)S(1)} custom-call(bf16[8,128]{1,0:T(8,128)(2,1)S(1)} %convert_convert_fusion.mask_ref, bf16[64,4224]{1,0:T(8,128)(2,1)} %copy-done.2, bf16[64,4224]{1,0:T(8,128)(2,1)} %collective-permute-done.3.refs_1_.refs_9_, bf16[64,4224]{1,0:T(8,128)(2,1)} %copy-done.1, ...), custom_call_target="tpu_custom_call" | custom-call | flops 3221225472 | bytes 10485760 | tf_op jit(solution)/shard_map/expert_slots/pallas_call | solution.py:108
  75.6 0.7 collective-permute-start.15
  76.3 4.8 %collective-permute-done.13.refs_3_.refs_7_ = bf16[64,4224]{1,0:T(8,128)(2,1)} collective-permute-done((bf16[64,4224]{1,0:T(8,128)(2,1)}, bf16[64,4224]{1,0:T(8,128)(2,1)}, u32[]{:S(2)}, u32[]{:S(2)}) %collective-permute-start.13) | collective-permute-done | bytes 540704 | tf_op jit(solution)/shard_map/ppermute | solution.py:21
  81.1 1.4 collective-permute-start.16
  82.4 0.6 collective-permute-start.18
  83.0 5.0 %expert_slots.4 = bf16[96,384]{1,0:T(8,128)(2,1)S(1)} custom-call(bf16[8,128]{1,0:T(8,128)(2,1)S(1)} %convert_convert_fusion.mask_ref, bf16[64,4224]{1,0:T(8,128)(2,1)} %collective-permute-done.10.refs_0_.refs_4_, bf16[64,4224]{1,0:T(8,128)(2,1)} %collective-permute-done.11.refs_1_.refs_5_, bf16[64,4224]{1,0:T(8,128)(2,1)} %collective-permute-done.12.refs_2_.refs_6_, ...), custom_call_target="tpu_custom_call" | custom-call | flops 1610612736 | bytes 8388608 | tf_op jit(solution)/shard_map/expert_slots/pallas_call | solution.py:108
  88.1 0.6 collective-permute-done.17.refs_2_.refs_6_
  88.7 2.0 %collective-permute-done.16.refs_1_.refs_5_ = bf16[64,4224]{1,0:T(8,128)(2,1)S(1)} collective-permute-done((bf16[64,4224]{1,0:T(8,128)(2,1)}, bf16[64,4224]{1,0:T(8,128)(2,1)S(1)}, u32[]{:S(2)}, u32[]{:S(2)}) %collective-permute-start.16) | collective-permute-done | bytes 540704 | tf_op jit(solution)/shard_map/ppermute | solution.py:21
  90.7 1.3 collective-permute-done.18.refs_3_.refs_7_
  92.0 4.6 %expert_slots.5 = bf16[96,384]{1,0:T(8,128)(2,1)S(1)} custom-call(bf16[8,128]{1,0:T(8,128)(2,1)S(1)} %convert_convert_fusion.mask_ref, bf16[64,4224]{1,0:T(8,128)(2,1)S(1)} %collective-permute-done.15.refs_0_.refs_4_, bf16[64,4224]{1,0:T(8,128)(2,1)S(1)} %collective-permute-done.16.refs_1_.refs_5_, ...), custom_call_target="tpu_custom_call" | custom-call | flops 1610612736 | bytes 8388608 | tf_op jit(solution)/shard_map/expert_slots/pallas_call | solution.py:108
  96.7 2.9 %collective-permute-start.19 = (bf16[384,384]{1,0:T(8,128)(2,1)S(1)}, bf16[384,384]{1,0:T(8,128)(2,1)S(1)}, u32[]{:S(2)}, u32[]{:S(2)}) collective-permute-start(bf16[384,384]{1,0:T(8,128)(2,1)S(1)} %pad_maximum_fusion.2.refs_0_), channel_id=1, source_target_pairs={{0,7},{1,0},{2,1},{3,2},{4,3},{5,4},{6,5},{7,6},{8,15},{9,8},{10,9... | collective-permute-start | bytes 884744 | tf_op jit(solution)/shard_map/ppermute | solution.py:21
  99.6 5.2 %collective-permute-done.19.refs_1_ = bf16[384,384]{1,0:T(8,128)(2,1)S(1)} collective-permute-done((bf16[384,384]{1,0:T(8,128)(2,1)S(1)}, bf16[384,384]{1,0:T(8,128)(2,1)S(1)}, u32[]{:S(2)}, u32[]{:S(2)}) %collective-permute-start.19) | collective-permute-done | bytes 294944 | tf_op jit(solution)/shard_map/ppermute | solution.py:21
  104.9 3.5 %collective-permute-start.20 = (bf16[384,384]{1,0:T(8,128)(2,1)S(1)}, bf16[384,384]{1,0:T(8,128)(2,1)S(1)}, u32[]{:S(2)}, u32[]{:S(2)}) collective-permute-start(bf16[384,384]{1,0:T(8,128)(2,1)S(1)} %collective-permute-done.19.refs_1_), channel_id=1, source_target_pairs={{0,7},{1,0},{2,1},{3,2},{4,3},{5,4},{6,5},{7,6},{8,15},{9,8},{10,9... | collective-permute-start | bytes 884744 | tf_op jit(solution)/shard_map/ppermute | solution.py:21
  108.7 5.9 %collective-permute-done.20.refs_2_ = bf16[384,384]{1,0:T(8,128)(2,1)S(1)} collective-permute-done((bf16[384,384]{1,0:T(8,128)(2,1)S(1)}, bf16[384,384]{1,0:T(8,128)(2,1)S(1)}, u32[]{:S(2)}, u32[]{:S(2)}) %collective-permute-start.20) | collective-permute-done | bytes 294944 | tf_op jit(solution)/shard_map/ppermute | solution.py:21
  114.6 3.7 %collective-permute-start.21 = (bf16[384,384]{1,0:T(8,128)(2,1)S(1)}, bf16[384,384]{1,0:T(8,128)(2,1)S(1)}, u32[]{:S(2)}, u32[]{:S(2)}) collective-permute-start(bf16[384,384]{1,0:T(8,128)(2,1)S(1)} %collective-permute-done.20.refs_2_), channel_id=1, source_target_pairs={{0,7},{1,0},{2,1},{3,2},{4,3},{5,4},{6,5},{7,6},{8,15},{9,8},{10,9... | collective-permute-start | bytes 884744 | tf_op jit(solution)/shard_map/ppermute | solution.py:21
  118.3 0.6 collective-permute-done.24.refs_6_
  119.0 5.1 %collective-permute-done.21.refs_3_ = bf16[384,384]{1,0:T(8,128)(2,1)S(1)} collective-permute-done((bf16[384,384]{1,0:T(8,128)(2,1)S(1)}, bf16[384,384]{1,0:T(8,128)(2,1)S(1)}, u32[]{:S(2)}, u32[]{:S(2)}) %collective-permute-start.21) | collective-permute-done | bytes 294944 | tf_op jit(solution)/shard_map/ppermute | solution.py:21
  124.1 3.8 %collective-permute-start.22 = (bf16[192,384]{1,0:T(8,128)(2,1)S(1)}, bf16[192,384]{1,0:T(8,128)(2,1)S(1)}, u32[]{:S(2)}, u32[]{:S(2)}) collective-permute-start(bf16[192,384]{1,0:T(8,128)(2,1)S(1)} %slice.52), channel_id=1, source_target_pairs={{0,7},{1,0},{2,1},{3,2},{4,3},{5,4},{6,5},{7,6},{8,15},{9,8},{10,9... | collective-permute-start | bytes 442376 | tf_op jit(solution)/shard_map/ppermute | solution.py:21
  127.9 0.3 collective-permute-done.25.refs_5_
  128.4 2.1 %collective-permute-done.22 = bf16[192,384]{1,0:T(8,128)(2,1)S(1)} collective-permute-done((bf16[192,384]{1,0:T(8,128)(2,1)S(1)}, bf16[192,384]{1,0:T(8,128)(2,1)S(1)}, u32[]{:S(2)}, u32[]{:S(2)}) %collective-permute-start.22) | collective-permute-done | bytes 147488 | tf_op jit(solution)/shard_map/ppermute | solution.py:21
  130.6 4.1 %collective-permute-done.26 = bf16[192,384]{1,0:T(8,128)(2,1)S(1)} collective-permute-done((bf16[192,384]{1,0:T(8,128)(2,1)S(1)}, bf16[192,384]{1,0:T(8,128)(2,1)S(1)}, u32[]{:S(2)}, u32[]{:S(2)}) %collective-permute-start.26) | collective-permute-done | bytes 147488 | tf_op jit(solution)/shard_map/ppermute | solution.py:21
  134.7 5.5 %lower.1 = bf16[16,2,24,512]{3,2,1,0:T(8,128)(2,1)} custom-call(s32[3]{0:T(128)S(1)} %pad_add_fusion.place_ref, bf16[8,192,512]{2,1,0:T(8,128)(2,1)} %bitcast.14.own_ref, bf16[8,192,512]{2,1,0:T(8,128)(2,1)} %collective-permute-done.14.other_ref, bf16[384,384]{1,0:T(8,128)(2,1)S(1)} %pad_maximum_fusion.2.refs_0_, ...), custom_call_target="tpu_custom_call" | custom-call | flops 1207959552 | bytes 5505024 | tf_op jit(solution)/shard_map/lower/pallas_call | solution.py:180
  140.2 5.8 %all-to-all-start.2 = ((bf16[16,48,512]{2,1,0:T(8,128)(2,1)}), bf16[16,48,512]{2,1,0:T(8,128)(2,1)S(1)}, u32[]{:S(2)}, u32[]{:S(2)}) async-start(bf16[16,48,512]{2,1,0:T(8,128)(2,1)} %bitcast.15), calls=%async_computation.2 | async-start | bytes 1572864 | tf_op jit(solution)/shard_map/all_to_all | solution.py:452
  146.6 9.6 %all-to-all-done.2 = bf16[16,48,512]{2,1,0:T(8,128)(2,1)S(1)} async-done(((bf16[16,48,512]{2,1,0:T(8,128)(2,1)}), bf16[16,48,512]{2,1,0:T(8,128)(2,1)S(1)}, u32[]{:S(2)}, u32[]{:S(2)}) %all-to-all-start.2) | async-done | bytes 786464 | tf_op jit(solution)/shard_map/all_to_all | solution.py:452
  156.2 0.5 fusion
  156.7 0.8 broadcast_in_dim.18
  157.5 4.5 %all-to-all-start.3 = ((bf16[8,64,512]{2,1,0:T(8,128)(2,1)}), bf16[8,64,512]{2,1,0:T(8,128)(2,1)S(1)}, u32[]{:S(2)}, u32[]{:S(2)}) async-start(bf16[8,64,512]{2,1,0:T(8,128)(2,1)} %broadcast_in_dim.18), calls=%async_computation.3 | async-start | bytes 1048576 | tf_op jit(solution)/shard_map/all_to_all | solution.py:39
  162.1 13.3 %all-to-all-done.3.stream_ref = bf16[8,64,512]{2,1,0:T(8,128)(2,1)S(1)} async-done(((bf16[8,64,512]{2,1,0:T(8,128)(2,1)}), bf16[8,64,512]{2,1,0:T(8,128)(2,1)S(1)}, u32[]{:S(2)}, u32[]{:S(2)}) %all-to-all-start.3) | async-done | bytes 524320 | tf_op jit(solution)/shard_map/all_to_all | solution.py:39
  175.5 7.3 %attend.1 = (bf16[8,4096]{1,0:T(8,128)(2,1)}, bf16[64,512]{1,0:T(8,128)(2,1)}) custom-call(s32[3]{0:T(128)S(1)} %pad_add_fusion.place_ref, bf16[8,64,512]{2,1,0:T(8,128)(2,1)S(1)} %all-to-all-done.3.stream_ref, bf16[4096,512]{1,0:T(8,128)(2,1)} %wq_ref.1, bf16[4096,128]{1,0:T(8,128)(2,1)} %wk_ref.1, bf16[4096,128]{1,0:T(8,128)(2,1)} %wv_ref.1, ...), custom_call_target="tpu_custom_call" | custom-call | flops 402653184 | bytes 6291456 | tf_op jit(solution)/shard_map/attend/pallas_call | solution.py:285
  (69 shorter events, 2.3 us)
Async XLA Ops:
  0.6 28.0 %collective-permute-start = (bf16[192,4096]{1,0:T(8,128)(2,1)}, bf16[192,4096]{1,0:T(8,128)(2,1)S(1)}, u32[]{:S(2)}, u32[]{:S(2)}) collective-permute-start(bf16[192,4096]{1,0:T(8,128)(2,1)} %bitcast.31), channel_id=1, source_target_pairs={{0,8},{8,0},{1,9},{9,1},{2,10},{10,2},{3,11},{11,3},{4,12},{12,4},... | collective-permute-start | bytes 4718600 | tf_op jit(solution)/shard_map/ppermute | solution.py:21
  0.7 27.9 %collective-permute-start.1 = (bf16[192,4096]{1,0:T(8,128)(2,1)}, bf16[192,4096]{1,0:T(8,128)(2,1)}, u32[]{:S(2)}, u32[]{:S(2)}) collective-permute-start(bf16[192,4096]{1,0:T(8,128)(2,1)} %bitcast.35), channel_id=1, source_target_pairs={{0,8},{8,0},{1,9},{9,1},{2,10},{10,2},{3,11},{11,3},{4,12},{12,4},... | collective-permute-start | bytes 4718600 | tf_op jit(solution)/shard_map/ppermute | solution.py:21
  28.6 2.5 %copy-start.6 = (bf16[1,192,4096]{2,1,0:T(8,128)(2,1)S(1)}, bf16[1,192,4096]{2,1,0:T(8,128)(2,1)}, u32[]{:S(2)}) copy-start(bf16[1,192,4096]{2,1,0:T(8,128)(2,1)} %param.17) | copy-start | bytes 4718596
  28.6 3.8 %copy-start = (bf16[192,4096]{1,0:T(8,128)(2,1)}, bf16[192,4096]{1,0:T(8,128)(2,1)S(1)}, u32[]{:S(2)}) copy-start(bf16[192,4096]{1,0:T(8,128)(2,1)S(1)} %collective-permute-done.refs_18_.refs_10_) | copy-start | bytes 4718596
  29.0 7.7 %collective-permute-start.4 = (bf16[32,4224]{1,0:T(8,128)(2,1)S(1)}, bf16[32,4224]{1,0:T(8,128)(2,1)S(1)}, u32[]{:S(2)}, u32[]{:S(2)}) collective-permute-start(bf16[32,4224]{1,0:T(8,128)(2,1)S(1)} %get-tuple-element.24), channel_id=1, source_target_pairs={{0,16},{16,0},{32,48},{48,32},{1,17},{17,1},{33,49},{49,33},{2,18}... | collective-permute-start | bytes 811016 | tf_op jit(solution)/shard_map/ppermute | solution.py:424
  29.6 9.7 %collective-permute-start.2 = (bf16[32,4224]{1,0:T(8,128)(2,1)S(1)}, bf16[32,4224]{1,0:T(8,128)(2,1)S(1)}, u32[]{:S(2)}, u32[]{:S(2)}) collective-permute-start(bf16[32,4224]{1,0:T(8,128)(2,1)S(1)} %get-tuple-element.25), channel_id=1, source_target_pairs={{0,64},{64,0},{128,192},{192,128},{1,65},{65,1},{129,193},{193,129... | collective-permute-start | bytes 811016 | tf_op jit(solution)/shard_map/ppermute | solution.py:424
  32.4 55.6 %all-to-all-start.1 = ((bf16[192,8,512]{2,0,1:T(8,128)(2,1)}), bf16[192,8,512]{2,0,1:T(8,128)(2,1)}, u32[]{:S(2)}, u32[]{:S(2)}) async-start(bf16[192,8,512]{2,0,1:T(8,128)(2,1)} %bitcast.24), calls=%async_computation.1 | async-start | bytes 3145728 | tf_op jit(solution)/shard_map/all_to_all | solution.py:407
  36.8 31.6 %copy-start.1 = (bf16[64,4224]{1,0:T(8,128)(2,1)}, bf16[64,4224]{1,0:T(8,128)(2,1)S(1)}, u32[]{:S(2)}) copy-start(bf16[64,4224]{1,0:T(8,128)(2,1)S(1)} %pad_maximum_fusion.1.refs_2_.refs_10_) | copy-start | bytes 1622020
  36.8 15.2 %collective-permute-start.5 = (bf16[64,4224]{1,0:T(8,128)(2,1)S(1)}, bf16[64,4224]{1,0:T(8,128)(2,1)}, u32[]{:S(2)}, u32[]{:S(2)}) collective-permute-start(bf16[64,4224]{1,0:T(8,128)(2,1)S(1)} %pad_maximum_fusion.1.refs_2_.refs_10_), channel_id=1, source_target_pairs={{0,48},{16,32},{32,16},{48,0},{1,49},{17,33},{33,17},{49,1},{2,50}... | collective-permute-start | bytes 1622024 | tf_op jit(solution)/shard_map/ppermute | solution.py:424
  39.3 29.1 %copy-start.2 = (bf16[64,4224]{1,0:T(8,128)(2,1)}, bf16[64,4224]{1,0:T(8,128)(2,1)S(1)}, u32[]{:S(2)}) copy-start(bf16[64,4224]{1,0:T(8,128)(2,1)S(1)} %pad_maximum_fusion.refs_0_.refs_8_) | copy-start | bytes 1622020
  39.3 16.6 %collective-permute-start.3 = (bf16[64,4224]{1,0:T(8,128)(2,1)S(1)}, bf16[64,4224]{1,0:T(8,128)(2,1)}, u32[]{:S(2)}, u32[]{:S(2)}) collective-permute-start(bf16[64,4224]{1,0:T(8,128)(2,1)S(1)} %pad_maximum_fusion.refs_0_.refs_8_), channel_id=1, source_target_pairs={{0,192},{64,128},{128,64},{192,0},{1,193},{65,129},{129,65},{193,1... | collective-permute-start | bytes 1622024 | tf_op jit(solution)/shard_map/ppermute | solution.py:424
  41.5 22.8 %collective-permute-start.9 = (bf16[64,4224]{1,0:T(8,128)(2,1)S(1)}, bf16[64,4224]{1,0:T(8,128)(2,1)S(1)}, u32[]{:S(2)}, u32[]{:S(2)}) collective-permute-start(bf16[64,4224]{1,0:T(8,128)(2,1)S(1)} %pad_maximum_fusion.1.refs_2_.refs_10_), channel_id=1, source_target_pairs={{0,64},{64,128},{128,192},{192,0},{1,65},{65,129},{129,193},{193,1... | collective-permute-start | bytes 1622024 | tf_op jit(solution)/shard_map/ppermute | solution.py:21
  42.1 22.3 %collective-permute-start.7 = (bf16[64,4224]{1,0:T(8,128)(2,1)S(1)}, bf16[64,4224]{1,0:T(8,128)(2,1)S(1)}, u32[]{:S(2)}, u32[]{:S(2)}) collective-permute-start(bf16[64,4224]{1,0:T(8,128)(2,1)S(1)} %pad_maximum_fusion.refs_0_.refs_8_), channel_id=1, source_target_pairs={{0,16},{16,32},{32,48},{48,0},{1,17},{17,33},{33,49},{49,1},{2,18}... | collective-permute-start | bytes 1622024 | tf_op jit(solution)/shard_map/ppermute | solution.py:21
  42.1 23.7 %collective-permute-start.8 = (bf16[64,4224]{1,0:T(8,128)(2,1)S(1)}, bf16[64,4224]{1,0:T(8,128)(2,1)S(1)}, u32[]{:S(2)}, u32[]{:S(2)}) collective-permute-start(bf16[64,4224]{1,0:T(8,128)(2,1)S(1)} %pad_maximum_fusion.1.refs_2_.refs_10_), channel_id=1, source_target_pairs={{0,192},{64,0},{128,64},{192,128},{1,193},{65,1},{129,65},{193,129... | collective-permute-start | bytes 1622024 | tf_op jit(solution)/shard_map/ppermute | solution.py:21
  52.0 14.7 %collective-permute-start.6 = (bf16[64,4224]{1,0:T(8,128)(2,1)S(1)}, bf16[64,4224]{1,0:T(8,128)(2,1)}, u32[]{:S(2)}, u32[]{:S(2)}) collective-permute-start(bf16[64,4224]{1,0:T(8,128)(2,1)S(1)} %pad_maximum_fusion.refs_0_.refs_8_), channel_id=1, source_target_pairs={{0,48},{16,0},{32,16},{48,32},{1,49},{17,1},{33,17},{49,33},{2,50}... | collective-permute-start | bytes 1622024 | tf_op jit(solution)/shard_map/ppermute | solution.py:21
  55.9 19.6 %collective-permute-start.12 = (bf16[64,4224]{1,0:T(8,128)(2,1)}, bf16[64,4224]{1,0:T(8,128)(2,1)}, u32[]{:S(2)}, u32[]{:S(2)}) collective-permute-start(bf16[64,4224]{1,0:T(8,128)(2,1)} %collective-permute-done.5.refs_3_.refs_11_), channel_id=1, source_target_pairs={{0,192},{64,0},{128,64},{192,128},{1,193},{65,1},{129,65},{193,129... | collective-permute-start | bytes 1622024 | tf_op jit(solution)/shard_map/ppermute | solution.py:21
  64.4 4.1 %copy-start.3 = (bf16[64,4224]{1,0:T(8,128)(2,1)}, bf16[64,4224]{1,0:T(8,128)(2,1)S(1)}, u32[]{:S(2)}) copy-start(bf16[64,4224]{1,0:T(8,128)(2,1)S(1)} %collective-permute-done.9.refs_7_.refs_15_) | copy-start | bytes 1622020
  64.4 16.7 %collective-permute-start.13 = (bf16[64,4224]{1,0:T(8,128)(2,1)}, bf16[64,4224]{1,0:T(8,128)(2,1)}, u32[]{:S(2)}, u32[]{:S(2)}) collective-permute-start(bf16[64,4224]{1,0:T(8,128)(2,1)} %collective-permute-done.5.refs_3_.refs_11_), channel_id=1, source_target_pairs={{0,64},{64,128},{128,192},{192,0},{1,65},{65,129},{129,193},{193,1... | collective-permute-start | bytes 1622024 | tf_op jit(solution)/shard_map/ppermute | solution.py:21
  64.4 4.1 %copy-start.4 = (bf16[64,4224]{1,0:T(8,128)(2,1)}, bf16[64,4224]{1,0:T(8,128)(2,1)S(1)}, u32[]{:S(2)}) copy-start(bf16[64,4224]{1,0:T(8,128)(2,1)S(1)} %collective-permute-done.7.refs_5_.refs_13_) | copy-start | bytes 1622020
  64.4 16.7 %collective-permute-start.10 = (bf16[64,4224]{1,0:T(8,128)(2,1)}, bf16[64,4224]{1,0:T(8,128)(2,1)}, u32[]{:S(2)}, u32[]{:S(2)}) collective-permute-start(bf16[64,4224]{1,0:T(8,128)(2,1)} %collective-permute-done.3.refs_1_.refs_9_), channel_id=1, source_target_pairs={{0,48},{16,0},{32,16},{48,32},{1,49},{17,1},{33,17},{49,33},{2,50}... | collective-permute-start | bytes 1622024 | tf_op jit(solution)/shard_map/ppermute | solution.py:21
  65.8 0.9 copy-start.5
  65.8 15.3 %collective-permute-start.11 = (bf16[64,4224]{1,0:T(8,128)(2,1)}, bf16[64,4224]{1,0:T(8,128)(2,1)}, u32[]{:S(2)}, u32[]{:S(2)}) collective-permute-start(bf16[64,4224]{1,0:T(8,128)(2,1)} %collective-permute-done.3.refs_1_.refs_9_), channel_id=1, source_target_pairs={{0,16},{16,32},{32,48},{48,0},{1,17},{17,33},{33,49},{49,1},{2,18}... | collective-permute-start | bytes 1622024 | tf_op jit(solution)/shard_map/ppermute | solution.py:21
  66.7 21.9 %collective-permute-start.17 = (bf16[64,4224]{1,0:T(8,128)(2,1)S(1)}, bf16[64,4224]{1,0:T(8,128)(2,1)S(1)}, u32[]{:S(2)}, u32[]{:S(2)}) collective-permute-start(bf16[64,4224]{1,0:T(8,128)(2,1)S(1)} %collective-permute-done.9.refs_7_.refs_15_), channel_id=1, source_target_pairs={{0,64},{64,128},{128,192},{192,0},{1,65},{65,129},{129,193},{193,1... | collective-permute-start | bytes 1622024 | tf_op jit(solution)/shard_map/ppermute | solution.py:21
  75.6 13.1 %collective-permute-start.15 = (bf16[64,4224]{1,0:T(8,128)(2,1)}, bf16[64,4224]{1,0:T(8,128)(2,1)S(1)}, u32[]{:S(2)}, u32[]{:S(2)}) collective-permute-start(bf16[64,4224]{1,0:T(8,128)(2,1)} %copy-done.4), channel_id=1, source_target_pairs={{0,16},{16,32},{32,48},{48,0},{1,17},{17,33},{33,49},{49,1},{2,18}... | collective-permute-start | bytes 1622024 | tf_op jit(solution)/shard_map/ppermute | solution.py:21
  81.1 9.6 %collective-permute-start.16 = (bf16[64,4224]{1,0:T(8,128)(2,1)}, bf16[64,4224]{1,0:T(8,128)(2,1)S(1)}, u32[]{:S(2)}, u32[]{:S(2)}) collective-permute-start(bf16[64,4224]{1,0:T(8,128)(2,1)} %collective-permute-done.10.refs_0_.refs_4_), channel_id=1, source_target_pairs={{0,48},{16,0},{32,16},{48,32},{1,49},{17,1},{33,17},{49,33},{2,50}... | collective-permute-start | bytes 1622024 | tf_op jit(solution)/shard_map/ppermute | solution.py:21
  82.4 9.6 %collective-permute-start.18 = (bf16[64,4224]{1,0:T(8,128)(2,1)}, bf16[64,4224]{1,0:T(8,128)(2,1)S(1)}, u32[]{:S(2)}, u32[]{:S(2)}) collective-permute-start(bf16[64,4224]{1,0:T(8,128)(2,1)} %collective-permute-done.12.refs_2_.refs_6_), channel_id=1, source_target_pairs={{0,192},{64,0},{128,64},{192,128},{1,193},{65,1},{129,65},{193,129... | collective-permute-start | bytes 1622024 | tf_op jit(solution)/shard_map/ppermute | solution.py:21
  88.0 46.7 %collective-permute-start.14 = (bf16[8,192,512]{2,1,0:T(8,128)(2,1)}, bf16[8,192,512]{2,1,0:T(8,128)(2,1)}, u32[]{:S(2)}, u32[]{:S(2)}) collective-permute-start(bf16[8,192,512]{2,1,0:T(8,128)(2,1)} %bitcast.14.own_ref), channel_id=1, source_target_pairs={{0,8},{8,0},{1,9},{9,1},{2,10},{10,2},{3,11},{11,3},{4,12},{12,4},... | collective-permute-start | bytes 4718600 | tf_op jit(solution)/shard_map/ppermute | solution.py:21
  96.7 8.2 %collective-permute-start.19 = (bf16[384,384]{1,0:T(8,128)(2,1)S(1)}, bf16[384,384]{1,0:T(8,128)(2,1)S(1)}, u32[]{:S(2)}, u32[]{:S(2)}) collective-permute-start(bf16[384,384]{1,0:T(8,128)(2,1)S(1)} %pad_maximum_fusion.2.refs_0_), channel_id=1, source_target_pairs={{0,7},{1,0},{2,1},{3,2},{4,3},{5,4},{6,5},{7,6},{8,15},{9,8},{10,9... | collective-permute-start | bytes 884744 | tf_op jit(solution)/shard_map/ppermute | solution.py:21
  99.6 9.0 %collective-permute-start.23 = (bf16[384,384]{1,0:T(8,128)(2,1)S(1)}, bf16[384,384]{1,0:T(8,128)(2,1)S(1)}, u32[]{:S(2)}, u32[]{:S(2)}) collective-permute-start(bf16[384,384]{1,0:T(8,128)(2,1)S(1)} %pad_maximum_fusion.2.refs_0_), channel_id=1, source_target_pairs={{0,1},{1,2},{2,3},{3,4},{4,5},{5,6},{6,7},{7,0},{8,9},{9,10},{10,1... | collective-permute-start | bytes 884744 | tf_op jit(solution)/shard_map/ppermute | solution.py:21
  104.9 9.7 %collective-permute-start.20 = (bf16[384,384]{1,0:T(8,128)(2,1)S(1)}, bf16[384,384]{1,0:T(8,128)(2,1)S(1)}, u32[]{:S(2)}, u32[]{:S(2)}) collective-permute-start(bf16[384,384]{1,0:T(8,128)(2,1)S(1)} %collective-permute-done.19.refs_1_), channel_id=1, source_target_pairs={{0,7},{1,0},{2,1},{3,2},{4,3},{5,4},{6,5},{7,6},{8,15},{9,8},{10,9... | collective-permute-start | bytes 884744 | tf_op jit(solution)/shard_map/ppermute | solution.py:21
  108.7 10.2 %collective-permute-start.24 = (bf16[384,384]{1,0:T(8,128)(2,1)S(1)}, bf16[384,384]{1,0:T(8,128)(2,1)S(1)}, u32[]{:S(2)}, u32[]{:S(2)}) collective-permute-start(bf16[384,384]{1,0:T(8,128)(2,1)S(1)} %collective-permute-done.23.refs_7_), channel_id=1, source_target_pairs={{0,1},{1,2},{2,3},{3,4},{4,5},{5,6},{6,7},{7,0},{8,9},{9,10},{10,1... | collective-permute-start | bytes 884744 | tf_op jit(solution)/shard_map/ppermute | solution.py:21
  114.6 9.5 %collective-permute-start.21 = (bf16[384,384]{1,0:T(8,128)(2,1)S(1)}, bf16[384,384]{1,0:T(8,128)(2,1)S(1)}, u32[]{:S(2)}, u32[]{:S(2)}) collective-permute-start(bf16[384,384]{1,0:T(8,128)(2,1)S(1)} %collective-permute-done.20.refs_2_), channel_id=1, source_target_pairs={{0,7},{1,0},{2,1},{3,2},{4,3},{5,4},{6,5},{7,6},{8,15},{9,8},{10,9... | collective-permute-start | bytes 884744 | tf_op jit(solution)/shard_map/ppermute | solution.py:21
  118.9 9.3 %collective-permute-start.25 = (bf16[384,384]{1,0:T(8,128)(2,1)S(1)}, bf16[384,384]{1,0:T(8,128)(2,1)S(1)}, u32[]{:S(2)}, u32[]{:S(2)}) collective-permute-start(bf16[384,384]{1,0:T(8,128)(2,1)S(1)} %collective-permute-done.24.refs_6_), channel_id=1, source_target_pairs={{0,1},{1,2},{2,3},{3,4},{4,5},{5,6},{6,7},{7,0},{8,9},{9,10},{10,1... | collective-permute-start | bytes 884744 | tf_op jit(solution)/shard_map/ppermute | solution.py:21
  124.1 6.4 %collective-permute-start.22 = (bf16[192,384]{1,0:T(8,128)(2,1)S(1)}, bf16[192,384]{1,0:T(8,128)(2,1)S(1)}, u32[]{:S(2)}, u32[]{:S(2)}) collective-permute-start(bf16[192,384]{1,0:T(8,128)(2,1)S(1)} %slice.52), channel_id=1, source_target_pairs={{0,7},{1,0},{2,1},{3,2},{4,3},{5,4},{6,5},{7,6},{8,15},{9,8},{10,9... | collective-permute-start | bytes 442376 | tf_op jit(solution)/shard_map/ppermute | solution.py:21
  128.3 6.4 %collective-permute-start.26 = (bf16[192,384]{1,0:T(8,128)(2,1)S(1)}, bf16[192,384]{1,0:T(8,128)(2,1)S(1)}, u32[]{:S(2)}, u32[]{:S(2)}) collective-permute-start(bf16[192,384]{1,0:T(8,128)(2,1)S(1)} %slice.53), channel_id=1, source_target_pairs={{0,1},{1,2},{2,3},{3,4},{4,5},{5,6},{6,7},{7,0},{8,9},{9,10},{10,1... | collective-permute-start | bytes 442376 | tf_op jit(solution)/shard_map/ppermute | solution.py:21
  140.2 15.9 %all-to-all-start.2 = ((bf16[16,48,512]{2,1,0:T(8,128)(2,1)}), bf16[16,48,512]{2,1,0:T(8,128)(2,1)S(1)}, u32[]{:S(2)}, u32[]{:S(2)}) async-start(bf16[16,48,512]{2,1,0:T(8,128)(2,1)} %bitcast.15), calls=%async_computation.2 | async-start | bytes 1572864 | tf_op jit(solution)/shard_map/all_to_all | solution.py:452
  146.5 15.5 %copy-start.7 = (s32[64]{0:T(128)S(1)}, s32[64]{0:T(128)}, u32[]{:S(2)}) copy-start(s32[64]{0:T(128)} %param.23) | copy-start | bytes 772
  157.5 17.8 %all-to-all-start.3 = ((bf16[8,64,512]{2,1,0:T(8,128)(2,1)}), bf16[8,64,512]{2,1,0:T(8,128)(2,1)S(1)}, u32[]{:S(2)}, u32[]{:S(2)}) async-start(bf16[8,64,512]{2,1,0:T(8,128)(2,1)} %broadcast_in_dim.18), calls=%async_computation.3 | async-start | bytes 1048576 | tf_op jit(solution)/shard_map/all_to_all | solution.py:39
